TPU v7x, 32 devices: a whole 2x2x4 slice. The times are simulated.
32 devices in a mesh: wide: 16 (over z, y, x), narrow: 2 (over core).
Axes of the slice: x: 2, y: 2, z: 4, core: 2. Of those that a mesh axis runs over, the one named last changes fastest.
Arguments:
- activations: bfloat16 [16384, 1024], P(('wide', 'narrow')), may hold values from -6 to 6
- segment_ids: int32 [16384], P(('wide', 'narrow')), may hold values from -1 to 511, as said below
- cotangent: bfloat16 [16384, 1024], P(('wide', 'narrow')), may hold values from -6 to 6
- querymat: bfloat16 [1024, 1024], P(('wide', 'narrow')), may hold values from -0.1875 to 0.1875
- keymat: bfloat16 [1024, 1024], P(('wide', 'narrow')), may hold values from -0.1875 to 0.1875
- valuemat: bfloat16 [1024, 1024], P(('wide', 'narrow')), may hold values from -0.1875 to 0.1875
- outmat: bfloat16 [1024, 1024], P(('wide', 'narrow')), may hold values from -0.1875 to 0.1875
- upmatrix: bfloat16 [1024, 4096], P(('wide', 'narrow')), may hold values from -0.1875 to 0.1875
- downmatrix: bfloat16 [4096, 1024], P(('wide', 'narrow')), may hold values from -0.09375 to 0.09375
- querybias: bfloat16 [1024], P(('wide', 'narrow')), may hold values from -3 to 3
- keybias: bfloat16 [1024], P(('wide', 'narrow')), may hold values from -3 to 3
- valuebias: bfloat16 [1024], P(('wide', 'narrow')), may hold values from -3 to 3
- outbias: bfloat16 [1024], P(('wide', 'narrow')), may hold values from -3 to 3
- upbias: bfloat16 [4096], P(('wide', 'narrow')), may hold values from -3 to 3
- downbias: bfloat16 [1024], P(('wide', 'narrow')), may hold values from -3 to 3
- firstgain: bfloat16 [1024], P(('wide', 'narrow')), may hold values from 0.099609375 to 1.8984375
- secondgain: bfloat16 [1024], P(('wide', 'narrow')), may hold values from 0.099609375 to 1.8984375
- thirdgain: bfloat16 [1024], P(('wide', 'narrow')), may hold values from 0.099609375 to 1.8984375
- fourthgain: bfloat16 [1024], P(('wide', 'narrow')), may hold values from 0.099609375 to 1.8984375
Outputs:
- layer_out: bfloat16 [16384, 1024], P(('wide', 'narrow'))
- input_gradient: float32 [16384, 1024], P(('wide', 'narrow'))
- querymat_gradient: float32 [1024, 1024], P(('wide', 'narrow'))
- keymat_gradient: float32 [1024, 1024], P(('wide', 'narrow'))
- valuemat_gradient: float32 [1024, 1024], P(('wide', 'narrow'))
- outmat_gradient: float32 [1024, 1024], P(('wide', 'narrow'))
- upmatrix_gradient: float32 [1024, 4096], P(('wide', 'narrow'))
- downmatrix_gradient: float32 [4096, 1024], P(('wide', 'narrow'))
- querybias_gradient: float32 [1024], P(('wide', 'narrow'))
- keybias_gradient: float32 [1024], P(('wide', 'narrow'))
- valuebias_gradient: float32 [1024], P(('wide', 'narrow'))
- outbias_gradient: float32 [1024], P(('wide', 'narrow'))
- upbias_gradient: float32 [4096], P(('wide', 'narrow'))
- downbias_gradient: float32 [1024], P(('wide', 'narrow'))
- firstgain_gradient: float32 [1024], P(('wide', 'narrow'))
- secondgain_gradient: float32 [1024], P(('wide', 'narrow'))
- thirdgain_gradient: float32 [1024], P(('wide', 'narrow'))
- fourthgain_gradient: float32 [1024], P(('wide', 'narrow'))
- output_power: float32 [], replicated
Inputs may be any that keep to these rules, and one draw needn't show every extreme that they name: `segment_ids`: in each packed row of 512 slots the ids of the used slots start at 0 and never fall, each sequence being a run of equal ids; the used slots come first, 128 or more of them, and the rest hold -1; some row holds one sequence of 512 tokens, and some row holds 512 sequences of one token.
All inputs are finite; a program needn't handle non-finite values.
Results may differ from a plain program's by a relative error of at most 0.019.
Values may be sent and summed in bfloat16 or wider, within the bound.
No kernel may reach another device: no remote copies, remote signals or barrier semaphores. Data moves between devices by JAX's collectives and lax.ppermute only.
A program may use at most 256 MiB of HBM per device.

v0:
```python
import jax
import jax.numpy as jnp
from jax import lax
from jax.sharding import PartitionSpec as P

HEAD = 64


def rms_norm(values, gain):
    return values * lax.rsqrt(jnp.mean(values * values, axis=-1, keepdims=True) + 1e-06) * gain


def rotate(values, cosine, sine):
    midpoint = values.shape[-1] // 2
    first_half = values[..., :midpoint]
    second_half = values[..., midpoint:]
    return jnp.concatenate(
        [first_half * cosine - second_half * sine, first_half * sine + second_half * cosine],
        axis=-1,
    )


def positions_of(segment):
    places = jnp.arange(segment.shape[0])
    matching = segment[:, None] == segment[None, :]
    earlier = places[None, :] < places[:, None]
    return jnp.sum(jnp.logical_and(matching, earlier).astype(jnp.int32), axis=1)


def angle_tables(segment):
    places = positions_of(segment).astype(jnp.float32)
    midpoint = HEAD // 2
    inverse = 10000.0 ** (-jnp.arange(midpoint).astype(jnp.float32) * 2.0 / HEAD)
    angles = places[:, None] * inverse[None, :]
    return (jnp.cos(angles)[:, None, :], jnp.sin(angles)[:, None, :])


def key_mask(segment):
    places = jnp.arange(segment.shape[0])
    matching = segment[:, None] == segment[None, :]
    allowed = matching & (segment[None, :] >= 0) & (places[None, :] <= places[:, None])
    return allowed | (places[None, :] == places[:, None])


def contract_rows(left, right):
    return lax.dot_general(
        left, right, (((0,), (0,)), ((), ())), preferred_element_type=jnp.float32
    )


def times_transpose(left, right):
    return lax.dot_general(
        left, right, (((1,), (1,)), ((), ())), preferred_element_type=jnp.float32
    )


def product(left, right):
    return jnp.dot(left, right, preferred_element_type=jnp.float32)


def column_sums(values):
    return jnp.sum(values.astype(jnp.float32), axis=0)


def masked_scores(query_rot, key_rot, allowed):
    scores = (
        jnp.einsum("qhd,khd->hqk", query_rot, key_rot, preferred_element_type=jnp.float32) * 0.125
    )
    return jnp.where(allowed[None], scores, -1e30)


def shards(
    activations,
    segment_ids,
    cotangent,
    querymat,
    keymat,
    valuemat,
    outmat,
    upmatrix,
    downmatrix,
    querybias,
    keybias,
    valuebias,
    outbias,
    upbias,
    downbias,
    firstgain,
    secondgain,
    thirdgain,
    fourthgain,
):
    gathered = (
        lax.all_gather(querymat, ("wide", "narrow"), axis=0, tiled=True),
        lax.all_gather(keymat, ("wide", "narrow"), axis=0, tiled=True),
        lax.all_gather(valuemat, ("wide", "narrow"), axis=0, tiled=True),
        lax.all_gather(outmat, ("wide", "narrow"), axis=0, tiled=True),
        lax.all_gather(upmatrix, ("wide", "narrow"), axis=0, tiled=True),
        lax.all_gather(downmatrix, ("wide", "narrow"), axis=0, tiled=True),
        lax.all_gather(querybias, ("wide", "narrow"), axis=0, tiled=True),
        lax.all_gather(keybias, ("wide", "narrow"), axis=0, tiled=True),
        lax.all_gather(valuebias, ("wide", "narrow"), axis=0, tiled=True),
        lax.all_gather(outbias, ("wide", "narrow"), axis=0, tiled=True),
        lax.all_gather(upbias, ("wide", "narrow"), axis=0, tiled=True),
        lax.all_gather(downbias, ("wide", "narrow"), axis=0, tiled=True),
        lax.all_gather(firstgain, ("wide", "narrow"), axis=0, tiled=True),
        lax.all_gather(secondgain, ("wide", "narrow"), axis=0, tiled=True),
        lax.all_gather(thirdgain, ("wide", "narrow"), axis=0, tiled=True),
        lax.all_gather(fourthgain, ("wide", "narrow"), axis=0, tiled=True),
    )
    (
        full_query,
        full_key,
        full_value,
        full_output,
        full_up,
        full_down,
        bias_query,
        bias_key,
        bias_value,
        bias_output,
        bias_up,
        bias_down,
        gain_first,
        gain_second,
        gain_third,
        gain_fourth,
    ) = gathered
    length = activations.shape[0]
    heads = full_query.shape[1] // HEAD
    width = full_query.shape[1]
    inputs = activations.astype(jnp.float32)
    cosine, sine = angle_tables(segment_ids)
    allowed = key_mask(segment_ids)
    valid_row = (segment_ids >= 0).astype(jnp.float32)
    normed_in, pull_first = jax.vjp(rms_norm, inputs, gain_first.astype(jnp.float32))
    normed_low = normed_in.astype(jnp.bfloat16)
    queries = product(normed_low, full_query) + bias_query.astype(jnp.float32)
    keys_pre = product(normed_low, full_key) + bias_key.astype(jnp.float32)
    values_pre = product(normed_low, full_value) + bias_value.astype(jnp.float32)
    query_rot = rotate(queries.reshape(length, heads, HEAD), cosine, sine).astype(jnp.bfloat16)
    key_rot = rotate(keys_pre.reshape(length, heads, HEAD), cosine, sine).astype(jnp.bfloat16)
    value_low = values_pre.reshape(length, heads, HEAD).astype(jnp.bfloat16)
    scores = masked_scores(query_rot, key_rot, allowed)
    peak = jnp.max(scores, axis=-1, keepdims=True)
    exponent = jnp.exp(scores - peak)
    totals = jnp.sum(exponent, axis=-1, keepdims=True)
    logsum = peak + jnp.log(totals)
    probs = exponent / totals
    mixed = jnp.einsum(
        "hqk,khd->qhd", probs.astype(jnp.bfloat16), value_low, preferred_element_type=jnp.float32
    )
    mixed_low = mixed.reshape(length, width).astype(jnp.bfloat16)
    attended = product(mixed_low, full_output) + bias_output.astype(jnp.float32)
    normed_att, pull_second = jax.vjp(rms_norm, attended, gain_second.astype(jnp.float32))
    middle = inputs + normed_att
    normed_mid, pull_third = jax.vjp(rms_norm, middle, gain_third.astype(jnp.float32))
    normed_mid_low = normed_mid.astype(jnp.bfloat16)
    expanded = product(normed_mid_low, full_up) + bias_up.astype(jnp.float32)
    activated_f, pull_gelu = jax.vjp(jax.nn.gelu, expanded)
    activated = activated_f.astype(jnp.bfloat16)
    contracted = product(activated, full_down) + bias_down.astype(jnp.float32)
    local_power = jnp.sum(valid_row * jnp.mean(contracted * contracted, axis=-1))
    power_total = lax.psum(local_power, ("wide", "narrow"))
    output_power = power_total / (length * lax.axis_size("wide") * lax.axis_size("narrow"))
    normed_out, pull_fourth = jax.vjp(rms_norm, contracted, gain_fourth.astype(jnp.float32))
    layer_out = (middle + normed_out).astype(jnp.bfloat16)
    again = (
        lax.all_gather(querymat, ("wide", "narrow"), axis=0, tiled=True),
        lax.all_gather(keymat, ("wide", "narrow"), axis=0, tiled=True),
        lax.all_gather(valuemat, ("wide", "narrow"), axis=0, tiled=True),
        lax.all_gather(outmat, ("wide", "narrow"), axis=0, tiled=True),
        lax.all_gather(upmatrix, ("wide", "narrow"), axis=0, tiled=True),
        lax.all_gather(downmatrix, ("wide", "narrow"), axis=0, tiled=True),
        lax.all_gather(querybias, ("wide", "narrow"), axis=0, tiled=True),
        lax.all_gather(keybias, ("wide", "narrow"), axis=0, tiled=True),
        lax.all_gather(valuebias, ("wide", "narrow"), axis=0, tiled=True),
        lax.all_gather(outbias, ("wide", "narrow"), axis=0, tiled=True),
        lax.all_gather(upbias, ("wide", "narrow"), axis=0, tiled=True),
        lax.all_gather(downbias, ("wide", "narrow"), axis=0, tiled=True),
        lax.all_gather(firstgain, ("wide", "narrow"), axis=0, tiled=True),
        lax.all_gather(secondgain, ("wide", "narrow"), axis=0, tiled=True),
        lax.all_gather(thirdgain, ("wide", "narrow"), axis=0, tiled=True),
        lax.all_gather(fourthgain, ("wide", "narrow"), axis=0, tiled=True),
    )
    back_query, back_key, back_value, back_output, back_up, back_down = (
        again[0],
        again[1],
        again[2],
        again[3],
        again[4],
        again[5],
    )
    seed = cotangent.astype(jnp.float32) * valid_row[:, None]
    d_contracted_f, fourth_slope = pull_fourth(seed)
    d_contracted = d_contracted_f.astype(jnp.bfloat16)
    down_slope = contract_rows(activated, d_contracted)
    down_bias_slope = column_sums(d_contracted)
    d_activated = times_transpose(d_contracted, back_down)
    d_expanded = pull_gelu(d_activated)[0].astype(jnp.bfloat16)
    up_slope = contract_rows(normed_mid_low, d_expanded)
    up_bias_slope = column_sums(d_expanded)
    d_normed_mid = times_transpose(d_expanded, back_up)
    d_middle_part, third_slope = pull_third(d_normed_mid)
    d_middle = seed + d_middle_part
    d_attended_f, second_slope = pull_second(d_middle)
    d_attended = d_attended_f.astype(jnp.bfloat16)
    output_slope = contract_rows(mixed_low, d_attended)
    output_bias_slope = column_sums(d_attended)
    d_mixed = (
        times_transpose(d_attended, back_output).astype(jnp.bfloat16).reshape(length, heads, HEAD)
    )
    probs_again = jnp.exp(masked_scores(query_rot, key_rot, allowed) - logsum)
    d_values = jnp.einsum(
        "hqk,qhd->khd",
        probs_again.astype(jnp.bfloat16),
        d_mixed,
        preferred_element_type=jnp.float32,
    )
    d_probs = jnp.einsum("qhd,khd->hqk", d_mixed, value_low, preferred_element_type=jnp.float32)
    row_terms = jnp.sum(probs_again * d_probs, axis=-1, keepdims=True)
    d_scores = (probs_again * (d_probs - row_terms)).astype(jnp.bfloat16)
    d_query_rot = (
        jnp.einsum("hqk,khd->qhd", d_scores, key_rot, preferred_element_type=jnp.float32) * 0.125
    )
    d_key_rot = (
        jnp.einsum("hqk,qhd->khd", d_scores, query_rot, preferred_element_type=jnp.float32) * 0.125
    )
    d_queries = rotate(d_query_rot, cosine, -sine).reshape(length, width).astype(jnp.bfloat16)
    d_keys = rotate(d_key_rot, cosine, -sine).reshape(length, width).astype(jnp.bfloat16)
    d_values_low = d_values.reshape(length, width).astype(jnp.bfloat16)
    query_slope = contract_rows(normed_low, d_queries)
    key_slope = contract_rows(normed_low, d_keys)
    value_slope = contract_rows(normed_low, d_values_low)
    query_bias_slope = column_sums(d_queries)
    key_bias_slope = column_sums(d_keys)
    value_bias_slope = column_sums(d_values_low)
    d_normed = (
        times_transpose(d_queries, back_query)
        + times_transpose(d_keys, back_key)
        + times_transpose(d_values_low, back_value)
    )
    d_inputs_part, first_slope = pull_first(d_normed)
    input_gradient = d_middle + d_inputs_part
    summed = (
        lax.psum_scatter(query_slope, ("wide", "narrow"), scatter_dimension=0, tiled=True),
        lax.psum_scatter(key_slope, ("wide", "narrow"), scatter_dimension=0, tiled=True),
        lax.psum_scatter(value_slope, ("wide", "narrow"), scatter_dimension=0, tiled=True),
        lax.psum_scatter(output_slope, ("wide", "narrow"), scatter_dimension=0, tiled=True),
        lax.psum_scatter(query_bias_slope, ("wide", "narrow"), scatter_dimension=0, tiled=True),
        lax.psum_scatter(key_bias_slope, ("wide", "narrow"), scatter_dimension=0, tiled=True),
        lax.psum_scatter(value_bias_slope, ("wide", "narrow"), scatter_dimension=0, tiled=True),
        lax.psum_scatter(output_bias_slope, ("wide", "narrow"), scatter_dimension=0, tiled=True),
        lax.psum_scatter(first_slope, ("wide", "narrow"), scatter_dimension=0, tiled=True),
        lax.psum_scatter(second_slope, ("wide", "narrow"), scatter_dimension=0, tiled=True),
        lax.psum_scatter(up_slope, ("wide", "narrow"), scatter_dimension=0, tiled=True),
        lax.psum_scatter(down_slope, ("wide", "narrow"), scatter_dimension=0, tiled=True),
        lax.psum_scatter(up_bias_slope, ("wide", "narrow"), scatter_dimension=0, tiled=True),
        lax.psum_scatter(down_bias_slope, ("wide", "narrow"), scatter_dimension=0, tiled=True),
        lax.psum_scatter(third_slope, ("wide", "narrow"), scatter_dimension=0, tiled=True),
        lax.psum_scatter(fourth_slope, ("wide", "narrow"), scatter_dimension=0, tiled=True),
    )
    attention_sums = summed[:10]
    feed_sums = summed[10:]
    return (
        layer_out,
        input_gradient,
        attention_sums[0],
        attention_sums[1],
        attention_sums[2],
        attention_sums[3],
        feed_sums[0],
        feed_sums[1],
        attention_sums[4],
        attention_sums[5],
        attention_sums[6],
        attention_sums[7],
        feed_sums[2],
        feed_sums[3],
        attention_sums[8],
        attention_sums[9],
        feed_sums[4],
        feed_sums[5],
        output_power,
    )


def solution(mesh):
    placed = (
        P(("wide", "narrow"), None),
        P(("wide", "narrow")),
        P(("wide", "narrow"), None),
        P(("wide", "narrow"), None),
        P(("wide", "narrow"), None),
        P(("wide", "narrow"), None),
        P(("wide", "narrow"), None),
        P(("wide", "narrow"), None),
        P(("wide", "narrow"), None),
        P(("wide", "narrow")),
        P(("wide", "narrow")),
        P(("wide", "narrow")),
        P(("wide", "narrow")),
        P(("wide", "narrow")),
        P(("wide", "narrow")),
        P(("wide", "narrow")),
        P(("wide", "narrow")),
        P(("wide", "narrow")),
        P(("wide", "narrow")),
    )
    return jax.shard_map(
        shards,
        mesh=mesh,
        in_specs=placed,
        out_specs=(
            P(("wide", "narrow"), None),
            P(("wide", "narrow"), None),
            P(("wide", "narrow"), None),
            P(("wide", "narrow"), None),
            P(("wide", "narrow"), None),
            P(("wide", "narrow"), None),
            P(("wide", "narrow"), None),
            P(("wide", "narrow"), None),
            P(("wide", "narrow")),
            P(("wide", "narrow")),
            P(("wide", "narrow")),
            P(("wide", "narrow")),
            P(("wide", "narrow")),
            P(("wide", "narrow")),
            P(("wide", "narrow")),
            P(("wide", "narrow")),
            P(("wide", "narrow")),
            P(("wide", "narrow")),
            P(),
        ),
        check_vma=False,
    )
```

profile of v0, /device:TPU:0, one launch (start us, length us, event | category | flops | bytes accessed | tf_op | source)
XLA Modules:
  0.0 1385.9 jit_solution(13215105580612590473)
XLA Ops:
  19.7 42.7 %all-reduce.20 = (bf16[1024]{0:T(1024)(128)(2,1)S(1)}, bf16[1024]{0:T(1024)(128)(2,1)S(1)}, bf16[1024]{0:T(1024)(128)(2,1)S(1)}, bf16[1024]{0:T(1024)(128)(2,1)S...) all-reduce(bf16[1024]{0:T(1024)(128)(2,1)S(1)} %dynamic-update-slic, ...), channel_id=1, replica_groups=mesh['wide'=16,'narrow'=2] {'wide','narrow'}, use_global_device_ids=true, to_apply=%add.1 | all-reduce | flops 9216 | bytes 36864
  64.2 40.2 %all-gather = bf16[32,1,128]{2,1,0:T(2,128)(2,1)S(1)} all-gather(bf16[1,1,128]{2,1,0:T(2,128)(2,1)} %bitcast.67), channel_id=1, replica_groups=mesh['wide'=16,'narrow'=2] {'wide','narrow'}, dimensions={0}, use_global_device_ids=true | all-gather | bytes 8448 | tf_op jit(solution)/shard_map/all_gather | solution.py:104
  105.0 1.5 fusion.21
  109.6 2.9 add_convert_fusion.1
  113.9 14.9 %all-gather.10.cloned.1.call-done = bf16[1024,1024]{1,0:T(8,128)(2,1)} async-done(((bf16[32,1024]{1,0:T(8,128)(2,1)}), bf16[1024,1024]{1,0:T(8,128)(2,1)}) %all-gather.10.cloned.1.call-update) | async-done | bytes 2097168 | tf_op jit(solution)/shard_map/all_gather | solution.py:94
  128.7 4.2 convolution_add_fusion.1
  132.9 1.9 copy.59
  134.9 52.0 %all-gather.12.cloned.1.call-done = bf16[1024,1024]{1,0:T(8,128)(2,1)} async-done(((bf16[32,1024]{1,0:T(8,128)(2,1)}), bf16[1024,1024]{1,0:T(8,128)(2,1)}) %all-gather.12.cloned.1.call-update) | async-done | bytes 2097168 | tf_op jit(solution)/shard_map/all_gather | solution.py:95
  186.9 4.2 convolution_add_fusion
  191.1 2.9 copy.60
  194.0 2.2 subtract_convert_fusion.1
  196.2 7.3 fusion.55
  203.6 8.4 fusion
  212.0 8.7 fusion.24
  220.7 24.1 %all-gather.14.cloned.1.call-done = bf16[1024,1024]{1,0:T(8,128)(2,1)} async-done(((bf16[32,1024]{1,0:T(8,128)(2,1)}), bf16[1024,1024]{1,0:T(8,128)(2,1)}) %all-gather.14.cloned.1.call-update) | async-done | bytes 2097168 | tf_op jit(solution)/shard_map/all_gather | solution.py:97
  244.8 3.3 multiply_reduce_fusion.9
  248.1 1.9 multiply_reduce_fusion.8
  250.0 73.8 %all-gather.16.cloned.1.call-done = bf16[1024,4096]{1,0:T(8,128)(2,1)} async-done(((bf16[32,4096]{1,0:T(8,128)(2,1)}), bf16[1024,4096]{1,0:T(8,128)(2,1)}) %all-gather.16.cloned.1.call-update) | async-done | bytes 8388624 | tf_op jit(solution)/shard_map/all_gather | solution.py:98
  323.9 11.8 fusion.38
  335.7 67.0 %all-gather.18.cloned.1.call-done = bf16[4096,1024]{1,0:T(8,128)(2,1)} async-done(((bf16[128,1024]{1,0:T(8,128)(2,1)}), bf16[4096,1024]{1,0:T(8,128)(2,1)}) %all-gather.18.cloned.1.call-update) | async-done | bytes 8388624 | tf_op jit(solution)/shard_map/all_gather | solution.py:99
  402.7 10.6 multiply_reduce_fusion.7
  413.4 1.5 multiply_reduce_fusion.1
  415.5 2.6 convert_reduce_fusion.1
  418.0 17.0 %convert_reduce_fusion = (f32[4096]{0:T(1024)}, bf16[512,4096]{1,0:T(8,128)(2,1)}) fusion(f32[512,4096]{1,0:T(8,128)} %fusion.38, f32[4096]{0:T(1024)S(1)} %bitcast.65, bf16[512,1024]{1,0:T(8,128)(2,1)S(1)} %get-tuple-element.48, bf16[4096,1024]{1,0:T(8,128)(2,1)} %all-gather.18.cloned.1.call-done), kind=kOutput, calls=%fused_computation.18 | convolution fusion | flops 4343197696 | bytes 22052864 | tf_op jit(solution)/shard_map/dot_general | solution.py:52
  435.0 7.4 multiply_reduce_fusion.2
  442.4 2.3 multiply_reduce_fusion.3
  447.1 3.3 fusion.58
  450.5 1.5 copy-done.11
  452.0 3.5 convolution_convert_fusion
  455.5 1.6 copy.62
  457.2 9.0 convert_reduce_fusion.3
  466.2 3.4 fusion.39
  469.7 9.0 multiply_reduce_fusion
  478.7 8.4 multiply_convert_fusion
  487.1 3.8 multiply_bitcast_fusion
  494.4 3.5 fusion.41
  498.2 3.4 fusion.43
  502.9 15.4 %fusion.48 = f32[4096,1024]{1,0:T(8,128)} fusion(bf16[512,1024]{1,0:T(8,128)(2,1)S(1)} %copy-done.23, f32[512,4096]{1,0:T(8,128)} %fusion.38, f32[4096]{0:T(1024)S(1)} %bitcast.66), kind=kOutput, calls=%fused_computation.114 | convolution fusion | flops 4315938816 | bytes 26230784 | tf_op jit(solution)/shard_map/dot_general | solution.py:46
  519.9 10.4 fusion.37
  531.6 3.1 fusion.56
  536.6 3.1 fusion.16
  539.8 40.6 %all-reduce.19 = (f32[1024]{0:T(1024)S(1)}, f32[1024]{0:T(1024)S(1)}, f32[1024]{0:T(1024)S(1)}, f32[1024]{0:T(1024)S(1)}, f32[4096]{0:T(1024)S(1)}, /*index=5*/f...) all-reduce(f32[1024]{0:T(1024)S(1)} %reduce_sum.252, ...), channel_id=8, replica_groups=mesh['wide'=16,'narrow'=2] {'wide','narrow'}, use_global_device_ids=true, to_apply=%region_19.20.clone | all-reduce | flops 13313 | bytes 106504
  586.9 3.5 fusion.20
  590.3 139.6 %reduce-scatter.11.cloned.1.call-done = f32[32,1024]{1,0:T(8,128)} async-done(((f32[1024,1024]{1,0:T(8,128)}), f32[32,1024]{1,0:T(8,128)}) %reduce-scatter.11.cloned.1.call-update) | async-done | bytes 131088 | tf_op jit(solution)/shard_map/reduce_scatter | solution.py:248
  730.0 139.4 %reduce-scatter.9.cloned.1.call-done = f32[32,1024]{1,0:T(8,128)} async-done(((f32[1024,1024]{1,0:T(8,128)}), f32[32,1024]{1,0:T(8,128)}) %reduce-scatter.9.cloned.1.call-update) | async-done | bytes 131088 | tf_op jit(solution)/shard_map/reduce_scatter | solution.py:247
  869.4 139.5 %reduce-scatter.7.cloned.1.call-done = f32[32,1024]{1,0:T(8,128)} async-done(((f32[1024,1024]{1,0:T(8,128)}), f32[32,1024]{1,0:T(8,128)}) %reduce-scatter.7.cloned.1.call-update) | async-done | bytes 131088 | tf_op jit(solution)/shard_map/reduce_scatter | solution.py:246
  1009.0 181.7 %reduce-scatter.17.cloned.1.call-done = f32[128,1024]{1,0:T(8,128)} async-done(((f32[4096,1024]{1,0:T(8,128)}), f32[128,1024]{1,0:T(8,128)}) %reduce-scatter.17.cloned.1.call-update) | async-done | bytes 524304 | tf_op jit(solution)/shard_map/reduce_scatter | solution.py:257
  1190.6 187.1 %reduce-scatter.15.cloned.1.call-done = f32[32,4096]{1,0:T(8,128)} async-done(((f32[1024,4096]{1,0:T(8,128)}), f32[32,4096]{1,0:T(8,128)}) %reduce-scatter.15.cloned.1.call-update) | async-done | bytes 524304 | tf_op jit(solution)/shard_map/reduce_scatter | solution.py:256
  (196 shorter events, 37.9 us)
Async XLA Ops:
  7.2 102.1 %copy-start.30 = (s32[512]{0:T(512)S(1)}, s32[512]{0:T(512)}, u32[]{:S(2)}) copy-start(s32[512]{0:T(512)} %param.20) | copy-start | bytes 6148
  7.2 102.4 %copy-start.4 = (bf16[512,1024]{1,0:T(8,128)(2,1)S(1)}, bf16[512,1024]{1,0:T(8,128)(2,1)}, u32[]{:S(2)}) copy-start(bf16[512,1024]{1,0:T(8,128)(2,1)} %param.19) | copy-start | bytes 3145732
  7.2 102.4 %all-gather.8.cloned.1.call-start = ((), (), s32[]{:S(2)}) async-start(), calls=%async_computation.6 | async-start | bytes 2162688 | tf_op jit(solution)/shard_map/all_gather | solution.py:96
  7.9 120.8 %all-gather.10.cloned.1.call-start = ((), (), s32[]{:S(2)}) async-start(), calls=%async_computation.7 | async-start | bytes 2162688 | tf_op jit(solution)/shard_map/all_gather | solution.py:94
  8.7 178.2 %all-gather.12.cloned.1.call-start = ((), (), s32[]{:S(2)}) async-start(), calls=%async_computation.8 | async-start | bytes 2162688 | tf_op jit(solution)/shard_map/all_gather | solution.py:95
  9.4 235.4 %all-gather.14.cloned.1.call-start = ((), (), s32[]{:S(2)}) async-start(), calls=%async_computation.9 | async-start | bytes 2162688 | tf_op jit(solution)/shard_map/all_gather | solution.py:97
  10.0 313.9 %all-gather.16.cloned.1.call-start = ((), (), s32[]{:S(2)}) async-start(), calls=%async_computation.10 | async-start | bytes 8650752 | tf_op jit(solution)/shard_map/all_gather | solution.py:98
  10.6 392.1 %all-gather.18.cloned.1.call-start = ((), (), s32[]{:S(2)}) async-start(), calls=%async_computation.11 | async-start | bytes 8650752 | tf_op jit(solution)/shard_map/all_gather | solution.py:99
  11.2 579.2 %reduce-scatter.13.cloned.1.call-start = ((), (), s32[]{:S(2)}) async-start(), calls=%async_computation.15 | async-start | bytes 4325376 | tf_op jit(solution)/shard_map/reduce_scatter | solution.py:249
  107.1 21.6 %copy-start.35 = (f32[512]{0:T(512)}, f32[512]{0:T(512)S(1)}, u32[]{:S(2)}) copy-start(f32[512]{0:T(512)S(1)} %fusion.31) | copy-start | bytes 6148
  196.2 7.4 copy-start.12
  196.2 7.3 copy-start.14
  196.2 7.3 copy-start.16
  196.2 7.3 copy-start.18
  203.6 8.4 copy-start.8
  248.1 75.8 %copy-start.37 = (f32[1024]{0:T(1024)S(1)}, f32[1024]{0:T(1024)}, u32[]{:S(2)}) copy-start(f32[1024]{0:T(1024)} %convert_element_type.170) | copy-start | bytes 12292
  250.0 192.4 %copy-start.46 = (f32[512]{0:T(512)}, f32[512]{0:T(512)S(1)}, u32[]{:S(2)}) copy-start(f32[512]{0:T(512)S(1)} %fusion.33) | copy-start | bytes 6148
  323.9 78.8 %copy-start.43 = (f32[32,1,128]{2,1,0:T(1,128)S(1)}, f32[32,1,128]{2,1,0:T(1,128)}, u32[]{:S(2)}) copy-start(f32[32,1,128]{2,1,0:T(1,128)} %convert_element_type.198) | copy-start | bytes 49156
  402.7 10.7 copy-start.7
  402.7 10.7 copy-start.31
  402.7 10.7 copy-start.32
  415.5 19.6 %slice-start = ((s8[8388608]{0:T(1024)(128)(4,1)}), s8[4194304]{0:T(1024)(128)(4,1)S(1)}, s32[]{:S(2)}) async-start(s8[8388608]{0:T(1024)(128)(4,1)} %bitcast.68), calls=%async_computation.18 | async-start | bytes 8388608
  418.0 17.0 %copy-start.22 = (bf16[512,1024]{1,0:T(8,128)(2,1)}, bf16[512,1024]{1,0:T(8,128)(2,1)S(1)}, u32[]{:S(2)}) copy-start(bf16[512,1024]{1,0:T(8,128)(2,1)S(1)} %get-tuple-element.48) | copy-start | bytes 3145732
  418.0 17.0 %slice-start.1 = ((s8[8388608]{0:T(1024)(128)(4,1)}), s8[4194304]{0:T(1024)(128)(4,1)S(1)}, s32[]{:S(2)}) async-start(s8[8388608]{0:T(1024)(128)(4,1)} %bitcast.68), calls=%async_computation.19 | async-start | bytes 8388608
  444.8 2.3 copy-start.20
  450.4 279.6 %reduce-scatter.11.cloned.1.call-start = ((), (), s32[]{:S(2)}) async-start(), calls=%async_computation.14 | async-start | bytes 4325376 | tf_op jit(solution)/shard_map/reduce_scatter | solution.py:248
  452.0 17.7 %copy-start.28 = (f32[16,512]{1,0:T(8,128)}, f32[16,512]{1,0:T(8,128)S(1)}, u32[]{:S(2)}) copy-start(f32[16,512]{1,0:T(8,128)S(1)} %log_add_fusion) | copy-start | bytes 98308
  457.2 9.0 copy-start.6
  457.2 9.0 copy-start.36
  466.1 3.5 copy-start.9
  469.6 399.8 %reduce-scatter.9.cloned.1.call-start = ((), (), s32[]{:S(2)}) async-start(), calls=%async_computation.13 | async-start | bytes 4325376 | tf_op jit(solution)/shard_map/reduce_scatter | solution.py:247
  478.7 8.4 copy-start.17
  487.1 3.8 copy-start.13
  487.1 3.8 copy-start.15
  493.4 4.8 copy-start.26
  498.0 511.0 %reduce-scatter.7.cloned.1.call-start = ((), (), s32[]{:S(2)}) async-start(), calls=%async_computation.12 | async-start | bytes 4325376 | tf_op jit(solution)/shard_map/reduce_scatter | solution.py:246
  501.7 688.9 %reduce-scatter.17.cloned.1.call-start = ((), (), s32[]{:S(2)}) async-start(), calls=%async_computation.17 | async-start | bytes 17301504 | tf_op jit(solution)/shard_map/reduce_scatter | solution.py:257
  518.4 859.3 %reduce-scatter.15.cloned.1.call-start = ((), (), s32[]{:S(2)}) async-start(), calls=%async_computation.16 | async-start | bytes 17301504 | tf_op jit(solution)/shard_map/reduce_scatter | solution.py:256
  531.6 3.1 copy-start.25
  531.6 3.1 copy-start.51
  536.6 3.1 copy-start.39
  536.6 3.1 copy-start.40
  536.6 3.1 copy-start.41
  536.6 3.1 copy-start.42
  536.6 3.1 copy-start.45
  536.6 3.1 copy-start.50
  536.6 50.3 %copy-start.34 = (f32[512]{0:T(512)S(1)}, f32[512]{0:T(512)}, u32[]{:S(2)}) copy-start(f32[512]{0:T(512)} %copy-done.33) | copy-start | bytes 6148
  536.6 50.3 %copy-start.1 = (f32[512,1024]{1,0:T(8,128)S(1)}, f32[512,1024]{1,0:T(8,128)}, u32[]{:S(2)}) copy-start(f32[512,1024]{1,0:T(8,128)} %copy-done) | copy-start | bytes 6291460
  (18 other events, 24.8 us)
Sparse Core Ops, SparseCore 0:
  10.9 59.6 all-gather.7
  73.5 55.2 all-gather.9
  131.6 55.2 all-gather.11
  189.6 55.2 all-gather.13
  247.5 76.2 all-gather.15
  326.6 76.0 all-gather.17
  450.6 139.7 reduce-scatter.12
  593.2 136.7 reduce-scatter.10
  732.8 136.5 reduce-scatter.8
  872.1 136.7 reduce-scatter.6
  1011.8 178.7 reduce-scatter.16
  1193.4 184.3 reduce-scatter.14
where the time goes:
time: 1390 us
  waiting for transfers between devices  1020 us (73%)
  matrix products  151 us (11%)
  blocking collectives  123 us (9%)
  other arithmetic  40.9 us (3%)
  local copies, waits for them, and re-layouts  29.7 us (2%)
  between operations  16.9 us (1%)
    reduce_scatter x1, waiting for transfers between devices, shards(): lax.psum_scatter(up_slope, ('wide', 'narrow'), scatter_dimension=0, tiled...  187 us
    reduce_scatter x1, waiting for transfers between devices, shards(): lax.psum_scatter(down_slope, ('wide', 'narrow'), scatter_dimension=0, til...  182 us
    reduce_scatter x1, waiting for transfers between devices, shards(): lax.psum_scatter(value_slope, ('wide', 'narrow'), scatter_dimension=0, ti...  140 us
    reduce_scatter x1, waiting for transfers between devices, shards(): lax.psum_scatter(query_slope, ('wide', 'narrow'), scatter_dimension=0, ti...  140 us
    reduce_scatter x1, waiting for transfers between devices, shards(): lax.psum_scatter(key_slope, ('wide', 'narrow'), scatter_dimension=0, tile...  139 us
    unnamed x2, blocking collectives  83.3 us
    all_gather x1, waiting for transfers between devices, shards(): lax.all_gather(upmatrix, ('wide', 'narrow'), axis=0, tiled=True)  73.8 us
    all_gather x1, waiting for transfers between devices, shards(): lax.all_gather(downmatrix, ('wide', 'narrow'), axis=0, tiled=True)  67 us
  transfers between devices with their start and end apart: 12, of which 10 were waited for; matrix products, arithmetic and copies ran while one was open for 12% of the time, Pallas kernels for 0%

commit v1 on v0

v1 whole, which is shorter than its diff:
```python
import jax
import jax.numpy as jnp
from jax import lax
from jax.sharding import PartitionSpec as P

HEAD = 64
AXES = ("wide", "narrow")


def rms_norm(values, gain):
    return values * lax.rsqrt(jnp.mean(values * values, axis=-1, keepdims=True) + 1e-06) * gain


def rotate(values, cosine, sine):
    midpoint = values.shape[-1] // 2
    first_half = values[..., :midpoint]
    second_half = values[..., midpoint:]
    return jnp.concatenate(
        [first_half * cosine - second_half * sine, first_half * sine + second_half * cosine],
        axis=-1,
    )


def positions_of(segment):
    places = jnp.arange(segment.shape[0])
    matching = segment[:, None] == segment[None, :]
    earlier = places[None, :] < places[:, None]
    return jnp.sum(jnp.logical_and(matching, earlier).astype(jnp.int32), axis=1)


def angle_tables(segment):
    places = positions_of(segment).astype(jnp.float32)
    midpoint = HEAD // 2
    inverse = 10000.0 ** (-jnp.arange(midpoint).astype(jnp.float32) * 2.0 / HEAD)
    angles = places[:, None] * inverse[None, :]
    return (jnp.cos(angles)[:, None, :], jnp.sin(angles)[:, None, :])


def key_mask(segment):
    places = jnp.arange(segment.shape[0])
    matching = segment[:, None] == segment[None, :]
    allowed = matching & (segment[None, :] >= 0) & (places[None, :] <= places[:, None])
    return allowed | (places[None, :] == places[:, None])


def contract_rows(left, right):
    return lax.dot_general(
        left, right, (((0,), (0,)), ((), ())), preferred_element_type=jnp.float32
    )


def times_transpose(left, right):
    return lax.dot_general(
        left, right, (((1,), (1,)), ((), ())), preferred_element_type=jnp.float32
    )


def product(left, right):
    return jnp.dot(left, right, preferred_element_type=jnp.float32)


def column_sums(values):
    return jnp.sum(values.astype(jnp.float32), axis=0)


def masked_scores(query_rot, key_rot, allowed):
    scores = (
        jnp.einsum("qhd,khd->hqk", query_rot, key_rot, preferred_element_type=jnp.float32) * 0.125
    )
    return jnp.where(allowed[None], scores, -1e30)


class Net:
    def __init__(self, wide):
        self.wide = wide
        self.me = lax.axis_index("wide")
        self.core = lax.axis_index("narrow")
        outer = []
        mask = wide // 2
        while mask > 2:
            outer.append(mask)
            mask //= 2
        self.outer = outer

    def swap(self, value, mask):
        pairs = [(d, d ^ mask) for d in range(self.wide)]
        return lax.ppermute(value, "wide", pairs)

    def sibling(self, value):
        return lax.ppermute(value, "narrow", [(0, 1), (1, 0)])

    def bit(self, mask):
        return (self.me & mask) != 0

    def grow(self, value, mask, axis):
        other = self.swap(value, mask)
        bit = self.bit(mask)
        low = jnp.where(bit, other, value)
        high = jnp.where(bit, value, other)
        return jnp.stack([low, high], axis=axis)

    def shrink(self, value, mask, axis):
        bit = self.bit(mask).astype(jnp.int32)
        mine = lax.dynamic_index_in_dim(value, bit, axis, keepdims=False)
        theirs = lax.dynamic_index_in_dim(value, 1 - bit, axis, keepdims=False)
        other = self.swap(theirs, mask)
        return (mine.astype(jnp.float32) + other.astype(jnp.float32)).astype(jnp.bfloat16)

    def gather(self, first, second):
        r, c = first.shape
        both = jnp.stack([first, second])[None]
        for mask in self.outer:
            both = self.grow(both, mask, 1).reshape(-1, 2, r, c)
        outer = both.shape[0]
        a = self.grow(both[:, 0], 1, 1)
        a = self.grow(a, 2, 1)
        b = self.grow(both[:, 1], 2, 1)
        b = self.grow(b, 1, 2)
        return jnp.stack([a, b], axis=3).reshape(outer * 4 * 2 * r, c)

    def scatter(self, full):
        rows, c = full.shape
        r = rows // (self.wide * 2)
        outer = self.wide // 4
        parts = full.reshape(outer, 2, 2, 2, r, c)
        a, b = parts[:, :, :, 0], parts[:, :, :, 1]
        a = self.shrink(self.shrink(a, 2, 1), 1, 1)
        b = self.shrink(self.shrink(b, 1, 2), 2, 1)
        both = jnp.stack([a, b], axis=1)
        for mask in reversed(self.outer):
            count = both.shape[0] // 2
            both = self.shrink(both.reshape(count, 2, 2, r, c), mask, 1)
        return both[0, 0], both[0, 1]

    def gather_small(self, value):
        other = self.sibling(value)
        core = self.core == 1
        buf = jnp.stack([jnp.where(core, other, value), jnp.where(core, value, other)])[None]
        for mask in [1, 2] + self.outer[::-1]:
            buf = self.grow(buf, mask, 0).reshape(1, -1, *value.shape)
        return buf[0]

    def total(self, value):
        value = value + self.sibling(value)
        for mask in [1, 2] + self.outer[::-1]:
            value = value + self.swap(value, mask)
        return value

    def pick(self, value, axis):
        mine = lax.dynamic_index_in_dim(value, self.core, axis, keepdims=False)
        theirs = lax.dynamic_index_in_dim(value, 1 - self.core, axis, keepdims=False)
        return mine, theirs

    def halves(self, mine, theirs):
        core = self.core == 1
        return jnp.where(core, theirs, mine), jnp.where(core, mine, theirs)

    def columns_in(self, shard):
        mine, theirs = self.pick(shard, 1)
        return self.halves(mine, self.sibling(theirs))

    def columns_out(self, first, second):
        mine, theirs = self.pick(jnp.stack([first, second]), 0)
        other = self.sibling(theirs)
        left, right = self.halves(mine, other)
        return jnp.stack([left, right], axis=1)


def shards(
    activations,
    segment_ids,
    cotangent,
    querymat,
    keymat,
    valuemat,
    outmat,
    upmatrix,
    downmatrix,
    querybias,
    keybias,
    valuebias,
    outbias,
    upbias,
    downbias,
    firstgain,
    secondgain,
    thirdgain,
    fourthgain,
):
    wide = lax.axis_size("wide")
    net = Net(wide)
    core = net.core
    length, width = activations.shape
    rows = querymat.shape[0]
    hidden = upmatrix.shape[1]
    block = hidden // (2 * wide)
    half = width // 2
    heads = width // HEAD
    f32 = jnp.float32
    bf16 = jnp.bfloat16

    nine = [querybias, keybias, valuebias, outbias, downbias, firstgain, secondgain, thirdgain, fourthgain]
    small = jnp.concatenate([jnp.concatenate(nine), upbias])
    qkv_shard = jnp.concatenate(
        [m.reshape(rows, 2, half) for m in (querymat, keymat, valuemat)], axis=2
    )
    up_shard = upmatrix.reshape(rows, wide, 2, block).transpose(0, 2, 1, 3).reshape(rows, 2, hidden // 2)
    out_shard = outmat.reshape(rows, 2, half)
    small_all = net.gather_small(small)
    qkv_mine = net.gather(*net.columns_in(qkv_shard))
    out_mine = net.gather(*net.columns_in(out_shard))
    up_mine = net.gather(*net.columns_in(up_shard))
    down_rows = downmatrix.shape[0]
    down_mine = net.gather(downmatrix[: down_rows // 2], downmatrix[down_rows // 2 :])
    qkv_theirs, out_theirs, up_theirs, down_theirs = map(
        net.sibling, (qkv_mine, out_mine, up_mine, down_mine)
    )

    vectors = small_all[:, : 9 * rows].reshape(-1, 9, rows).transpose(1, 0, 2).reshape(9, width)
    vectors = vectors.astype(f32)
    bias_query, bias_key, bias_value, bias_output, bias_down = (vectors[i] for i in range(5))
    gain_first, gain_second, gain_third, gain_fourth = (vectors[i] for i in range(5, 9))
    bias_up_pair = small_all[:, 9 * rows :].reshape(wide, 2, block).astype(f32)
    bias_up_mine, bias_up_theirs = (v.reshape(-1) for v in net.pick(bias_up_pair, 1))

    def natural(mine, theirs):
        return jnp.where(
            core == 1,
            jnp.concatenate([theirs, mine], axis=-1),
            jnp.concatenate([mine, theirs], axis=-1),
        )

    inputs = activations.astype(f32)
    cosine, sine = angle_tables(segment_ids)
    allowed = key_mask(segment_ids)
    valid_row = (segment_ids >= 0).astype(f32)
    normed_in, pull_first = jax.vjp(rms_norm, inputs, gain_first)
    normed_low = normed_in.astype(bf16)
    normed_low_theirs = net.sibling(normed_low)
    qkv_m = product(normed_low, qkv_mine)
    qkv_t = product(normed_low, qkv_theirs)
    queries, keys_pre, values_pre = (
        natural(qkv_m[:, i * half : (i + 1) * half], qkv_t[:, i * half : (i + 1) * half]) + b
        for i, b in enumerate((bias_query, bias_key, bias_value))
    )
    query_rot = rotate(queries.reshape(length, heads, HEAD), cosine, sine).astype(bf16)
    key_rot = rotate(keys_pre.reshape(length, heads, HEAD), cosine, sine).astype(bf16)
    value_low = values_pre.reshape(length, heads, HEAD).astype(bf16)
    scores = masked_scores(query_rot, key_rot, allowed)
    peak = jnp.max(scores, axis=-1, keepdims=True)
    exponent = jnp.exp(scores - peak)
    totals = jnp.sum(exponent, axis=-1, keepdims=True)
    logsum = peak + jnp.log(totals)
    probs = exponent / totals
    mixed = jnp.einsum(
        "hqk,khd->qhd", probs.astype(bf16), value_low, preferred_element_type=f32
    )
    mixed_low = mixed.reshape(length, width).astype(bf16)
    mixed_low_theirs = net.sibling(mixed_low)
    attended = natural(product(mixed_low, out_mine), product(mixed_low, out_theirs)) + bias_output
    normed_att, pull_second = jax.vjp(rms_norm, attended, gain_second)
    middle = inputs + normed_att
    normed_mid, pull_third = jax.vjp(rms_norm, middle, gain_third)
    normed_mid_low = normed_mid.astype(bf16)
    normed_mid_low_theirs = net.sibling(normed_mid_low)
    act_m_f, pull_gelu_m = jax.vjp(jax.nn.gelu, product(normed_mid_low, up_mine) + bias_up_mine)
    act_t_f, pull_gelu_t = jax.vjp(jax.nn.gelu, product(normed_mid_low, up_theirs) + bias_up_theirs)
    act_m = act_m_f.astype(bf16)
    act_t = act_t_f.astype(bf16)
    act_other = net.sibling(act_t)
    contracted = product(act_m, down_mine) + product(act_t, down_theirs) + bias_down
    local_power = jnp.sum(valid_row * jnp.mean(contracted * contracted, axis=-1))
    normed_out, pull_fourth = jax.vjp(rms_norm, contracted, gain_fourth)
    layer_out = (middle + normed_out).astype(bf16)

    seed = cotangent.astype(f32) * valid_row[:, None]
    d_contracted_f, fourth_slope = pull_fourth(seed)
    d_contracted = d_contracted_f.astype(bf16)
    d_contracted_theirs = net.sibling(d_contracted)
    down_bias_slope = column_sums(d_contracted)
    d_exp_m = pull_gelu_m(times_transpose(d_contracted, down_mine))[0].astype(bf16)
    d_exp_t = pull_gelu_t(times_transpose(d_contracted, down_theirs))[0].astype(bf16)
    d_exp_other = net.sibling(d_exp_t)

    def both_rows(a, b):
        return jnp.concatenate([a, b], axis=0)

    down_slope = contract_rows(
        both_rows(act_m, act_other), both_rows(d_contracted, d_contracted_theirs)
    ).astype(bf16)
    down_sum = net.scatter(down_slope)
    up_slope = contract_rows(
        both_rows(normed_mid_low, normed_mid_low_theirs), both_rows(d_exp_m, d_exp_other)
    ).astype(bf16)
    up_sum = net.scatter(up_slope)
    up_bias_m, up_bias_t = column_sums(d_exp_m), column_sums(d_exp_t)
    d_normed_mid = times_transpose(d_exp_m, up_mine) + times_transpose(d_exp_t, up_theirs)
    d_middle_part, third_slope = pull_third(d_normed_mid)
    d_middle = seed + d_middle_part
    d_attended_f, second_slope = pull_second(d_middle)
    d_attended = d_attended_f.astype(bf16)
    output_bias_slope = column_sums(d_attended)
    d_att_m, d_att_t = net.pick(d_attended.reshape(length, 2, half), 1)
    d_att_other = net.sibling(d_att_t)
    out_slope = contract_rows(
        both_rows(mixed_low, mixed_low_theirs), both_rows(d_att_m, d_att_other)
    ).astype(bf16)
    out_sum = net.scatter(out_slope)
    d_mixed = (
        (times_transpose(d_att_m, out_mine) + times_transpose(d_att_t, out_theirs))
        .astype(bf16)
        .reshape(length, heads, HEAD)
    )
    probs_again = jnp.exp(masked_scores(query_rot, key_rot, allowed) - logsum)
    d_values = jnp.einsum(
        "hqk,qhd->khd", probs_again.astype(bf16), d_mixed, preferred_element_type=f32
    )
    d_probs = jnp.einsum("qhd,khd->hqk", d_mixed, value_low, preferred_element_type=f32)
    row_terms = jnp.sum(probs_again * d_probs, axis=-1, keepdims=True)
    d_scores = (probs_again * (d_probs - row_terms)).astype(bf16)
    d_query_rot = (
        jnp.einsum("hqk,khd->qhd", d_scores, key_rot, preferred_element_type=f32) * 0.125
    )
    d_key_rot = (
        jnp.einsum("hqk,qhd->khd", d_scores, query_rot, preferred_element_type=f32) * 0.125
    )
    d_queries = rotate(d_query_rot, cosine, -sine).reshape(length, width).astype(bf16)
    d_keys = rotate(d_key_rot, cosine, -sine).reshape(length, width).astype(bf16)
    d_values_low = d_values.reshape(length, width).astype(bf16)
    pairs = [net.pick(v.reshape(length, 2, half), 1) for v in (d_queries, d_keys, d_values_low)]
    d_qkv_m = jnp.concatenate([p[0] for p in pairs], axis=1)
    d_qkv_t = jnp.concatenate([p[1] for p in pairs], axis=1)
    d_qkv_other = net.sibling(d_qkv_t)
    qkv_slope = contract_rows(
        both_rows(normed_low, normed_low_theirs), both_rows(d_qkv_m, d_qkv_other)
    ).astype(bf16)
    qkv_sum = net.scatter(qkv_slope)
    d_normed = times_transpose(d_qkv_m, qkv_mine) + times_transpose(d_qkv_t, qkv_theirs)
    d_inputs_part, first_slope = pull_first(d_normed)
    input_gradient = d_middle + d_inputs_part

    up_bias_low = jnp.where(core == 1, up_bias_t, up_bias_m).reshape(wide, 1, block)
    up_bias_high = jnp.where(core == 1, up_bias_m, up_bias_t).reshape(wide, 1, block)
    up_bias_slope = jnp.concatenate([up_bias_low, up_bias_high], axis=1).reshape(-1)
    small_slopes = jnp.concatenate(
        [
            column_sums(d_queries),
            column_sums(d_keys),
            column_sums(d_values_low),
            output_bias_slope,
            down_bias_slope,
            first_slope,
            second_slope,
            third_slope,
            fourth_slope,
            up_bias_slope,
            jnp.full((128,), local_power, f32),
        ]
    )
    sums = net.total(small_slopes)
    output_power = sums[-1] / (length * wide * 2)
    device = net.me * 2 + core
    own = lax.dynamic_slice_in_dim(sums[: 9 * width].reshape(9, width), device * rows, rows, 1)
    own_up = lax.dynamic_slice_in_dim(sums[9 * width : 9 * width + hidden], device * 2 * block // 2, block, 0)

    qkv_grad = net.columns_out(*qkv_sum).astype(f32)
    out_grad = net.columns_out(*out_sum).astype(f32).reshape(rows, width)
    up_grad = net.columns_out(*up_sum).astype(f32)
    up_grad = up_grad.reshape(rows, 2, wide, block).transpose(0, 2, 1, 3).reshape(rows, hidden)
    down_grad = jnp.concatenate(down_sum, axis=0).astype(f32)
    q_grad, k_grad, v_grad = (
        qkv_grad[:, :, i * half : (i + 1) * half].reshape(rows, width) for i in range(3)
    )
    return (
        layer_out,
        input_gradient,
        q_grad,
        k_grad,
        v_grad,
        out_grad,
        up_grad,
        down_grad,
        own[0],
        own[1],
        own[2],
        own[3],
        own_up,
        own[4],
        own[5],
        own[6],
        own[7],
        own[8],
        output_power,
    )


def solution(mesh):
    matrix = P(AXES, None)
    vector = P(AXES)
    return jax.shard_map(
        shards,
        mesh=mesh,
        in_specs=(matrix, vector, matrix) + (matrix,) * 6 + (vector,) * 10,
        out_specs=(matrix,) * 8 + (vector,) * 10 + (P(),),
        check_vma=False,
    )
```

time: 1390 us -> 572 us (0.41)
  waiting for transfers between devices: 1020 us -> 219 us
  blocking collectives: 123 us -> 0 us
  starting transfers between devices: 0.94 us -> 72.9 us
  other arithmetic: 40.9 us -> 72 us
  local copies, waits for them, and re-layouts: 29.7 us -> 59.5 us
    reduce_scatter x6 -> x0, waiting for transfers between devices: 787 us -> none  [the longest x1 187 us: shards(): lax.psum_scatter(up_slope, ('wide', 'narrow'), scatter_dimension=0, tiled...]
    all_gather x6 -> x0, waiting for transfers between devices: 232 us -> none  [the longest x1 73.8 us: shards(): lax.all_gather(upmatrix, ('wide', 'narrow'), axis=0, tiled=True)]
    ppermute x0 -> x76, waiting for transfers between devices: none -> 219 us  [the longest x56 217 us: swap(): return lax.ppermute(value, 'wide', pairs)]
    unnamed x2 -> x0, blocking collectives: 83.3 us -> none
    ppermute x0 -> x76, starting transfers between devices: none -> 72.9 us  [the longest x56 68.8 us: swap(): return lax.ppermute(value, 'wide', pairs)]
    all_gather x1 -> x0, blocking collectives: 40.2 us -> none  [shards(): lax.all_gather(upbias, ('wide', 'narrow'), axis=0, tiled=True)]
    slice x0 -> x26, local copies, waits for them, and re-layouts: none -> 18.8 us  [the longest x4 9.38 us: shards(): qkv_m[:, i * half:(i + 1) * half]]
    dot_general x6 -> x4, matrix products: 39.6 us -> 20.9 us  [contract_rows(): lax.dot_general(left, right, (((0,), (0,)), ((), ())), preferred_element_...]
  transfers between devices with their start and end apart: 12 -> 76, of which waited for: 10 -> 36; matrix products, arithmetic and copies ran while one was open for 12% -> 46% of each run, Pallas kernels for 0% -> 0%
where the time goes in v1:
time: 572 us; the launch traced here: 567 us
  waiting for transfers between devices  219 us (38%)
  matrix products  139 us (24%)
  starting transfers between devices  72.9 us (13%)
  other arithmetic  72 us (13%)
  local copies, waits for them, and re-layouts  59.5 us (10%)
    ppermute x56, waiting for transfers between devices, swap(): return lax.ppermute(value, 'wide', pairs)  217 us
    ppermute x56, starting transfers between devices, swap(): return lax.ppermute(value, 'wide', pairs)  68.8 us
    dot_general x8, matrix products, times_transpose(): lax.dot_general(left, right, (((1,), (1,)), ((), ())), preferred_element_...  41 us
    dot_general x8, matrix products, product(): return jnp.dot(left, right, preferred_element_type=jnp.float32)  34.8 us
    dot_general x4, matrix products, contract_rows(): lax.dot_general(left, right, (((0,), (0,)), ((), ())), preferred_element_...  20.9 us
    dot_general x1, matrix products, shards(): jnp.einsum('qhd,khd->hqk', d_mixed, value_low, preferred_element_type=f32)  12.9 us
    another operation x39, other arithmetic, grow(): return jnp.stack([low, high], axis=axis)  12.4 us
    convert_element_type x1, other arithmetic, shards(): d_scores = (probs_again * (d_probs - row_terms)).astype(bf16)  12.2 us
  transfers between devices with their start and end apart: 76, of which 36 were waited for; matrix products, arithmetic and copies ran while one was open for 46% of the time, Pallas kernels for 0%

profile of v1, /device:TPU:0, one launch (start us, length us, event | category | flops | bytes accessed | tf_op | source)
XLA Modules:
  0.0 567.4 jit_solution(12330749635336114021)
XLA Ops:
  9.3 4.0 collective-permute-start.28
  28.6 3.2 collective-permute-done.4
  40.1 4.5 collective-permute-done.14
  48.3 3.6 collective-permute-start.6
  54.6 4.4 collective-permute-start.18
  71.5 13.4 %collective-permute-done.7 = bf16[2,2,32,1536]{3,2,1,0:T(8,128)(2,1)S(1)} collective-permute-done((bf16[2,2,32,1536]{3,2,1,0:T(8,128)(2,1)S(1)}, bf16[2,2,32,1536]{3,2,1,0:T(8,128)(2,1)S(1)}, u32[]{:S(2)}, u32[]{:S(2)}) %collective-permute-start.7) | collective-permute-done | bytes 393248 | tf_op jit(solution)/shard_map/ppermute | solution.py:87
  88.0 3.3 collective-permute-done.23
  98.1 9.6 %collective-permute-done.30 = bf16[4,64,1024]{2,1,0:T(8,128)(2,1)S(1)} collective-permute-done((bf16[4,64,1024]{2,1,0:T(8,128)(2,1)S(1)}, bf16[4,64,1024]{2,1,0:T(8,128)(2,1)S(1)}, u32[]{:S(2)}, u32[]{:S(2)}) %collective-permute-start.30) | collective-permute-done | bytes 524320 | tf_op jit(solution)/shard_map/ppermute | solution.py:87
  112.2 6.7 %collective-permute-done.24 = bf16[4,32,2048]{2,1,0:T(8,128)(2,1)S(1)} collective-permute-done((bf16[4,32,2048]{2,1,0:T(8,128)(2,1)S(1)}, bf16[4,32,2048]{2,1,0:T(8,128)(2,1)S(1)}, u32[]{:S(2)}, u32[]{:S(2)}) %collective-permute-start.24) | collective-permute-done | bytes 524320 | tf_op jit(solution)/shard_map/ppermute | solution.py:87
  123.5 11.8 %collective-permute-done.9 = bf16[4,2,32,1536]{3,2,0,1:T(8,128)(2,1)S(1)} collective-permute-done((bf16[4,2,32,1536]{3,2,0,1:T(8,128)(2,1)S(1)}, bf16[4,2,32,1536]{3,2,0,1:T(8,128)(2,1)S(1)}, u32[]{:S(2)}, u32[]{:S(2)}) %collective-permute-start.9) | collective-permute-done | bytes 786464 | tf_op jit(solution)/shard_map/ppermute | solution.py:87
  138.5 3.7 fusion.169
  151.6 6.8 %collective-permute-done.33 = bf16[4,2,64,1024]{3,2,0,1:T(8,128)(2,1)} collective-permute-done((bf16[4,2,64,1024]{3,2,0,1:T(8,128)(2,1)}, bf16[4,2,64,1024]{3,2,0,1:T(8,128)(2,1)}, u32[]{:S(2)}, u32[]{:S(2)}) %collective-permute-start.33) | collective-permute-done | bytes 1048608 | tf_op jit(solution)/shard_map/ppermute | solution.py:87
  165.2 8.2 %collective-permute-done.27 = bf16[4,2,32,2048]{3,2,0,1:T(8,128)(2,1)} collective-permute-done((bf16[4,2,32,2048]{3,2,0,1:T(8,128)(2,1)}, bf16[4,2,32,2048]{3,2,0,1:T(8,128)(2,1)}, u32[]{:S(2)}, u32[]{:S(2)}) %collective-permute-start.27) | collective-permute-done | bytes 1048608 | tf_op jit(solution)/shard_map/ppermute | solution.py:87
  180.9 3.7 fusion.168
  191.7 4.0 fusion.53
  196.7 7.4 %fusion.167 = (f32[16,512]{1,0:T(8,128)S(1)}, f32[16,512,512]{1,2,0:T(8,128)}) fusion(bf16[512,16,32]{0,2,1:T(8,128)(2,1)S(1)} %get-tuple-element.236, bf16[512,16,32]{0,2,1:T(8,128)(2,1)S(1)} %get-tuple-element.237, bf16[512,16,32]{0,2,1:T(8,128)(2,1)S(1)} %get-tuple-element.118, bf16[512,16,32]{0,2,1:T(8,128)(2,1)S(1)} %get-tuple-element.117, ...), kind=kOutput, calls=%fused_computation.496 | convolution fusion | flops 553639936 | bytes 19169280 | tf_op jit(solution)/shard_map/qhd,khd->hqk/dot_general | solution.py:68
  204.1 8.4 %fusion = f32[16,512]{1,0:T(8,128)S(1)} fusion(f32[16,512,512]{1,2,0:T(8,128)} %get-tuple-element.275, f32[16,512]{1,0:T(8,128)S(1)} %get-tuple-element.274), kind=kLoop, calls=%fused_computation.6 | loop fusion | flops 8380416 | bytes 16842752 | tf_op jit(solution)/shard_map/reduce_sum | solution.py:252
  212.5 8.7 %fusion.82 = bf16[16,64,512]{2,1,0:T(8,128)(2,1)} fusion(f32[16,512,512]{1,2,0:T(8,128)} %get-tuple-element.275, f32[16,512]{1,0:T(8,128)S(1)} %fusion, f32[16,512]{1,0:T(8,128)S(1)} %get-tuple-element.274, f32[512,8,64]{0,2,1:T(8,128)S(1)} %bitcast.629, f32[512,8,64]{0,2,1:T(8,128)S(1)} %bitcast.630, f32[16,64]{1,0:T(8,128)S(1)} %copy-done.62, pred[]{:T(512)S(6)} %eq.18), kind=kOutput, calls=%fused_computation.146 | convolution fusion | flops 552599552 | bytes 19992576 | tf_op jit(solution)/shard_map/hqk,khd->qhd/dot_general | solution.py:255
  228.1 5.8 %multiply_convert_fusion.2 = (bf16[512,2048]{1,0:T(8,128)(2,1)S(1)}, f32[512,2048]{1,0:T(8,128)S(1)}) fusion(f32[2048]{0:T(1024)S(1)} %bitcast.674, bf16[512,1024]{0,1:T(8,128)(2,1)S(1)} %multiply_convert_fusion.3, bf16[1024,2048]{1,0:T(8,128)(2,1)} %bitcast.95), kind=kOutput, calls=%fused_computation.42 | convolution fusion | flops 2157969408 | bytes 11542528 | tf_op jit(solution)/shard_map/dot_general | solution.py:59
  233.9 5.3 fusion.172
  239.3 5.8 %multiply_convert_fusion.1 = (bf16[512,2048]{1,0:T(8,128)(2,1)S(1)}, f32[512,2048]{1,0:T(8,128)S(1)}) fusion(f32[2048]{0:T(1024)S(1)} %bitcast.672, bf16[512,1024]{0,1:T(8,128)(2,1)S(1)} %multiply_convert_fusion.3, bf16[1024,2048]{1,0:T(8,128)(2,1)} %collective-permute-done.34), kind=kOutput, calls=%fused_computation.41 | convolution fusion | flops 2157969408 | bytes 11542528 | tf_op jit(solution)/shard_map/dot_general | solution.py:59
  245.2 5.8 %multiply_reduce_fusion.7 = (f32[512]{0:T(512)S(1)}, f32[512,1024]{0,1:T(8,128)S(1)}) fusion(f32[1024]{0:T(1024)S(1)} %copy-done.70, f32[512,1024]{0,1:T(8,128)S(1)} %fusion.172, bf16[512,2048]{1,0:T(8,128)(2,1)S(1)} %get-tuple-element.278, bf16[2048,1024]{1,0:T(8,128)(2,1)} %collective-permute-done.35), kind=kOutput, calls=%fused_computation.126 | convolution fusion | flops 2149580288 | bytes 10491904 | tf_op jit(solution)/shard_map/dot_general | solution.py:59
  254.4 7.9 %convert_reduce_fusion = (f32[2048]{0:T(1024)S(1)}, bf16[512,2048]{1,0:T(8,128)(2,1)S(1)}) fusion(f32[512,2048]{1,0:T(8,128)S(1)} %get-tuple-element.277, f32[2048]{0:T(1024)S(1)} %bitcast.675, bf16[512,1024]{0,1:T(8,128)(2,1)S(1)} %get-tuple-element.89, bf16[2048,1024]{1,0:T(8,128)(2,1)} %bitcast.121), kind=kOutput, calls=%fused_computation.39 | convolution fusion | flops 2171598848 | bytes 11550720 | tf_op jit(solution)/shard_map/dot_general | solution.py:53
  262.3 5.3 fusion.173
  267.7 7.7 %convert_reduce_fusion.1 = (f32[2048]{0:T(1024)S(1)}, bf16[512,2048]{1,0:T(8,128)(2,1)S(1)}) fusion(f32[512,2048]{1,0:T(8,128)S(1)} %get-tuple-element.279, f32[2048]{0:T(1024)S(1)} %bitcast.673, bf16[512,1024]{0,1:T(8,128)(2,1)S(1)} %get-tuple-element.89, bf16[2048,1024]{1,0:T(8,128)(2,1)} %collective-permute-done.35), kind=kOutput, calls=%fused_computation.40 | convolution fusion | flops 2171598848 | bytes 11550720 | tf_op jit(solution)/shard_map/dot_general | solution.py:53
  275.4 5.7 %multiply_reduce_fusion.2 = (f32[1024]{0:T(1024)S(1)}, f32[512]{0:T(512)S(1)}, f32[512,1024]{0,1:T(8,128)S(1)}) fusion(f32[512,1024]{0,1:T(8,128)S(1)} %get-tuple-element.100, f32[512]{0:T(512)S(1)} %fusion.141, f32[1024]{0:T(1024)S(1)} %mul.501, f32[512,1024]{0,1:T(8,128)S(1)} %fusion.173, bf16[512,2048]{1,0:T(8,128)(2,1)S(1)} %get-tuple-element.85, ...), kind=kOutput, calls=%fused_computation.110 | convolution fusion | flops 2151152128 | bytes 12595200 | tf_op jit(solution)/shard_map/dot_general | solution.py:53
  294.2 12.9 %multiply_reduce_fusion = (f32[16,512]{1,0:T(8,128)S(1)}, f32[16,512,512]{1,2,0:T(8,128)}) fusion(f32[16,512,512]{1,2,0:T(8,128)} %get-tuple-element.275, f32[16,512]{1,0:T(8,128)S(1)} %log_add_fusion, bf16[512,16,64]{0,2,1:T(8,128)(2,1)} %bitcast.616, f32[512,8,64]{0,2,1:T(8,128)} %bitcast.628, f32[512,8,64]{0,2,1:T(8,128)} %bitcast.631, ...), kind=kOutput, calls=%fused_computation.1 | convolution fusion | flops 552067072 | bytes 36769792 | tf_op jit(solution)/shard_map/qhd,khd->hqk/dot_general | solution.py:318
  307.1 12.2 %multiply_convert_fusion = bf16[16,512,512]{1,2,0:T(8,128)(2,1)S(1)} fusion(f32[16,512,512]{1,2,0:T(8,128)} %get-tuple-element.284, f32[16,512,512]{1,2,0:T(8,128)} %get-tuple-element.275, f32[16,512]{1,0:T(8,128)S(1)} %get-tuple-element.283, f32[16,512]{1,0:T(8,128)S(1)} %log_add_fusion), kind=kLoop, calls=%fused_computation | loop fusion | flops 16777216 | bytes 42008576 | tf_op jit(solution)/shard_map/convert_element_type | solution.py:320
  323.4 9.5 %convert_reduce_fusion.4 = (f32[16,64]{1,0:T(8,128)S(1)}, bf16[16,64,512]{2,1,0:T(8,128)(2,1)}) fusion(bf16[512,16,64]{0,2,1:T(8,128)(2,1)S(1)} %bitcast.617, f32[16,512,512]{1,2,0:T(8,128)} %get-tuple-element.275, f32[16,512]{1,0:T(8,128)S(1)} %log_add_fusion), kind=kOutput, calls=%fused_computation.114 | convolution fusion | flops 546831360 | bytes 18911232 | tf_op jit(solution)/shard_map/hqk,qhd->khd/dot_general | solution.py:315
  340.5 3.9 fusion.74
  344.5 5.3 fusion.44
  363.5 5.0 collective-permute-done.49
  369.4 5.7 %collective-permute-done.47 = bf16[4,2,32,512]{3,2,1,0:T(8,128)(2,1)S(1)} collective-permute-done((bf16[4,2,32,512]{3,2,1,0:T(8,128)(2,1)S(1)}, bf16[4,2,32,512]{3,2,1,0:T(8,128)(2,1)S(1)}, u32[]{:S(2)}, u32[]{:S(2)}) %collective-permute-start.47) | collective-permute-done | bytes 262176 | tf_op jit(solution)/shard_map/ppermute | solution.py:87
  375.9 4.1 collective-permute-done.50
  380.9 4.0 collective-permute-done.48
  385.2 6.3 %collective-permute-start.75 = (f32[13440]{0:T(1024)S(1)}, f32[13440]{0:T(1024)S(1)}, u32[]{:S(2)}, u32[]{:S(2)}) collective-permute-start(f32[13440]{0:T(1024)S(1)} %add.470), channel_id=1, source_target_pairs={{0,16},{2,18},{4,20},{6,22},{8,24},{10,26},{12,28},{14,30},{16,0},... | collective-permute-start | bytes 161288 | tf_op jit(solution)/shard_map/ppermute | solution.py:87
  391.6 3.7 collective-permute-start.52
  406.3 5.6 convolution_convert_fusion
  414.6 6.0 %fusion.28 = bf16[2048,1024]{1,0:T(8,128)(2,1)S(1)} fusion(bf16[512,2048]{1,0:T(8,128)(2,1)S(1)} %collective-permute-done.63, bf16[512,2048]{1,0:T(8,128)(2,1)S(1)} %copy-done.84, bf16[512,1024]{0,1:T(8,128)(2,1)} %collective-permute-done.64, bf16[512,1024]{0,1:T(8,128)(2,1)S(1)} %copy-done.44), kind=kOutput, calls=%fused_computation.48 | convolution fusion | flops 4309647360 | bytes 10485760 | tf_op jit(solution)/shard_map/dot_general | solution.py:47
  424.4 6.1 %fusion.31 = bf16[1024,2048]{1,0:T(8,128)(2,1)S(1)} fusion(bf16[512,2048]{1,0:T(8,128)(2,1)S(1)} %collective-permute-done.55, bf16[512,2048]{1,0:T(8,128)(2,1)S(1)} %copy-done.86, bf16[512,1024]{0,1:T(8,128)(2,1)} %collective-permute-done.54, bf16[512,1024]{0,1:T(8,128)(2,1)S(1)} %copy-done.40), kind=kOutput, calls=%fused_computation.49 | convolution fusion | flops 4309647360 | bytes 10485760 | tf_op jit(solution)/shard_map/dot_general | solution.py:47
  435.3 51.1 %collective-permute-done.41 = bf16[4,32,1536]{2,1,0:T(8,128)(2,1)S(1)} collective-permute-done((bf16[4,32,1536]{2,1,0:T(8,128)(2,1)S(1)}, bf16[4,32,1536]{2,1,0:T(8,128)(2,1)S(1)}, u32[]{:S(2)}, u32[]{:S(2)}) %collective-permute-start.41) | collective-permute-done | bytes 393248 | tf_op jit(solution)/shard_map/ppermute | solution.py:87
  487.1 9.2 %collective-permute-done.39 = bf16[4,32,1536]{2,1,0:T(8,128)(2,1)S(1)} collective-permute-done((bf16[4,32,1536]{2,1,0:T(8,128)(2,1)S(1)}, bf16[4,32,1536]{2,1,0:T(8,128)(2,1)S(1)}, u32[]{:S(2)}, u32[]{:S(2)}) %collective-permute-start.39) | collective-permute-done | bytes 393248 | tf_op jit(solution)/shard_map/ppermute | solution.py:87
  503.2 3.6 collective-permute-done.42
  507.5 8.3 %collective-permute-done.43 = bf16[1,2,32,1536]{3,2,1,0:T(8,128)(2,1)S(1)} collective-permute-done((bf16[1,2,32,1536]{3,2,1,0:T(8,128)(2,1)S(1)}, bf16[1,2,32,1536]{3,2,1,0:T(8,128)(2,1)S(1)}, u32[]{:S(2)}, u32[]{:S(2)}) %collective-permute-start.43) | collective-permute-done | bytes 196640 | tf_op jit(solution)/shard_map/ppermute | solution.py:87
  518.4 4.0 collective-permute-done.59
  522.5 7.9 %collective-permute-done.57 = bf16[4,32,2048]{2,1,0:T(8,128)(2,1)S(1)} collective-permute-done((bf16[4,32,2048]{2,1,0:T(8,128)(2,1)S(1)}, bf16[4,32,2048]{2,1,0:T(8,128)(2,1)S(1)}, u32[]{:S(2)}, u32[]{:S(2)}) %collective-permute-start.57) | collective-permute-done | bytes 524320 | tf_op jit(solution)/shard_map/ppermute | solution.py:87
  534.8 15.1 %collective-permute-done.60 = bf16[2,2,32,2048]{3,2,1,0:T(8,128)(2,1)S(1)} collective-permute-done((bf16[2,2,32,2048]{3,2,1,0:T(8,128)(2,1)S(1)}, bf16[2,2,32,2048]{3,2,1,0:T(8,128)(2,1)S(1)}, u32[]{:S(2)}, u32[]{:S(2)}) %collective-permute-start.60) | collective-permute-done | bytes 524320 | tf_op jit(solution)/shard_map/ppermute | solution.py:87
  550.3 12.4 %collective-permute-done.61 = bf16[1,2,32,2048]{3,2,1,0:T(8,128)(2,1)S(1)} collective-permute-done((bf16[1,2,32,2048]{3,2,1,0:T(8,128)(2,1)S(1)}, bf16[1,2,32,2048]{3,2,1,0:T(8,128)(2,1)S(1)}, u32[]{:S(2)}, u32[]{:S(2)}) %collective-permute-start.61) | collective-permute-done | bytes 262176 | tf_op jit(solution)/shard_map/ppermute | solution.py:87
  (579 shorter events, 195.3 us)
Async XLA Ops:
  2.9 49.0 %collective-permute-start.21 = (bf16[32,2048]{1,0:T(8,128)(2,1)}, bf16[32,2048]{1,0:T(8,128)(2,1)}, u32[]{:S(2)}, u32[]{:S(2)}) collective-permute-start(bf16[32,2048]{1,0:T(8,128)(2,1)} %dynamic-slice_bitcast_fusion.22), channel_id=1, source_target_pairs={{0,1},{1,0},{2,3},{3,2},{4,5},{5,4},{6,7},{7,6},{8,9},{9,8},{10,11... | collective-permute-start | bytes 393224 | tf_op jit(solution)/shard_map/ppermute | solution.py:90
  5.6 32.9 %collective-permute-start.13 = (bf16[32,512]{1,0:T(8,128)(2,1)}, bf16[32,512]{1,0:T(8,128)(2,1)}, u32[]{:S(2)}, u32[]{:S(2)}) collective-permute-start(bf16[32,512]{1,0:T(8,128)(2,1)} %bitcast.615), channel_id=1, source_target_pairs={{0,1},{1,0},{2,3},{3,2},{4,5},{5,4},{6,7},{7,6},{8,9},{9,8},{10,11... | collective-permute-start | bytes 98312 | tf_op jit(solution)/shard_map/ppermute | solution.py:90
  7.8 39.6 %collective-permute-start.5 = (bf16[32,1536]{1,0:T(8,128)(2,1)}, bf16[32,1536]{1,0:T(8,128)(2,1)}, u32[]{:S(2)}, u32[]{:S(2)}) collective-permute-start(bf16[32,1536]{1,0:T(8,128)(2,1)} %bitcast.614), channel_id=1, source_target_pairs={{0,1},{1,0},{2,3},{3,2},{4,5},{5,4},{6,7},{7,6},{8,9},{9,8},{10,11... | collective-permute-start | bytes 294920 | tf_op jit(solution)/shard_map/ppermute | solution.py:90
  9.3 49.8 %collective-permute-start.28 = (bf16[1,2,64,1024]{3,2,1,0:T(8,128)(2,1)}, bf16[1,2,64,1024]{3,2,1,0:T(8,128)(2,1)}, u32[]{:S(2)}, u32[]{:S(2)}) collective-permute-start(bf16[1,2,64,1024]{3,2,1,0:T(8,128)(2,1)} %maximum_bitcast_fusion.12), channel_id=1, source_target_pairs={{0,16},{2,18},{4,20},{6,22},{8,24},{10,26},{12,28},{14,30},{16,0},... | collective-permute-start | bytes 786440 | tf_op jit(solution)/shard_map/ppermute | solution.py:87
  48.3 12.7 %collective-permute-start.6 = (bf16[1,2,32,1536]{3,2,1,0:T(8,128)(2,1)S(1)}, bf16[1,2,32,1536]{3,2,1,0:T(8,128)(2,1)S(1)}, u32[]{:S(2)}, u32[]{:S(2)}) collective-permute-start(bf16[1,2,32,1536]{3,2,1,0:T(8,128)(2,1)S(1)} %maximum_bitcast_fusion.13), channel_id=1, source_target_pairs={{0,16},{2,18},{4,20},{6,22},{8,24},{10,26},{12,28},{14,30},{16,0},... | collective-permute-start | bytes 589832 | tf_op jit(solution)/shard_map/ppermute | solution.py:87
  52.9 13.0 %collective-permute-start.22 = (bf16[1,2,32,2048]{3,2,1,0:T(8,128)(2,1)S(1)}, bf16[1,2,32,2048]{3,2,1,0:T(8,128)(2,1)S(1)}, u32[]{:S(2)}, u32[]{:S(2)}) collective-permute-start(bf16[1,2,32,2048]{3,2,1,0:T(8,128)(2,1)S(1)} %maximum_bitcast_fusion.11), channel_id=1, source_target_pairs={{0,16},{2,18},{4,20},{6,22},{8,24},{10,26},{12,28},{14,30},{16,0},... | collective-permute-start | bytes 786440 | tf_op jit(solution)/shard_map/ppermute | solution.py:87
  60.1 26.6 %collective-permute-start.29 = (bf16[2,2,64,1024]{3,2,1,0:T(8,128)(2,1)S(1)}, bf16[2,2,64,1024]{3,2,1,0:T(8,128)(2,1)S(1)}, u32[]{:S(2)}, u32[]{:S(2)}) collective-permute-start(bf16[2,2,64,1024]{3,2,1,0:T(8,128)(2,1)S(1)} %maximum_bitcast_fusion.9), channel_id=1, source_target_pairs={{0,8},{2,10},{4,12},{6,14},{8,0},{10,2},{12,4},{14,6},{16,24},{18,... | collective-permute-start | bytes 1572872 | tf_op jit(solution)/shard_map/ppermute | solution.py:87
  61.1 23.8 %collective-permute-start.7 = (bf16[2,2,32,1536]{3,2,1,0:T(8,128)(2,1)S(1)}, bf16[2,2,32,1536]{3,2,1,0:T(8,128)(2,1)S(1)}, u32[]{:S(2)}, u32[]{:S(2)}) collective-permute-start(bf16[2,2,32,1536]{3,2,1,0:T(8,128)(2,1)S(1)} %maximum_bitcast_fusion.10), channel_id=1, source_target_pairs={{0,8},{2,10},{4,12},{6,14},{8,0},{10,2},{12,4},{14,6},{16,24},{18,... | collective-permute-start | bytes 1179656 | tf_op jit(solution)/shard_map/ppermute | solution.py:87
  65.9 25.4 %collective-permute-start.23 = (bf16[2,2,32,2048]{3,2,1,0:T(8,128)(2,1)S(1)}, bf16[2,2,32,2048]{3,2,1,0:T(8,128)(2,1)S(1)}, u32[]{:S(2)}, u32[]{:S(2)}) collective-permute-start(bf16[2,2,32,2048]{3,2,1,0:T(8,128)(2,1)S(1)} %maximum_bitcast_fusion.8), channel_id=1, source_target_pairs={{0,8},{2,10},{4,12},{6,14},{8,0},{10,2},{12,4},{14,6},{16,24},{18,... | collective-permute-start | bytes 1572872 | tf_op jit(solution)/shard_map/ppermute | solution.py:87
  71.5 152.6 %collective-permute-start.20 = (bf16[1024,512]{1,0:T(8,128)(2,1)}, bf16[1024,512]{1,0:T(8,128)(2,1)}, u32[]{:S(2)}, u32[]{:S(2)}) collective-permute-start(bf16[1024,512]{1,0:T(8,128)(2,1)} %bitcast.67), channel_id=1, source_target_pairs={{0,1},{1,0},{2,3},{3,2},{4,5},{5,4},{6,7},{7,6},{8,9},{9,8},{10,11... | collective-permute-start | bytes 3145736 | tf_op jit(solution)/shard_map/ppermute | solution.py:90
  85.7 11.7 %collective-permute-start.8 = (bf16[4,32,1536]{2,1,0:T(8,128)(2,1)S(1)}, bf16[4,32,1536]{2,1,0:T(8,128)(2,1)S(1)}, u32[]{:S(2)}, u32[]{:S(2)}) collective-permute-start(bf16[4,32,1536]{2,1,0:T(8,128)(2,1)S(1)} %get-tuple-element.178), channel_id=1, source_target_pairs={{0,2},{2,0},{4,6},{6,4},{8,10},{10,8},{12,14},{14,12},{16,18},{18,... | collective-permute-start | bytes 1179656 | tf_op jit(solution)/shard_map/ppermute | solution.py:87
  86.9 20.8 %collective-permute-start.30 = (bf16[4,64,1024]{2,1,0:T(8,128)(2,1)S(1)}, bf16[4,64,1024]{2,1,0:T(8,128)(2,1)S(1)}, u32[]{:S(2)}, u32[]{:S(2)}) collective-permute-start(bf16[4,64,1024]{2,1,0:T(8,128)(2,1)S(1)} %get-tuple-element.164), channel_id=1, source_target_pairs={{0,2},{2,0},{4,6},{6,4},{8,10},{10,8},{12,14},{14,12},{16,18},{18,... | collective-permute-start | bytes 1572872 | tf_op jit(solution)/shard_map/ppermute | solution.py:87
  91.4 16.8 %collective-permute-start.32 = (bf16[4,64,1024]{2,1,0:T(8,128)(2,1)S(1)}, bf16[4,64,1024]{2,1,0:T(8,128)(2,1)S(1)}, u32[]{:S(2)}, u32[]{:S(2)}) collective-permute-start(bf16[4,64,1024]{2,1,0:T(8,128)(2,1)S(1)} %get-tuple-element.165), channel_id=1, source_target_pairs={{0,4},{2,6},{4,0},{6,2},{8,12},{10,14},{12,8},{14,10},{16,20},{18,... | collective-permute-start | bytes 1572872 | tf_op jit(solution)/shard_map/ppermute | solution.py:87
  95.9 23.0 %collective-permute-start.24 = (bf16[4,32,2048]{2,1,0:T(8,128)(2,1)S(1)}, bf16[4,32,2048]{2,1,0:T(8,128)(2,1)S(1)}, u32[]{:S(2)}, u32[]{:S(2)}) collective-permute-start(bf16[4,32,2048]{2,1,0:T(8,128)(2,1)S(1)} %get-tuple-element.170), channel_id=1, source_target_pairs={{0,2},{2,0},{4,6},{6,4},{8,10},{10,8},{12,14},{14,12},{16,18},{18,... | collective-permute-start | bytes 1572872 | tf_op jit(solution)/shard_map/ppermute | solution.py:87
  97.4 22.8 %collective-permute-start.26 = (bf16[4,32,2048]{2,1,0:T(8,128)(2,1)S(1)}, bf16[4,32,2048]{2,1,0:T(8,128)(2,1)S(1)}, u32[]{:S(2)}, u32[]{:S(2)}) collective-permute-start(bf16[4,32,2048]{2,1,0:T(8,128)(2,1)S(1)} %get-tuple-element.171), channel_id=1, source_target_pairs={{0,4},{2,6},{4,0},{6,2},{8,12},{10,14},{12,8},{14,10},{16,20},{18,... | collective-permute-start | bytes 1572872 | tf_op jit(solution)/shard_map/ppermute | solution.py:87
  107.7 27.5 %collective-permute-start.9 = (bf16[4,2,32,1536]{3,2,0,1:T(8,128)(2,1)S(1)}, bf16[4,2,32,1536]{3,2,0,1:T(8,128)(2,1)S(1)}, u32[]{:S(2)}, u32[]{:S(2)}) collective-permute-start(bf16[4,2,32,1536]{3,2,0,1:T(8,128)(2,1)S(1)} %pad_maximum_fusion.14), channel_id=1, source_target_pairs={{0,4},{2,6},{4,0},{6,2},{8,12},{10,14},{12,8},{14,10},{16,20},{18,... | collective-permute-start | bytes 2359304 | tf_op jit(solution)/shard_map/ppermute | solution.py:87
  108.2 27.8 %collective-permute-start.11 = (bf16[4,2,32,1536]{3,2,0,1:T(8,128)(2,1)S(1)}, bf16[4,2,32,1536]{3,2,0,1:T(8,128)(2,1)S(1)}, u32[]{:S(2)}, u32[]{:S(2)}) collective-permute-start(bf16[4,2,32,1536]{3,2,0,1:T(8,128)(2,1)S(1)} %pad_maximum_fusion.15), channel_id=1, source_target_pairs={{0,2},{2,0},{4,6},{6,4},{8,10},{10,8},{12,14},{14,12},{16,18},{18,... | collective-permute-start | bytes 2359304 | tf_op jit(solution)/shard_map/ppermute | solution.py:87
  119.0 39.4 %collective-permute-start.33 = (bf16[4,2,64,1024]{3,2,0,1:T(8,128)(2,1)}, bf16[4,2,64,1024]{3,2,0,1:T(8,128)(2,1)}, u32[]{:S(2)}, u32[]{:S(2)}) collective-permute-start(bf16[4,2,64,1024]{3,2,0,1:T(8,128)(2,1)} %pad_maximum_fusion.12), channel_id=1, source_target_pairs={{0,2},{2,0},{4,6},{6,4},{8,10},{10,8},{12,14},{14,12},{16,18},{18,... | collective-permute-start | bytes 3145736 | tf_op jit(solution)/shard_map/ppermute | solution.py:87
  120.2 40.3 %collective-permute-start.31 = (bf16[4,2,64,1024]{3,2,0,1:T(8,128)(2,1)}, bf16[4,2,64,1024]{3,2,0,1:T(8,128)(2,1)}, u32[]{:S(2)}, u32[]{:S(2)}) collective-permute-start(bf16[4,2,64,1024]{3,2,0,1:T(8,128)(2,1)} %pad_maximum_fusion.11), channel_id=1, source_target_pairs={{0,4},{2,6},{4,0},{6,2},{8,12},{10,14},{12,8},{14,10},{16,20},{18,... | collective-permute-start | bytes 3145736 | tf_op jit(solution)/shard_map/ppermute | solution.py:87
  135.3 38.2 %collective-permute-start.27 = (bf16[4,2,32,2048]{3,2,0,1:T(8,128)(2,1)}, bf16[4,2,32,2048]{3,2,0,1:T(8,128)(2,1)}, u32[]{:S(2)}, u32[]{:S(2)}) collective-permute-start(bf16[4,2,32,2048]{3,2,0,1:T(8,128)(2,1)} %pad_maximum_fusion.9), channel_id=1, source_target_pairs={{0,2},{2,0},{4,6},{6,4},{8,10},{10,8},{12,14},{14,12},{16,18},{18,... | collective-permute-start | bytes 3145736 | tf_op jit(solution)/shard_map/ppermute | solution.py:87
  138.5 42.3 %collective-permute-start.12 = (bf16[1024,1536]{1,0:T(8,128)(2,1)}, bf16[1024,1536]{1,0:T(8,128)(2,1)}, u32[]{:S(2)}, u32[]{:S(2)}) collective-permute-start(bf16[1024,1536]{1,0:T(8,128)(2,1)} %bitcast.35), channel_id=1, source_target_pairs={{0,1},{1,0},{2,3},{3,2},{4,5},{5,4},{6,7},{7,6},{8,9},{9,8},{10,11... | collective-permute-start | bytes 9437192 | tf_op jit(solution)/shard_map/ppermute | solution.py:90
  158.4 19.1 %collective-permute-start.25 = (bf16[4,2,32,2048]{3,2,0,1:T(8,128)(2,1)}, bf16[4,2,32,2048]{3,2,0,1:T(8,128)(2,1)S(1)}, u32[]{:S(2)}, u32[]{:S(2)}) collective-permute-start(bf16[4,2,32,2048]{3,2,0,1:T(8,128)(2,1)} %pad_maximum_fusion.8), channel_id=1, source_target_pairs={{0,4},{2,6},{4,0},{6,2},{8,12},{10,14},{12,8},{14,10},{16,20},{18,... | collective-permute-start | bytes 3145736 | tf_op jit(solution)/shard_map/ppermute | solution.py:87
  165.2 80.0 %collective-permute-start.35 = (bf16[2048,1024]{1,0:T(8,128)(2,1)}, bf16[2048,1024]{1,0:T(8,128)(2,1)}, u32[]{:S(2)}, u32[]{:S(2)}) collective-permute-start(bf16[2048,1024]{1,0:T(8,128)(2,1)} %bitcast.121), channel_id=1, source_target_pairs={{0,1},{1,0},{2,3},{3,2},{4,5},{5,4},{6,7},{7,6},{8,9},{9,8},{10,11... | collective-permute-start | bytes 12582920 | tf_op jit(solution)/shard_map/ppermute | solution.py:90
  180.9 58.4 %collective-permute-start.34 = (bf16[1024,2048]{1,0:T(8,128)(2,1)}, bf16[1024,2048]{1,0:T(8,128)(2,1)}, u32[]{:S(2)}, u32[]{:S(2)}) collective-permute-start(bf16[1024,2048]{1,0:T(8,128)(2,1)} %bitcast.95), channel_id=1, source_target_pairs={{0,1},{1,0},{2,3},{3,2},{4,5},{5,4},{6,7},{7,6},{8,9},{9,8},{10,11... | collective-permute-start | bytes 12582920 | tf_op jit(solution)/shard_map/ppermute | solution.py:90
  223.5 134.1 %collective-permute-start.45 = (bf16[512,1024]{0,1:T(8,128)(2,1)}, bf16[512,1024]{0,1:T(8,128)(2,1)}, u32[]{:S(2)}, u32[]{:S(2)}) collective-permute-start(bf16[512,1024]{0,1:T(8,128)(2,1)} %bitcast.44), channel_id=1, source_target_pairs={{0,1},{1,0},{2,3},{3,2},{4,5},{5,4},{6,7},{7,6},{8,9},{9,8},{10,11... | collective-permute-start | bytes 3145736 | tf_op jit(solution)/shard_map/ppermute | solution.py:90
  333.0 24.7 %collective-permute-start.46 = (bf16[512,512]{0,1:T(8,128)(2,1)}, bf16[512,512]{0,1:T(8,128)(2,1)}, u32[]{:S(2)}, u32[]{:S(2)}) collective-permute-start(bf16[512,512]{0,1:T(8,128)(2,1)} %get-tuple-element.160), channel_id=1, source_target_pairs={{0,1},{1,0},{2,3},{3,2},{4,5},{5,4},{6,7},{7,6},{8,9},{9,8},{10,11... | collective-permute-start | bytes 1572872 | tf_op jit(solution)/shard_map/ppermute | solution.py:90
  353.7 52.1 %collective-permute-start.36 = (bf16[512,1024]{0,1:T(8,128)(2,1)}, bf16[512,1024]{0,1:T(8,128)(2,1)}, u32[]{:S(2)}, u32[]{:S(2)}) collective-permute-start(bf16[512,1024]{0,1:T(8,128)(2,1)} %fusion.43), channel_id=1, source_target_pairs={{0,1},{1,0},{2,3},{3,2},{4,5},{5,4},{6,7},{7,6},{8,9},{9,8},{10,11... | collective-permute-start | bytes 3145736 | tf_op jit(solution)/shard_map/ppermute | solution.py:90
  353.8 69.0 %collective-permute-start.54 = (bf16[512,1024]{0,1:T(8,128)(2,1)}, bf16[512,1024]{0,1:T(8,128)(2,1)}, u32[]{:S(2)}, u32[]{:S(2)}) collective-permute-start(bf16[512,1024]{0,1:T(8,128)(2,1)} %copy-done.39), channel_id=1, source_target_pairs={{0,1},{1,0},{2,3},{3,2},{4,5},{5,4},{6,7},{7,6},{8,9},{9,8},{10,11... | collective-permute-start | bytes 3145736 | tf_op jit(solution)/shard_map/ppermute | solution.py:90
  363.4 42.9 %collective-permute-start.37 = (bf16[512,1536]{0,1:T(8,128)(2,1)}, bf16[512,1536]{0,1:T(8,128)(2,1)}, u32[]{:S(2)}, u32[]{:S(2)}) collective-permute-start(bf16[512,1536]{0,1:T(8,128)(2,1)} %pad_maximum_fusion.3), channel_id=1, source_target_pairs={{0,1},{1,0},{2,3},{3,2},{4,5},{5,4},{6,7},{7,6},{8,9},{9,8},{10,11... | collective-permute-start | bytes 4718600 | tf_op jit(solution)/shard_map/ppermute | solution.py:90
  363.4 21.8 %collective-permute-start.74 = (f32[13440]{0:T(1024)S(1)}, f32[13440]{0:T(1024)S(1)}, u32[]{:S(2)}, u32[]{:S(2)}) collective-permute-start(f32[13440]{0:T(1024)S(1)} %add.469), channel_id=1, source_target_pairs={{0,8},{2,10},{4,12},{6,14},{8,0},{10,2},{12,4},{14,6},{16,24},{18,... | collective-permute-start | bytes 161288 | tf_op jit(solution)/shard_map/ppermute | solution.py:87
  385.2 16.6 %collective-permute-start.75 = (f32[13440]{0:T(1024)S(1)}, f32[13440]{0:T(1024)S(1)}, u32[]{:S(2)}, u32[]{:S(2)}) collective-permute-start(f32[13440]{0:T(1024)S(1)} %add.470), channel_id=1, source_target_pairs={{0,16},{2,18},{4,20},{6,22},{8,24},{10,26},{12,28},{14,30},{16,0},... | collective-permute-start | bytes 161288 | tf_op jit(solution)/shard_map/ppermute | solution.py:87
  401.8 12.0 %collective-permute-start.64 = (bf16[512,1024]{0,1:T(8,128)(2,1)S(1)}, bf16[512,1024]{0,1:T(8,128)(2,1)}, u32[]{:S(2)}, u32[]{:S(2)}) collective-permute-start(bf16[512,1024]{0,1:T(8,128)(2,1)S(1)} %copy-done.44), channel_id=1, source_target_pairs={{0,1},{1,0},{2,3},{3,2},{4,5},{5,4},{6,7},{7,6},{8,9},{9,8},{10,11... | collective-permute-start | bytes 3145736 | tf_op jit(solution)/shard_map/ppermute | solution.py:90
  405.8 17.9 %collective-permute-start.55 = (bf16[512,2048]{1,0:T(8,128)(2,1)}, bf16[512,2048]{1,0:T(8,128)(2,1)S(1)}, u32[]{:S(2)}, u32[]{:S(2)}) collective-permute-start(bf16[512,2048]{1,0:T(8,128)(2,1)} %copy-done.82), channel_id=1, source_target_pairs={{0,1},{1,0},{2,3},{3,2},{4,5},{5,4},{6,7},{7,6},{8,9},{9,8},{10,11... | collective-permute-start | bytes 6291464 | tf_op jit(solution)/shard_map/ppermute | solution.py:90
  412.2 20.5 %collective-permute-start.40 = (bf16[4,2,32,1536]{3,2,1,0:T(8,128)(2,1)S(1)}, bf16[4,2,32,1536]{3,2,1,0:T(8,128)(2,1)S(1)}, u32[]{:S(2)}, u32[]{:S(2)}) collective-permute-start(bf16[4,2,32,1536]{3,2,1,0:T(8,128)(2,1)S(1)} %dynamic-slice_bitcast_fusion.2), channel_id=1, source_target_pairs={{0,2},{2,0},{4,6},{6,4},{8,10},{10,8},{12,14},{14,12},{16,18},{18,... | collective-permute-start | bytes 2359304 | tf_op jit(solution)/shard_map/ppermute | solution.py:87
  413.8 20.5 %collective-permute-start.38 = (bf16[4,2,32,1536]{3,2,1,0:T(8,128)(2,1)S(1)}, bf16[4,2,32,1536]{3,2,1,0:T(8,128)(2,1)S(1)}, u32[]{:S(2)}, u32[]{:S(2)}) collective-permute-start(bf16[4,2,32,1536]{3,2,1,0:T(8,128)(2,1)S(1)} %dynamic-slice_bitcast_fusion.3), channel_id=1, source_target_pairs={{0,4},{2,6},{4,0},{6,2},{8,12},{10,14},{12,8},{14,10},{16,20},{18,... | collective-permute-start | bytes 2359304 | tf_op jit(solution)/shard_map/ppermute | solution.py:87
  421.4 77.6 %collective-permute-start.67 = (bf16[4,2,64,1024]{3,2,0,1:T(8,128)(2,1)S(1)}, bf16[4,2,64,1024]{3,2,0,1:T(8,128)(2,1)S(1)}, u32[]{:S(2)}, u32[]{:S(2)}) collective-permute-start(bf16[4,2,64,1024]{3,2,0,1:T(8,128)(2,1)S(1)} %bitcast.650), channel_id=1, source_target_pairs={{0,2},{2,0},{4,6},{6,4},{8,10},{10,8},{12,14},{14,12},{16,18},{18,... | collective-permute-start | bytes 3145736 | tf_op jit(solution)/shard_map/ppermute | solution.py:87
  422.8 77.6 %collective-permute-start.65 = (bf16[4,2,64,1024]{3,2,0,1:T(8,128)(2,1)S(1)}, bf16[4,2,64,1024]{3,2,0,1:T(8,128)(2,1)S(1)}, u32[]{:S(2)}, u32[]{:S(2)}) collective-permute-start(bf16[4,2,64,1024]{3,2,0,1:T(8,128)(2,1)S(1)} %bitcast.649), channel_id=1, source_target_pairs={{0,4},{2,6},{4,0},{6,2},{8,12},{10,14},{12,8},{14,10},{16,20},{18,... | collective-permute-start | bytes 3145736 | tf_op jit(solution)/shard_map/ppermute | solution.py:87
  430.9 71.0 %collective-permute-start.58 = (bf16[4,2,32,2048]{3,2,1,0:T(8,128)(2,1)S(1)}, bf16[4,2,32,2048]{3,2,1,0:T(8,128)(2,1)S(1)}, u32[]{:S(2)}, u32[]{:S(2)}) collective-permute-start(bf16[4,2,32,2048]{3,2,1,0:T(8,128)(2,1)S(1)} %dynamic-slice_bitcast_fusion), channel_id=1, source_target_pairs={{0,2},{2,0},{4,6},{6,4},{8,10},{10,8},{12,14},{14,12},{16,18},{18,... | collective-permute-start | bytes 3145736 | tf_op jit(solution)/shard_map/ppermute | solution.py:87
  432.6 74.4 %collective-permute-start.56 = (bf16[4,2,32,2048]{3,2,1,0:T(8,128)(2,1)S(1)}, bf16[4,2,32,2048]{3,2,1,0:T(8,128)(2,1)S(1)}, u32[]{:S(2)}, u32[]{:S(2)}) collective-permute-start(bf16[4,2,32,2048]{3,2,1,0:T(8,128)(2,1)S(1)} %dynamic-slice_bitcast_fusion.1), channel_id=1, source_target_pairs={{0,4},{2,6},{4,0},{6,2},{8,12},{10,14},{12,8},{14,10},{16,20},{18,... | collective-permute-start | bytes 3145736 | tf_op jit(solution)/shard_map/ppermute | solution.py:87
  434.3 52.1 %collective-permute-start.41 = (bf16[4,32,1536]{2,1,0:T(8,128)(2,1)S(1)}, bf16[4,32,1536]{2,1,0:T(8,128)(2,1)S(1)}, u32[]{:S(2)}, u32[]{:S(2)}) collective-permute-start(bf16[4,32,1536]{2,1,0:T(8,128)(2,1)S(1)} %dynamic-slice_bitcast_fusion.16), channel_id=1, source_target_pairs={{0,4},{2,6},{4,0},{6,2},{8,12},{10,14},{12,8},{14,10},{16,20},{18,... | collective-permute-start | bytes 1179656 | tf_op jit(solution)/shard_map/ppermute | solution.py:87
  499.5 17.8 %collective-permute-start.68 = (bf16[4,64,1024]{2,1,0:T(8,128)(2,1)S(1)}, bf16[4,64,1024]{2,1,0:T(8,128)(2,1)S(1)}, u32[]{:S(2)}, u32[]{:S(2)}) collective-permute-start(bf16[4,64,1024]{2,1,0:T(8,128)(2,1)S(1)} %dynamic-slice_bitcast_fusion.4), channel_id=1, source_target_pairs={{0,4},{2,6},{4,0},{6,2},{8,12},{10,14},{12,8},{14,10},{16,20},{18,... | collective-permute-start | bytes 1572872 | tf_op jit(solution)/shard_map/ppermute | solution.py:87
  500.8 16.7 %collective-permute-start.66 = (bf16[4,64,1024]{2,1,0:T(8,128)(2,1)S(1)}, bf16[4,64,1024]{2,1,0:T(8,128)(2,1)S(1)}, u32[]{:S(2)}, u32[]{:S(2)}) collective-permute-start(bf16[4,64,1024]{2,1,0:T(8,128)(2,1)S(1)} %dynamic-slice_bitcast_fusion.5), channel_id=1, source_target_pairs={{0,2},{2,0},{4,6},{6,4},{8,10},{10,8},{12,14},{14,12},{16,18},{18,... | collective-permute-start | bytes 1572872 | tf_op jit(solution)/shard_map/ppermute | solution.py:87
  502.4 20.0 %collective-permute-start.59 = (bf16[4,32,2048]{2,1,0:T(8,128)(2,1)S(1)}, bf16[4,32,2048]{2,1,0:T(8,128)(2,1)S(1)}, u32[]{:S(2)}, u32[]{:S(2)}) collective-permute-start(bf16[4,32,2048]{2,1,0:T(8,128)(2,1)S(1)} %dynamic-slice_bitcast_fusion.6), channel_id=1, source_target_pairs={{0,4},{2,6},{4,0},{6,2},{8,12},{10,14},{12,8},{14,10},{16,20},{18,... | collective-permute-start | bytes 1572872 | tf_op jit(solution)/shard_map/ppermute | solution.py:87
  516.0 14.4 %collective-permute-start.57 = (bf16[4,32,2048]{2,1,0:T(8,128)(2,1)S(1)}, bf16[4,32,2048]{2,1,0:T(8,128)(2,1)S(1)}, u32[]{:S(2)}, u32[]{:S(2)}) collective-permute-start(bf16[4,32,2048]{2,1,0:T(8,128)(2,1)S(1)} %dynamic-slice_bitcast_fusion.7), channel_id=1, source_target_pairs={{0,2},{2,0},{4,6},{6,4},{8,10},{10,8},{12,14},{14,12},{16,18},{18,... | collective-permute-start | bytes 1572872 | tf_op jit(solution)/shard_map/ppermute | solution.py:87
  517.9 15.4 %collective-permute-start.69 = (bf16[2,2,64,1024]{3,2,0,1:T(8,128)(2,1)S(1)}, bf16[2,2,64,1024]{3,2,0,1:T(8,128)(2,1)S(1)}, u32[]{:S(2)}, u32[]{:S(2)}) collective-permute-start(bf16[2,2,64,1024]{3,2,0,1:T(8,128)(2,1)S(1)} %fusion.104), channel_id=1, source_target_pairs={{0,8},{2,10},{4,12},{6,14},{8,0},{10,2},{12,4},{14,6},{16,24},{18,... | collective-permute-start | bytes 1572872 | tf_op jit(solution)/shard_map/ppermute | solution.py:87
  530.7 19.2 %collective-permute-start.60 = (bf16[2,2,32,2048]{3,2,1,0:T(8,128)(2,1)S(1)}, bf16[2,2,32,2048]{3,2,1,0:T(8,128)(2,1)S(1)}, u32[]{:S(2)}, u32[]{:S(2)}) collective-permute-start(bf16[2,2,32,2048]{3,2,1,0:T(8,128)(2,1)S(1)} %bitcast.655), channel_id=1, source_target_pairs={{0,8},{2,10},{4,12},{6,14},{8,0},{10,2},{12,4},{14,6},{16,24},{18,... | collective-permute-start | bytes 1572872 | tf_op jit(solution)/shard_map/ppermute | solution.py:87
  533.5 16.7 %collective-permute-start.70 = (bf16[1,2,64,1024]{3,2,0,1:T(8,128)(2,1)S(1)}, bf16[1,2,64,1024]{3,2,0,1:T(8,128)(2,1)S(1)}, u32[]{:S(2)}, u32[]{:S(2)}) collective-permute-start(bf16[1,2,64,1024]{3,2,0,1:T(8,128)(2,1)S(1)} %constant_dynamic-slice_fusion), channel_id=1, source_target_pairs={{0,16},{2,18},{4,20},{6,22},{8,24},{10,26},{12,28},{14,30},{16,0},... | collective-permute-start | bytes 786440 | tf_op jit(solution)/shard_map/ppermute | solution.py:87
  550.1 12.6 %collective-permute-start.61 = (bf16[1,2,32,2048]{3,2,1,0:T(8,128)(2,1)S(1)}, bf16[1,2,32,2048]{3,2,1,0:T(8,128)(2,1)S(1)}, u32[]{:S(2)}, u32[]{:S(2)}) collective-permute-start(bf16[1,2,32,2048]{3,2,1,0:T(8,128)(2,1)S(1)} %constant_dynamic-slice_fusion.6), channel_id=1, source_target_pairs={{0,16},{2,18},{4,20},{6,22},{8,24},{10,26},{12,28},{14,30},{16,0},... | collective-permute-start | bytes 786440 | tf_op jit(solution)/shard_map/ppermute | solution.py:87
  (115 other events, 978.6 us)

commit v2 on v1

--- a/solution.py
+++ b/solution.py
@@ -1,6 +1,10 @@
 import jax
 import jax.numpy as jnp
+import functools
+
 from jax import lax
+from jax.experimental import pallas as pl
+from jax.experimental.pallas import tpu as pltpu
 from jax.sharding import PartitionSpec as P
 
 HEAD = 64
@@ -166,7 +170,7 @@
         return jnp.stack([left, right], axis=1)
 
 
-def shards(
+def shards_any(
     activations,
     segment_ids,
     cotangent,
@@ -394,6 +398,902 @@
     )
 
 
+F32 = jnp.float32
+BF16 = jnp.bfloat16
+I32 = jnp.int32
+EPS = 1e-06
+VMEM_LIMIT = 60 * 1024 * 1024
+LANES = 128
+GELU_A = 0.7978845608028654
+GELU_B = 0.044715
+
+
+def whole_spec():
+    return pl.BlockSpec(memory_space=pltpu.VMEM)
+
+
+def hbm_spec():
+    return pl.BlockSpec(memory_space=pl.ANY)
+
+
+def smem_spec():
+    return pl.BlockSpec(memory_space=pltpu.SMEM)
+
+
+def params():
+    return pltpu.CompilerParams(vmem_limit_bytes=VMEM_LIMIT)
+
+
+def shape(dims, dtype):
+    return jax.ShapeDtypeStruct(dims, dtype)
+
+
+def cost(flops, bytes_accessed):
+    return pl.CostEstimate(flops=flops, bytes_accessed=bytes_accessed, transcendentals=0)
+
+
+def dot(a, b):
+    return lax.dot_general(a, b, (((1,), (0,)), ((), ())), preferred_element_type=F32)
+
+
+def dot_t(a, b):
+    return lax.dot_general(a, b, (((1,), (1,)), ((), ())), preferred_element_type=F32)
+
+
+def t_dot(a, b):
+    return lax.dot_general(a, b, (((0,), (0,)), ((), ())), preferred_element_type=F32)
+
+
+def pair_mask(place):
+    return place // 4 + 4 * (place % 4)
+
+
+def stack_rows(refs):
+    return jnp.concatenate([ref[...].reshape(-1, ref.shape[-1]) for ref in refs], axis=0)
+
+
+def inverse_rms(v):
+    return lax.rsqrt(jnp.mean(v * v, axis=-1, keepdims=True) + EPS)
+
+
+def rms_back(v, r, gain, e):
+    ge = gain * e
+    return r * ge - v * (r * r * r) * jnp.mean(v * ge, axis=-1, keepdims=True)
+
+
+def row_sum(v):
+    return jnp.sum(v, axis=0, keepdims=True)
+
+
+def turn(v, cosine, sine):
+    lane = lax.broadcasted_iota(I32, v.shape, 1)
+    swapped = jnp.where((lane & 63) < 32, pltpu.roll(v, 96, 1), pltpu.roll(v, 32, 1))
+    return v * cosine + swapped * sine
+
+
+def project_kernel(rope, x_own, x_sib, *refs):
+    own, sib = refs[:5], refs[5:10]
+    bias = refs[10]
+    out = refs[-1]
+    y = dot(x_own[...], stack_rows(own)) + dot(x_sib[...], stack_rows(sib)) + bias[...]
+    if rope:
+        cosine, sine = refs[11][...], refs[12][...]
+        scale = jnp.where(pl.program_id(0) == 0, 0.125, 1.0)
+        for c in range(0, y.shape[1], LANES):
+            out[:, c : c + LANES] = (turn(y[:, c : c + LANES], cosine, sine) * scale).astype(BF16)
+    else:
+        out[...] = y.astype(BF16)
+
+
+def project(x_own, x_sib, pieces, first, tiles, bias, tables=()):
+    t, half = x_own.shape
+    tn = 1024
+    weights = [
+        pl.BlockSpec((*p.shape[:2], tn), lambda i, f=first: (0, 0, i + f)) for p in pieces
+    ]
+    return pl.pallas_call(
+        functools.partial(project_kernel, bool(tables)),
+        grid=(tiles,),
+        in_specs=[pl.BlockSpec((t, half), lambda i: (0, 0))] * 2
+        + weights
+        + [pl.BlockSpec((1, tn), lambda i: (0, i))]
+        + [pl.BlockSpec((t, LANES), lambda i: (0, 0))] * len(tables),
+        out_specs=pl.BlockSpec((t, tn), lambda i: (0, i)),
+        out_shape=shape((t, tiles * tn), BF16),
+        compiler_params=params(),
+        cost_estimate=cost(4 * t * half * tiles * tn, 2 * tiles * 2 * half * tn),
+        name="project",
+    )(x_own, x_sib, *pieces, bias, *tables)
+
+
+def attend_kernel(q_ref, k_ref, v_ref, col_ref, row_ref, out_ref, lse_ref, open_ref):
+    t = q_ref.shape[0]
+    tile = 128
+
+    @pl.when(pl.program_id(0) == 0)
+    def _():
+        rows = lax.broadcasted_iota(I32, (t, t), 0)
+        cols = lax.broadcasted_iota(I32, (t, t), 1)
+        ok = (col_ref[...] == row_ref[...]) & (cols <= rows)
+        open_ref[...] = jnp.where(ok, 0.0, -1e30)
+
+    for i in range(t // tile):
+        rows = slice(i * tile, (i + 1) * tile)
+        seen = (i + 1) * tile
+        outs, sums = [], []
+        for h in range(2):
+            lanes = slice(h * HEAD, (h + 1) * HEAD)
+            s = dot_t(q_ref[rows, lanes], k_ref[:seen, lanes]) + open_ref[rows, :seen]
+            peak = jnp.max(s, axis=-1, keepdims=True)
+            e = jnp.exp(s - peak)
+            total = jnp.sum(e, axis=-1, keepdims=True)
+            outs.append(dot(e.astype(BF16), v_ref[:seen, lanes]) / total)
+            sums.append(jnp.broadcast_to(peak + jnp.log(total), (tile, HEAD)))
+        out_ref[rows, :] = jnp.concatenate(outs, axis=1).astype(BF16)
+        lse_ref[rows, :] = jnp.concatenate(sums, axis=1)
+
+
+def attend(qk, v, col, row):
+    t, width = v.shape
+    steps = width // LANES
+    block = lambda f: pl.BlockSpec((t, LANES), f)
+    return pl.pallas_call(
+        attend_kernel,
+        grid=(steps,),
+        in_specs=[
+            block(lambda i: (0, i)),
+            block(lambda i: (0, i + steps)),
+            block(lambda i: (0, i)),
+            pl.BlockSpec((t, 1), lambda i: (0, 0)),
+            pl.BlockSpec((1, t), lambda i: (0, 0)),
+        ],
+        out_specs=[block(lambda i: (0, i))] * 2,
+        out_shape=[shape((t, width), BF16), shape((t, width), F32)],
+        scratch_shapes=[pltpu.VMEM((t, t), F32)],
+        compiler_params=params(),
+        cost_estimate=cost(4 * t * t * width, 10 * t * width),
+        name="attend",
+    )(qk, qk, v, col, row)
+
+
+def attend_back_kernel(
+    q_ref, k_ref, v_ref, dm_ref, lse_ref, col_ref, row_ref, cos_ref, sin_ref,
+    dq_ref, dk_ref, dv_ref, sum_ref, open_ref, ak_ref, av_ref,
+):
+    t = q_ref.shape[0]
+    tile = 128
+
+    @pl.when(pl.program_id(0) == 0)
+    def _():
+        rows = lax.broadcasted_iota(I32, (t, t), 0)
+        cols = lax.broadcasted_iota(I32, (t, t), 1)
+        ok = (col_ref[...] == row_ref[...]) & (cols <= rows)
+        open_ref[...] = jnp.where(ok, 0.0, -1e30)
+
+    total_q = jnp.zeros((1, LANES), F32)
+    for i in reversed(range(t // tile)):
+        rows = slice(i * tile, (i + 1) * tile)
+        seen = (i + 1) * tile
+        dqs, dks, dvs = [], [], []
+        for h in range(2):
+            lanes = slice(h * HEAD, (h + 1) * HEAD)
+            q = q_ref[rows, lanes]
+            k = k_ref[:seen, lanes]
+            dm = dm_ref[rows, lanes]
+            s = dot_t(q, k) + open_ref[rows, :seen]
+            p = jnp.exp(s - lse_ref[rows, h * HEAD : h * HEAD + 1])
+            dp = dot_t(dm, v_ref[:seen, lanes])
+            delta = jnp.sum(p * dp, axis=-1, keepdims=True)
+            ds = (p * (dp - delta)).astype(BF16)
+            dqs.append(dot(ds, k))
+            dks.append(t_dot(ds, q))
+            dvs.append(t_dot(p.astype(BF16), dm))
+        dq = turn(jnp.concatenate(dqs, axis=1) * 0.125, cos_ref[rows, :], -sin_ref[rows, :])
+        dq = dq.astype(BF16)
+        dq_ref[rows, :] = dq
+        total_q += row_sum(dq.astype(F32))
+        dk = jnp.concatenate(dks, axis=1)
+        dv = jnp.concatenate(dvs, axis=1)
+        if seen == t:
+            ak_ref[...] = dk
+            av_ref[...] = dv
+        else:
+            ak_ref[:seen, :] += dk
+            av_ref[:seen, :] += dv
+    dk = turn(ak_ref[...], cos_ref[...], -sin_ref[...]).astype(BF16)
+    dv = av_ref[...].astype(BF16)
+    dk_ref[...] = dk
+    dv_ref[...] = dv
+    sum_ref[0:1, :] = total_q
+    sum_ref[1:2, :] = row_sum(dk.astype(F32))
+    sum_ref[2:3, :] = row_sum(dv.astype(F32))
+
+
+def attend_back(qk, v, dm, lse, col, row, cosine, sine, first, steps):
+    t, width = v.shape
+    key = width // LANES
+    part = steps * LANES
+    block = lambda f: pl.BlockSpec((t, LANES), f)
+    fixed = lambda a: pl.BlockSpec(a.shape, lambda i: (0, 0))
+    here = block(lambda i: (0, i))
+    read = block(lambda i: (0, i + first))
+    return pl.pallas_call(
+        attend_back_kernel,
+        grid=(steps,),
+        in_specs=[read, block(lambda i: (0, i + first + key)), read, read, read]
+        + [fixed(a) for a in (col, row, cosine, sine)],
+        out_specs=[here, here, here, pl.BlockSpec((8, LANES), lambda i: (0, i))],
+        out_shape=[shape((t, part), BF16)] * 3 + [shape((8, part), F32)],
+        scratch_shapes=[
+            pltpu.VMEM((t, t), F32),
+            pltpu.VMEM((t, LANES), F32),
+            pltpu.VMEM((t, LANES), F32),
+        ],
+        compiler_params=params(),
+        cost_estimate=cost(10 * t * t * part, 18 * t * part),
+        name="attend_back",
+    )(qk, qk, v, dm, lse, col, row, cosine, sine)
+
+
+def out_kernel(mixed, order, x, bias, g2, g3, *refs):
+    own, sib = refs[:5], refs[5:10]
+    m_own, m_sib, att_ref, mid_ref, n_ref, n_own, n_sib = refs[10:]
+    half = m_own.shape[1]
+    turned = dot(mixed[...], order[...]).astype(BF16)
+    m_own[...] = turned[:, :half]
+    m_sib[...] = turned[:, half:]
+    att = dot(turned[:, :half], stack_rows(own)) + dot(turned[:, half:], stack_rows(sib))
+    att = att + bias[...]
+    att_ref[...] = att
+    mid = x[...].astype(F32) + att * inverse_rms(att) * g2[...]
+    mid_ref[...] = mid
+    normed = (mid * inverse_rms(mid) * g3[...]).astype(BF16)
+    n_ref[...] = normed
+    turned = dot(normed, order[...]).astype(BF16)
+    n_own[...] = turned[:, :half]
+    n_sib[...] = turned[:, half:]
+
+
+def out_project(mixed, order, x, bias, g2, g3, pieces):
+    t, width = mixed.shape
+    half = width // 2
+    tm = 256
+    rows = lambda c: pl.BlockSpec((tm, c), lambda i: (i, 0))
+    vec = pl.BlockSpec((1, width), lambda i: (0, 0))
+    halves = [shape((t, half), BF16)] * 2
+    return pl.pallas_call(
+        out_kernel,
+        grid=(t // tm,),
+        in_specs=[rows(width), pl.BlockSpec((width, width), lambda i: (0, 0)), rows(width), vec, vec, vec]
+        + [pl.BlockSpec((*p.shape[:2], width), lambda i: (0, 0, 1)) for p in pieces],
+        out_specs=[rows(half)] * 2 + [rows(width)] * 3 + [rows(half)] * 2,
+        out_shape=halves + [shape((t, width), F32)] * 2 + [shape((t, width), BF16)] + halves,
+        compiler_params=params(),
+        cost_estimate=cost(6 * t * width * width, 16 * t * width),
+        name="out_project",
+    )(mixed, order, x, bias, g2, g3, *pieces)
+
+
+def up_kernel(where, x, bias, w_ref, a_own, a_sib, s_own, s_sib):
+    first = where[1] == 0
+    width = x.shape[1]
+    for j in range(w_ref.shape[3] // 256):
+        cols = slice(j * 256, (j + 1) * 256)
+        y = dot(x[...], w_ref[:, 0, :, cols].reshape(width, 256)) + bias[:, cols]
+        yy = y * y
+        t = jnp.tanh(y * (GELU_A + (GELU_A * GELU_B) * yy))
+        h = 0.5 * t + 0.5
+        act = (y * h).astype(BF16)
+        slope = h + (0.5 * y) * (1.0 - t * t) * (GELU_A + (3 * GELU_A * GELU_B) * yy)
+        slope = slope.astype(BF16)
+        dst = slice(j * 128, (j + 1) * 128)
+        a0, a1, s0, s1 = act[:, :128], act[:, 128:], slope[:, :128], slope[:, 128:]
+        a_own[:, dst] = jnp.where(first, a0, a1)
+        a_sib[:, dst] = jnp.where(first, a1, a0)
+        s_own[:, dst] = jnp.where(first, s0, s1)
+        s_sib[:, dst] = jnp.where(first, s1, s0)
+
+
+def up_project(where, x, bias, ffn):
+    t, width = x.shape
+    hidden = bias.shape[1]
+    tn = ffn.shape[3]
+    return pl.pallas_call(
+        up_kernel,
+        grid=(hidden // tn,),
+        in_specs=[
+            smem_spec(),
+            pl.BlockSpec((t, width), lambda i: (0, 0)),
+            pl.BlockSpec((1, tn), lambda i: (0, i)),
+            pl.BlockSpec((ffn.shape[0], 1, ffn.shape[2], tn), lambda i: (0, i, 0, 0)),
+        ],
+        out_specs=[pl.BlockSpec((t, tn // 2), lambda i: (0, i))] * 4,
+        out_shape=[shape((t, hidden // 2), BF16)] * 4,
+        compiler_params=params(),
+        cost_estimate=cost(2 * t * width * hidden, 2 * width * hidden + 4 * t * hidden),
+        name="up_project",
+    )(where, x, bias, ffn)
+
+
+def block_at(ref, where, place):
+    chip = where[0] ^ pair_mask(place)
+    return ref[:, pl.ds(pl.multiple_of(chip * LANES, LANES), LANES)]
+
+
+def down_copies(where, ffn, wbuf, sems):
+    copies = []
+    for e in range(2):
+        for g in range(4):
+            src = ffn.at[pl.ds(g * 4, 4), where[1] ^ e, pl.ds(4, 4)]
+            copies.append(pltpu.make_async_copy(src, wbuf.at[e, g], sems.at[e * 4 + g]))
+    for copy in copies:
+        copy.start()
+    return copies
+
+
+def down_kernel(
+    where, a_own, a_sib, bias, mid, cot, valid, g4, ffn,
+    out_ref, dc_ref, sums_ref, power_ref, wbuf, acc, sems,
+):
+    copies = down_copies(where, ffn, wbuf, sems)
+    width = acc.shape[1]
+    for e, act in enumerate((a_own, a_sib)):
+        for g in range(4):
+            copies[e * 4 + g].wait()
+            y = dot(act[:, g * 512 : (g + 1) * 512], wbuf[e, g].reshape(512, width))
+            if e + g == 0:
+                acc[...] = y + bias[...]
+            else:
+                acc[...] += y
+    t = acc.shape[0]
+    tile = 128
+    power = jnp.zeros((1, 1), F32)
+    gain_sum = jnp.zeros((1, acc.shape[1]), F32)
+    bias_sum = jnp.zeros((1, acc.shape[1]), F32)
+    gain = g4[...]
+    for i in range(t // tile):
+        rows = slice(i * tile, (i + 1) * tile)
+        v = acc[rows, :]
+        ok = valid[rows, :]
+        mean = jnp.mean(v * v, axis=-1, keepdims=True)
+        power += row_sum(mean * ok)
+        r = lax.rsqrt(mean + EPS)
+        out_ref[rows, :] = (mid[rows, :] + v * r * gain).astype(BF16)
+        seed = cot[rows, :].astype(F32) * ok
+        gain_sum += row_sum(v * r * seed)
+        dc = rms_back(v, r, gain, seed).astype(BF16)
+        dc_ref[rows, :] = dc
+        bias_sum += row_sum(dc.astype(F32))
+    sums_ref[0:1, :] = gain_sum
+    sums_ref[1:2, :] = bias_sum
+    power_ref[...] = jnp.broadcast_to(power, power_ref.shape)
+
+
+def down_buffers(ffn):
+    return [pltpu.VMEM((2, 4, 4, 4, ffn.shape[3], ffn.shape[4]), BF16)]
+
+
+def down_project(where, a_own, a_sib, bias, mid, cot, valid, g4, ffn):
+    t, width = mid.shape
+    hidden = 2 * a_own.shape[1]
+    return pl.pallas_call(
+        down_kernel,
+        in_specs=[smem_spec()] + [whole_spec()] * 7 + [hbm_spec()],
+        out_specs=[whole_spec()] * 4,
+        out_shape=[shape((t, width), BF16)] * 2 + [shape((8, width), F32), shape((1, LANES), F32)],
+        scratch_shapes=down_buffers(ffn)
+        + [pltpu.VMEM((t, width), F32), pltpu.SemaphoreType.DMA((8,))],
+        compiler_params=params(),
+        cost_estimate=cost(2 * t * hidden * width, 2 * hidden * width + 10 * t * width),
+        name="down_project",
+    )(where, a_own, a_sib, bias, mid, cot, valid, g4, ffn)
+
+
+def down_back_kernel(where, dc, s_own, s_sib, ffn, de_ref, sums_ref, wbuf, sems):
+    copies = down_copies(where, ffn, wbuf, sems)
+    for e, slope in enumerate((s_own, s_sib)):
+        for g in range(4):
+            copies[e * 4 + g].wait()
+            y = dot_t(dc[...], wbuf[e, g].reshape(512, -1))
+            for j in range(4):
+                chip = g * 4 + j
+                d = y[:, j * LANES : (j + 1) * LANES] * slope[:, chip * LANES : (chip + 1) * LANES].astype(F32)
+                d = d.astype(BF16)
+                at = (chip * 2 + (where[1] ^ e)) * LANES
+                at = pl.ds(pl.multiple_of(at, LANES), LANES)
+                de_ref[:, at] = d
+                sums_ref[:, at] = row_sum(d.astype(F32))
+
+
+def down_back(where, dc, s_own, s_sib, ffn):
+    t, width = dc.shape
+    hidden = 2 * s_own.shape[1]
+    return pl.pallas_call(
+        down_back_kernel,
+        in_specs=[smem_spec()] + [whole_spec()] * 3 + [hbm_spec()],
+        out_specs=[whole_spec()] * 2,
+        out_shape=[shape((t, hidden), BF16), shape((1, hidden), F32)],
+        scratch_shapes=down_buffers(ffn) + [pltpu.SemaphoreType.DMA((8,))],
+        compiler_params=params(),
+        cost_estimate=cost(2 * t * hidden * width, 2 * hidden * width),
+        name="down_back",
+    )(where, dc, s_own, s_sib, ffn)
+
+
+GRAD_PLACES = {
+    "to_x": (14, 15, 6, 7),
+    "to_y": (12, 13, 8, 9),
+    "x01": (4, 5),
+    "y23": (10, 11),
+    "f": (0, 1, 2, 3),
+}
+
+
+def runs_of(places):
+    return [(at, places[at : at + 2]) for at in range(0, len(places), 2)]
+
+
+def slope_kernel(parts, x_own, x_oth, *refs):
+    dy_own, dy_oth = refs[:parts], refs[parts : 2 * parts]
+    outs = refs[2 * parts :]
+    for places, out in zip(GRAD_PLACES.values(), outs):
+        r = out.shape[1]
+        if places == (0, 1, 2, 3):
+            runs = [(0, places)]
+        else:
+            runs = runs_of(places)
+        for at, run in runs:
+            cols = slice(run[0] * r, (run[-1] + 1) * r)
+            for i in range(parts):
+                n = dy_own[i].shape[1]
+                y = t_dot(x_own[:, cols], dy_own[i][...]) + t_dot(x_oth[:, cols], dy_oth[i][...])
+                out[at : at + len(run), :, i * n : (i + 1) * n] = y.astype(BF16).reshape(len(run), r, n)
+
+
+def row_slopes(x_own, x_oth, dy_own, dy_oth, tiles):
+    t, half = x_own.shape
+    r = half // 16
+    parts = len(dy_own)
+    n = dy_own[0].shape[1] // tiles
+    total = n * tiles * parts
+    fixed = pl.BlockSpec((t, half), lambda i: (0, 0))
+    return pl.pallas_call(
+        functools.partial(slope_kernel, parts),
+        grid=(tiles,),
+        in_specs=[fixed] * 2 + [pl.BlockSpec((t, n), lambda i: (0, i))] * (2 * parts),
+        out_specs=[
+            pl.BlockSpec((len(p), r, n * parts), lambda i: (0, 0, i)) for p in GRAD_PLACES.values()
+        ],
+        out_shape=[shape((len(p), r, total), BF16) for p in GRAD_PLACES.values()],
+        compiler_params=params(),
+        cost_estimate=cost(4 * t * half * total, 8 * t * total + 2 * half * total),
+        name="row_slopes",
+    )(x_own, x_oth, *dy_own, *dy_oth)
+
+
+def block_slope_kernel(where, a_own, a_oth, dy_own, dy_oth, *outs):
+    for places, out in zip(GRAD_PLACES.values(), outs):
+        for at, run in runs_of(places):
+            mine = jnp.concatenate([block_at(a_own, where, p) for p in run], axis=1)
+            other = jnp.concatenate([block_at(a_oth, where, p) for p in run], axis=1)
+            y = t_dot(mine, dy_own[...]) + t_dot(other, dy_oth[...])
+            out[at : at + 2] = y.astype(BF16).reshape(2, LANES, y.shape[1])
+
+
+def block_slopes(where, a_own, a_oth, dy_own, dy_oth):
+    t, half = a_own.shape
+    width = dy_own.shape[1]
+    return pl.pallas_call(
+        block_slope_kernel,
+        in_specs=[smem_spec()] + [whole_spec()] * 4,
+        out_specs=[whole_spec()] * 5,
+        out_shape=[shape((len(p), LANES, width), BF16) for p in GRAD_PLACES.values()],
+        compiler_params=params(),
+        cost_estimate=cost(4 * t * half * width, 4 * t * (half + width) + 2 * half * width),
+        name="block_slopes",
+    )(where, a_own, a_oth, dy_own, dy_oth)
+
+
+def to_natural(v, order):
+    high = v.astype(BF16)
+    low = (v - high.astype(F32)).astype(BF16)
+    return dot_t(high, order) + dot_t(low, order)
+
+
+def up_back_kernel(de, order, mid_ref, att_ref, cot, valid, g2_ref, g3_ref, w_ref, *refs):
+    out_own, out_sib = refs[:5], refs[5:10]
+    dmid_ref, datt_ref, dmix_ref, sums_ref, acc = refs[10:]
+    step = pl.program_id(0)
+    width = acc.shape[1]
+    y = dot_t(de[...], w_ref[:, 0].reshape(width, -1))
+
+    @pl.when(step == 0)
+    def _():
+        acc[...] = y
+
+    @pl.when(step > 0)
+    def _():
+        acc[...] += y
+
+    @pl.when(step == pl.num_programs(0) - 1)
+    def _():
+        tile = 256
+        g2, g3 = g2_ref[...], g3_ref[...]
+        w_own, w_sib = stack_rows(out_own), stack_rows(out_sib)
+        sums = [jnp.zeros((1, width), F32)] * 3
+        for i in range(acc.shape[0] // tile):
+            rows = slice(i * tile, (i + 1) * tile)
+            e = acc[rows, :]
+            mid = mid_ref[rows, :]
+            r3 = inverse_rms(mid)
+            dmid = cot[rows, :].astype(F32) * valid[rows, :] + rms_back(mid, r3, g3, e)
+            dmid_ref[rows, :] = dmid
+            att = att_ref[rows, :]
+            r2 = inverse_rms(att)
+            datt = rms_back(att, r2, g2, dmid).astype(BF16)
+            datt_ref[rows, :] = datt
+            sums[0] += row_sum(mid * r3 * e)
+            sums[1] += row_sum(att * r2 * dmid)
+            sums[2] += row_sum(datt.astype(F32))
+            turned = jnp.concatenate([dot_t(datt, w_own), dot_t(datt, w_sib)], axis=1)
+            dmix_ref[rows, :] = dot_t(turned.astype(BF16), order[...]).astype(BF16)
+        for i in range(3):
+            sums_ref[i : i + 1, :] = sums[i]
+
+
+def up_back(de, order, mid, att, cot, valid, g2, g3, ffn, out_pieces):
+    t, width = mid.shape
+    hidden = de.shape[1]
+    tk = ffn.shape[3]
+    fixed = lambda a: pl.BlockSpec(a.shape, lambda i: (0, 0))
+    return pl.pallas_call(
+        up_back_kernel,
+        grid=(hidden // tk,),
+        in_specs=[pl.BlockSpec((t, tk), lambda i: (0, i))]
+        + [fixed(a) for a in (order, mid, att, cot, valid, g2, g3)]
+        + [pl.BlockSpec((ffn.shape[0], 1, ffn.shape[2], tk), lambda i: (0, i, 0, 0))]
+        + [pl.BlockSpec((*p.shape[:2], width), lambda i: (0, 0, 1)) for p in out_pieces],
+        out_specs=[pl.BlockSpec((t, width), lambda i: (0, 0))] * 3
+        + [pl.BlockSpec((8, width), lambda i: (0, 0))],
+        out_shape=[shape((t, width), F32), shape((t, width), BF16), shape((t, width), BF16), shape((8, width), F32)],
+        scratch_shapes=[pltpu.VMEM((t, width), F32)],
+        compiler_params=params(),
+        cost_estimate=cost(2 * t * width * hidden, 2 * width * hidden + 2 * t * hidden),
+        name="up_back",
+    )(de, order, mid, att, cot, valid, g2, g3, ffn, *out_pieces)
+
+
+def in_back_kernel(dqa, dka, dva, dqb, dkb, dvb, order, x_ref, dmid_ref, g1_ref, *refs):
+    qk_own, qk_sib, v_own, v_sib = refs[:5], refs[5:10], refs[10:15], refs[15:20]
+    out_ref, sums_ref = refs[20:]
+    width = x_ref.shape[1]
+    half = width // 2
+    halves = []
+    for qk, v in ((qk_own, v_own), (qk_sib, v_sib)):
+        w = stack_rows(qk)
+        wv = stack_rows(v)
+        y = dot_t(dqa[...], w[:, :half]) + dot_t(dqb[...], w[:, half:width])
+        y = y + dot_t(dka[...], w[:, width : width + half]) + dot_t(dkb[...], w[:, width + half :])
+        halves.append(y + dot_t(dva[...], wv[:, :half]) + dot_t(dvb[...], wv[:, half:]))
+    turned = jnp.concatenate(halves, axis=1)
+    gain = g1_ref[...]
+    tile = 256
+    total = jnp.zeros((1, width), F32)
+    for i in range(x_ref.shape[0] // tile):
+        rows = slice(i * tile, (i + 1) * tile)
+        e = to_natural(turned[rows, :], order[...])
+        x = x_ref[rows, :].astype(F32)
+        r = inverse_rms(x)
+        out_ref[rows, :] = dmid_ref[rows, :] + rms_back(x, r, gain, e)
+        total += row_sum(x * r * e)
+    sums_ref[...] = total
+
+
+def in_back(d_a, d_b, order, x, dmid, g1, qk_pieces, vo_pieces):
+    t, width = x.shape
+    fixed = lambda a: pl.BlockSpec(a.shape, lambda i: (0, 0))
+    return pl.pallas_call(
+        in_back_kernel,
+        grid=(1,),
+        in_specs=[fixed(a) for a in (*d_a, *d_b, order, x, dmid, g1)]
+        + [pl.BlockSpec(p.shape, lambda i: (0, 0, 0)) for p in qk_pieces]
+        + [pl.BlockSpec((*p.shape[:2], width), lambda i: (0, 0, 0)) for p in vo_pieces],
+        out_specs=[pl.BlockSpec((t, width), lambda i: (0, 0)), pl.BlockSpec((1, width), lambda i: (0, 0))],
+        out_shape=[shape((t, width), F32), shape((1, width), F32)],
+        compiler_params=params(),
+        cost_estimate=cost(6 * t * width * width, 6 * width * width),
+        name="in_back",
+    )(*d_a, *d_b, order, x, dmid, g1, *qk_pieces, *vo_pieces)
+
+
+def after(*values):
+    return lax.optimization_barrier(values)
+
+
+def add(*values):
+    total = values[0].astype(F32)
+    for v in values[1:]:
+        total = total + v.astype(F32)
+    return total
+
+
+class Gather:
+    def __init__(self, net, shard):
+        self.net = net
+        self.line = [shard] + [net.swap(shard, 4 * m) for m in (1, 2, 3)]
+
+    def spread(self, line):
+        net = self.net
+        self.lines = jnp.stack(line)
+        self.x = net.swap(self.lines, 1)
+        self.y = net.swap(self.lines, 2)
+        self.sib = [net.sibling(self.lines)]
+
+    def corner(self, x, y):
+        net = self.net
+        self.x, self.y = x, y
+        self.d01 = net.swap(x[:2], 2)
+        self.d23 = net.swap(y[2:], 1)
+        self.sib += [net.sibling(x), net.sibling(y)]
+
+    def finish(self, d01, d23):
+        net = self.net
+        self.d01, self.d23 = d01, d23
+        self.sib += [net.sibling(d01), net.sibling(d23)]
+
+    def pieces(self):
+        return [self.lines, self.x, self.y, self.d01, self.d23] + self.sib
+
+
+class Scatter:
+    def __init__(self, net, pieces):
+        self.net = net
+        to_x, to_y, self.x01, self.y23, self.f = pieces
+        self.from_x = net.swap(to_x, 1)
+        self.from_y = net.swap(to_y, 2)
+
+    def second(self, from_x, from_y):
+        net = self.net
+        self.x23, self.y01 = from_x[2:], from_y[2:]
+        self.rx01 = net.swap(add(self.x01, from_y[:2]).astype(BF16), 1)
+        self.ry23 = net.swap(add(self.y23, from_x[:2]).astype(BF16), 2)
+
+    def third(self, rx01, ry23):
+        net = self.net
+        low = add(self.f[:2], rx01, self.y01)
+        high = add(self.f[2:], ry23, self.x23)
+        self.low = low
+        self.far = net.swap(high.astype(BF16), 8)
+
+    def fourth(self, far):
+        net = self.net
+        low = self.low + far.astype(F32)
+        self.own = low[0]
+        self.near = net.swap(low[1].astype(BF16), 4)
+
+    def result(self, near):
+        return add(self.own, near)
+
+
+def shards_16(
+    activations,
+    segment_ids,
+    cotangent,
+    querymat,
+    keymat,
+    valuemat,
+    outmat,
+    upmatrix,
+    downmatrix,
+    querybias,
+    keybias,
+    valuebias,
+    outbias,
+    upbias,
+    downbias,
+    firstgain,
+    secondgain,
+    thirdgain,
+    fourthgain,
+):
+    net = Net(16)
+    t, width = activations.shape
+    rows = querymat.shape[0]
+    hidden = upmatrix.shape[1]
+    block = upbias.shape[0]
+    half = width // 2
+    me, core = net.me, net.core
+    device = me * 2 + core
+    where = jnp.stack([me, core]).astype(I32)
+
+    dst = jnp.arange(width)
+    place = (dst // rows) % 16
+    chip = me ^ (place // 4 + 4 * (place % 4))
+    src = chip * (2 * rows) + (core ^ (dst // half)) * rows + dst % rows
+    order = (jnp.arange(width)[:, None] == src[None, :]).astype(BF16)
+    slots = jnp.arange(t)
+    segment = jnp.where(segment_ids >= 0, segment_ids, -1 - slots)
+    col, row = segment[:, None], segment[None, :]
+    valid = (segment_ids >= 0).astype(F32)[:, None]
+    spots = positions_of(segment_ids).astype(F32)
+    inverse = 10000.0 ** (-jnp.arange(HEAD // 2).astype(F32) * 2.0 / HEAD)
+    angles = spots[:, None] * inverse[None, :]
+    cosine = jnp.tile(jnp.cos(angles), (1, 4))
+    sine = jnp.sin(angles)
+    sine = jnp.tile(jnp.concatenate([-sine, sine], axis=1), (1, 2))
+
+    ffn_shard = jnp.concatenate(
+        [upmatrix.reshape(rows, 4, width).transpose(1, 0, 2), downmatrix.reshape(4, rows, width)]
+    )
+    ffn = lax.all_gather(ffn_shard, AXES, axis=0, tiled=False)
+    qk = Gather(net, jnp.concatenate([querymat, keymat], axis=1))
+    vo_shard = jnp.concatenate([valuemat, outmat], axis=1)
+    nine = [querybias, keybias, valuebias, outbias, downbias, firstgain, secondgain, thirdgain, fourthgain]
+    small = jnp.concatenate([jnp.pad(v[None], ((0, 0), (0, LANES - rows))) for v in nine] + [upbias[None]])
+    buf = small[None]
+    buf = jnp.concatenate([buf, net.sibling(buf)])
+    for mask in (1, 2, 4, 8):
+        buf = jnp.concatenate([buf, net.swap(buf, mask)])
+    line, buf, vo_shard = after(qk.line, buf, vo_shard)
+    qk.spread(line)
+    vo = Gather(net, vo_shard)
+
+    picks = (jnp.arange(32)[:, None] ^ device) == jnp.arange(32)[None, :]
+    small_all = dot(picks.astype(BF16), buf.reshape(32, -1)).reshape(32, 10, LANES)
+    b_q, b_k, b_v, b_o, b_d, g1, g2, g3, g4 = (
+        small_all[:, i, :rows].reshape(1, width) for i in range(9)
+    )
+    b_up = small_all[:, 9].reshape(1, hidden)
+    inputs = activations.astype(F32)
+    normed = (inputs * inverse_rms(inputs) * g1).astype(BF16)
+    turned = dot(normed, order).astype(BF16)
+    x_own, x_sib = turned[:, :half], turned[:, half:]
+
+    x, y, line = after(qk.x, qk.y, vo.line)
+    qk.corner(x, y)
+    vo.spread(line)
+    d01, d23, x_own, x_sib = after(qk.d01, qk.d23, x_own, x_sib)
+    qk.finish(d01, d23)
+    x_oth = net.sibling(x_sib)
+    x, y = after(vo.x, vo.y)
+    vo.corner(x, y)
+    qk_pieces = qk.pieces()
+    qk_rot = project(x_own, x_sib, qk_pieces, 0, 2, jnp.concatenate([b_q, b_k], axis=1), (cosine, sine))
+    d01, d23, qk_rot = after(vo.d01, vo.d23, qk_rot)
+    vo.finish(d01, d23)
+    vo_pieces = vo.pieces()
+    v = project(x_own, x_sib, vo_pieces, 0, 1, b_v)
+    mixed, lse = attend(qk_rot, v, col, row)
+    m_own, m_sib, att, mid, normed_mid, n_own, n_sib = out_project(
+        mixed, order, activations, b_o, g2, g3, vo_pieces
+    )
+    m_oth = net.sibling(m_sib)
+    n_oth = net.sibling(n_sib)
+    a_own, a_sib, s_own, s_sib = up_project(where, normed_mid, b_up, ffn)
+    a_oth = net.sibling(a_sib)
+    ffn_down = ffn.reshape(16, 2, 8, rows, width)
+    layer_out, dc, down_sums, power = down_project(
+        where, a_own, a_sib, b_d, mid, cotangent, valid, g4, ffn_down
+    )
+
+    dc_oth = net.sibling(dc)
+    de, up_bias_sum = down_back(where, dc, s_own, s_sib, ffn_down)
+    de, dc_oth, a_oth = after(de, dc_oth, a_oth)
+    de_oth = net.sibling(de)
+    slopes = block_slopes(where, a_own, a_oth, dc, dc_oth)
+    slopes, de = after(slopes, de)
+    down_sum = Scatter(net, slopes)
+    dmid, datt, dmix, mid_sums = up_back(
+        de, order, mid, att, cotangent, valid, g2, g3, ffn, vo_pieces
+    )
+    from_x, from_y, datt, dmix, de_oth = after(down_sum.from_x, down_sum.from_y, datt, dmix, de_oth)
+    down_sum.second(from_x, from_y)
+    datt_oth = net.sibling(datt)
+    slopes = row_slopes(n_own, n_oth, [de], [de_oth], 4)
+    slopes, rx01, ry23, datt_oth, datt, dmix = after(
+        slopes, down_sum.rx01, down_sum.ry23, datt_oth, datt, dmix
+    )
+    up_sum = Scatter(net, slopes)
+    down_sum.third(rx01, ry23)
+    steps = width // LANES // 2
+    d_a = attend_back(qk_rot, v, dmix, lse, col, row, cosine, sine, 0, steps)
+    d_a, dmix, from_x, from_y, far = after(d_a, dmix, up_sum.from_x, up_sum.from_y, down_sum.far)
+    up_sum.second(from_x, from_y)
+    down_sum.fourth(far)
+    *d_a, sums_a = d_a
+    oth_a = [net.sibling(d) for d in d_a]
+    slopes = row_slopes(m_own, m_oth, [datt], [datt_oth], 1)
+    slopes, dmix = after(slopes, dmix)
+    d_b = attend_back(qk_rot, v, dmix, lse, col, row, cosine, sine, steps, steps)
+    d_b, oth_a, near, rx01, ry23, slopes = after(
+        d_b, oth_a, down_sum.near, up_sum.rx01, up_sum.ry23, slopes
+    )
+    *d_b, sums_b = d_b
+    down_total = down_sum.result(near)
+    out_sum = Scatter(net, slopes)
+    up_sum.third(rx01, ry23)
+    oth_b = [net.sibling(d) for d in d_b]
+    slopes = row_slopes(x_own, x_oth, d_a, oth_a, 1)
+    slopes, oth_b, from_x, from_y, d_a, d_b = after(
+        slopes, oth_b, out_sum.from_x, out_sum.from_y, d_a, d_b
+    )
+    qkv_a = Scatter(net, slopes)
+    out_sum.second(from_x, from_y)
+    slopes = row_slopes(x_own, x_oth, d_b, oth_b, 1)
+    slopes, far, d_a, d_b, rx01, ry23 = after(
+        slopes, up_sum.far, d_a, d_b, out_sum.rx01, out_sum.ry23
+    )
+    up_sum.fourth(far)
+    qkv_b = Scatter(net, slopes)
+    out_sum.third(rx01, ry23)
+    input_gradient, first_sum = in_back(
+        d_a, d_b, order, activations, dmid, g1, qk_pieces, vo_pieces
+    )
+    first_sum, a_x, a_y, near, far = after(
+        first_sum, qkv_a.from_x, qkv_a.from_y, up_sum.near, out_sum.far
+    )
+    up_total = up_sum.result(near)
+    qkv_a.second(a_x, a_y)
+    out_sum.fourth(far)
+    b_x, b_y, first_sum = after(qkv_b.from_x, qkv_b.from_y, first_sum)
+    qkv_b.second(b_x, b_y)
+    out_total = out_sum.result(out_sum.near)
+    qkv_a.third(qkv_a.rx01, qkv_a.ry23)
+    qkv_a.fourth(qkv_a.far)
+    qkv_b.third(qkv_b.rx01, qkv_b.ry23)
+    qkv_b.fourth(qkv_b.far)
+    total_a = qkv_a.result(qkv_a.near).reshape(rows, 3, half)
+    total_b = qkv_b.result(qkv_b.near).reshape(rows, 3, half)
+    qkv_total = [jnp.concatenate([total_a[:, i], total_b[:, i]], axis=1) for i in range(3)]
+    qkv_sums = jnp.concatenate([sums_a, sums_b], axis=1)
+
+    sums = jnp.concatenate(
+        [
+            qkv_sums[0],
+            qkv_sums[1],
+            qkv_sums[2],
+            mid_sums[2],
+            down_sums[1],
+            first_sum[0],
+            mid_sums[1],
+            mid_sums[0],
+            down_sums[0],
+            up_bias_sum[0],
+            power[0],
+        ]
+    )
+    sums = net.total(sums.reshape(-1, LANES)).reshape(-1)
+    output_power = sums[-1] / (t * 32)
+    own = lax.dynamic_slice_in_dim(sums[: 9 * width].reshape(9, width), device * rows, rows, 1)
+    own_up = lax.dynamic_slice_in_dim(sums[9 * width : 9 * width + hidden], device * block, block, 0)
+    return (
+        layer_out,
+        input_gradient,
+        *qkv_total,
+        out_total,
+        up_total,
+        down_total,
+        own[0],
+        own[1],
+        own[2],
+        own[3],
+        own_up,
+        own[4],
+        own[5],
+        own[6],
+        own[7],
+        own[8],
+        output_power,
+    )
+
+
+def shards(*args):
+    rows, length = args[3].shape[0], args[0].shape[0]
+    if lax.axis_size("wide") == 16 and rows == 32 and length == 512:
+        return shards_16(*args)
+    return shards_any(*args)
+
+
 def solution(mesh):
     matrix = P(AXES, None)
     vector = P(AXES)

time: 572 us -> 436 us (0.76)
  Pallas kernels: 0 us -> 187 us
  matrix products: 139 us -> 2.25 us
  waiting for transfers between devices: 219 us -> 99.2 us
  other arithmetic: 72 us -> 26.3 us
  local copies, waits for them, and re-layouts: 59.5 us -> 28.2 us
  between operations: 5.14 us -> 17.4 us
    pallas_call x0 -> x16, Pallas kernels: none -> 187 us  [the longest x4 34.2 us: row_slopes(): pl.pallas_call(functools.partial(slope_kernel, parts), grid=(tiles,), in_...]
    dot_general x26 -> x2, matrix products: 139 us -> 2.25 us  [dot(): lax.dot_general(a, b, (((1,), (0,)), ((), ())), preferred_element_type=F32)]
    ppermute x56 -> x52, waiting for transfers between devices: 217 us -> 98.7 us  [swap(): return lax.ppermute(value, 'wide', pairs)]
    reduce_sum x11 -> x1, other arithmetic: 20.3 us -> 0.28 us  [inverse_rms(): return lax.rsqrt(jnp.mean(v * v, axis=-1, keepdims=True) + EPS)]
    another operation x57 -> x3, other arithmetic: 18.3 us -> 0.72 us  [the longest x1 0.58 us: shards_16(): where = jnp.stack([me, core]).astype(I32)]
    slice x26 -> x15, local copies, waits for them, and re-layouts: 18.8 us -> 8.2 us  [the longest x1 1.47 us: shards_16(): mid_sums[0]]
    unnamed x200 -> x149, local copies, waits for them, and re-layouts: 11.3 us -> 5.02 us
    convert_element_type x33 -> x17, other arithmetic: 19.8 us -> 13.9 us  [the longest x5 7.2 us: third(): self.far = net.swap(high.astype(BF16), 8)]
  transfers between devices with their start and end apart: 76 -> 78, of which waited for: 36 -> 23; matrix products, arithmetic and copies ran while one was open for 46% -> 11% of each run, Pallas kernels for 0% -> 40%
where the time goes in v2:
time: 436 us; the launch traced here: 430 us
  Pallas kernels  187 us (43%)
  waiting for transfers between devices  99.2 us (23%)
  starting transfers between devices  69.8 us (16%)
  local copies, waits for them, and re-layouts  28.2 us (6%)
  other arithmetic  26.3 us (6%)
  between operations  17.4 us (4%)
    ppermute x52, waiting for transfers between devices, swap(): return lax.ppermute(value, 'wide', pairs)  98.7 us
    ppermute x52, starting transfers between devices, swap(): return lax.ppermute(value, 'wide', pairs)  64.9 us
    pallas_call x4, Pallas kernels, row_slopes(): pl.pallas_call(functools.partial(slope_kernel, parts), grid=(tiles,), in_...  34.2 us
    pallas_call x2, Pallas kernels, attend_back(): pl.pallas_call(attend_back_kernel, grid=(steps,), in_specs=[read, block(l...  34 us
    pallas_call x1, Pallas kernels, attend(): pl.pallas_call(attend_kernel, grid=(steps,), in_specs=[block(lambda i: (0...  21.3 us
    pallas_call x1, Pallas kernels, up_back(): pl.pallas_call(up_back_kernel, grid=(hidden // tk,), in_specs=[pl.BlockSp...  17.5 us
    pallas_call x1, Pallas kernels, up_project(): pl.pallas_call(up_kernel, grid=(hidden // tn,), in_specs=[smem_spec(), pl...  13.7 us
    pallas_call x1, Pallas kernels, down_back(): pl.pallas_call(down_back_kernel, in_specs=[smem_spec()] + [whole_spec()]...  13 us
  transfers between devices with their start and end apart: 78, of which 23 were waited for; matrix products, arithmetic and copies ran while one was open for 11% of the time, Pallas kernels for 40%

profile of v2, /device:TPU:0, one launch (start us, length us, event | category | flops | bytes accessed | tf_op | source)
XLA Modules:
  0.0 430.5 jit_solution(10202112852216717498)
XLA Ops:
  11.3 5.1 %collective-permute-start.2 = (bf16[32,2048]{1,0:T(8,128)(2,1)S(1)}, bf16[32,2048]{1,0:T(8,128)(2,1)S(1)}, u32[]{:S(2)}, u32[]{:S(2)}) collective-permute-start(bf16[32,2048]{1,0:T(8,128)(2,1)S(1)} %constant_dynamic-update-slice_fusion), channel_id=1, source_target_pairs={{0,24},{2,26},{4,28},{6,30},{8,16},{10,18},{12,20},{14,22},{16,8},... | collective-permute-start | bytes 393224 | tf_op jit(solution)/shard_map/ppermute | solution.py:91
  20.6 2.0 collective-permute-done.4
  24.3 2.1 collective-permute-done.5
  27.9 4.8 %collective-permute-done.6 = bf16[8,10,128]{2,1,0:T(8,128)(2,1)S(1)} collective-permute-done((bf16[8,10,128]{2,1,0:T(8,128)(2,1)S(1)}, bf16[8,10,128]{2,1,0:T(8,128)(2,1)S(1)}, u32[]{:S(2)}, u32[]{:S(2)}) %collective-permute-start.6) | collective-permute-done | bytes 20512 | tf_op jit(solution)/shard_map/ppermute | solution.py:91
  35.5 6.4 %collective-permute-done.7 = bf16[16,10,128]{2,1,0:T(8,128)(2,1)S(1)} collective-permute-done((bf16[16,10,128]{2,1,0:T(8,128)(2,1)S(1)}, bf16[16,10,128]{2,1,0:T(8,128)(2,1)S(1)}, u32[]{:S(2)}, u32[]{:S(2)}) %collective-permute-start.7) | collective-permute-done | bytes 40992 | tf_op jit(solution)/shard_map/ppermute | solution.py:91
  42.1 1.9 collective-permute-start.8
  44.1 3.1 collective-permute-start.12
  50.6 3.0 collective-permute-done.12
  53.6 15.2 %collective-permute-done.11 = bf16[32,2048]{1,0:T(8,128)(2,1)S(1)} collective-permute-done((bf16[32,2048]{1,0:T(8,128)(2,1)S(1)}, bf16[32,2048]{1,0:T(8,128)(2,1)S(1)}, u32[]{:S(2)}, u32[]{:S(2)}) %collective-permute-start.11) | collective-permute-done | bytes 131104 | tf_op jit(solution)/shard_map/ppermute | solution.py:91
  73.1 1.9 collective-permute-start.17
  75.0 2.0 fusion.6
  77.1 7.5 %collective-permute-done.18.refs_4_ = bf16[2,32,2048]{2,1,0:T(8,128)(2,1)} collective-permute-done((bf16[2,32,2048]{2,1,0:T(8,128)(2,1)S(1)}, bf16[2,32,2048]{2,1,0:T(8,128)(2,1)}, u32[]{:S(2)}, u32[]{:S(2)}) %collective-permute-start.18) | collective-permute-done | bytes 262176 | tf_op jit(solution)/shard_map/ppermute | solution.py:91
  92.7 7.7 %project.2.q_ref.k_ref = bf16[512,2048]{1,0:T(8,128)(2,1)} custom-call(bf16[512,512]{1,0:T(8,128)(2,1)} %get-tuple-element.203.x_own, bf16[512,512]{1,0:T(8,128)(2,1)} %get-tuple-element.204.x_sib, bf16[4,32,2048]{2,1,0:T(8,128)(2,1)} %copy-done.8, bf16[4,32,2048]{2,1,0:T(8,128)(2,1)} %collective-permute-done.8.refs_1_, ...), custom_call_target="tpu_custom_call" | custom-call | flops 2147483648 | bytes 4194304 | tf_op jit(solution)/shard_map/project/pallas_call | solution.py:494
  100.5 3.8 collective-permute-done.16.refs_4_.refs_14_
  104.2 2.0 collective-permute-done.15.refs_3_.refs_13_
  106.7 2.3 fusion.order
  114.2 4.1 project.3.v_ref
  118.3 21.3 %attend.1 = (bf16[512,1024]{1,0:T(8,128)(2,1)}, f32[512,1024]{1,0:T(8,128)}) custom-call(bf16[512,2048]{1,0:T(8,128)(2,1)} %project.2.q_ref.k_ref, bf16[512,2048]{1,0:T(8,128)(2,1)} %project.2.q_ref.k_ref, bf16[512,1024]{1,0:T(8,128)(2,1)} %project.3.v_ref, s32[512,1]{1,0:T(8,128)} %copy.112.col_ref, s32[1,512]{1,0:T(1,128)} %bitcast.174), custom_call_target="tpu_custom_call" | custom-call | flops 1073741824 | bytes 5242880 | tf_op jit(solution)/shard_map/attend/pallas_call | solution.py:540
  139.6 8.6 %out_project.1 = (bf16[512,512]{1,0:T(8,128)(2,1)}, bf16[512,512]{1,0:T(8,128)(2,1)}, f32[512,1024]{1,0:T(8,128)}, f32[512,1024]{1,0:T(8,128)}, bf16[512,1024]{1...) custom-call(bf16[512,1024]{1,0:T(8,128)(2,1)} %get-tuple-element.210.mixed, ...), custom_call_target="tpu_custom_call" | custom-call | flops 3221225472 | bytes 8388608 | tf_op jit(solution)/shard_map/out_project/pallas_call | solution.py:664
  148.5 13.7 %up_project.1 = (bf16[512,2048]{1,0:T(8,128)(2,1)}, bf16[512,2048]{1,0:T(8,128)(2,1)}, bf16[512,2048]{1,0:T(8,128)(2,1)}, bf16[512,2048]{1,0:T(8,128)(2,1)}) custom-call(s32[2]{0:T(128)} %pad_add_fusion.where, bf16[512,1024]{1,0:T(8,128)(2,1)} %get-tuple-element.211.x, f32[1,4096]{1,0:T(1,128)} %bitcast.171, bf16[32,8,32,1024]{3,2,1,0:T(8,128)(2,1)} %bitcast.149), custom_call_target="tpu_custom_call" | custom-call | flops 4294967296 | bytes 16777216 | tf_op jit(solution)/shard_map/up_project/pallas_call | solution.py:701
  164.8 11.7 %down_project.1 = (bf16[512,1024]{1,0:T(8,128)(2,1)}, bf16[512,1024]{1,0:T(8,128)(2,1)}, f32[8,1024]{1,0:T(8,128)}, f32[1,128]{1,0:T(1,128)}) custom-call(s32[2]{0:T(128)} %pad_add_fusion.where, bf16[512,2048]{1,0:T(8,128)(2,1)} %get-tuple-element.212.a_own, bf16[512,2048]{1,0:T(8,128)(2,1)} %get-tuple-element.213.a_sib, f32[1,1024]{1,0:T(1,128)} %reshape_squeeze.37.bias, ...), custom_call_target="tpu_custom_call" | custom-call | flops 4294967296 | bytes 13631488 | tf_op jit(solution)/shard_map/down_project/pallas_call | solution.py:779
  176.8 13.0 %down_back.1 = (bf16[512,4096]{1,0:T(8,128)(2,1)}, f32[1,4096]{1,0:T(1,128)}) custom-call(s32[2]{0:T(128)} %pad_add_fusion.where, bf16[512,1024]{1,0:T(8,128)(2,1)} %get-tuple-element.218.dc.dy_own, bf16[512,2048]{1,0:T(8,128)(2,1)} %get-tuple-element.219.s_own, bf16[512,2048]{1,0:T(8,128)(2,1)} %get-tuple-element.220.s_sib, ...), custom_call_target="tpu_custom_call" | custom-call | flops 4294967296 | bytes 8388608 | tf_op jit(solution)/shard_map/down_back/pallas_call | solution.py:811
  191.5 8.6 %block_slopes.1 = (bf16[4,128,1024]{2,1,0:T(8,128)(2,1)}, bf16[4,128,1024]{2,1,0:T(8,128)(2,1)}, bf16[2,128,1024]{2,1,0:T(8,128)(2,1)}, bf16[2,128,1024]{2,1,0:T(8,128)(2,1)}, bf16[4,128,1024]{2,1,0:T(8,128)(2,1)}) custom-call(s32[2]{0:T(128)} %pad_add_fusion.where, bf16[512,2048]{1,0:T(8,128)(2,1)} %get-tuple-element.212.a_own, ...), custom_call_target="tpu_custom_call" | custom-call | flops 4294967296 | bytes 10485760 | tf_op jit(solution)/shard_map/block_slopes/pallas_call | solution.py:886
  201.7 17.5 %up_back.1 = (f32[512,1024]{1,0:T(8,128)}, bf16[512,1024]{1,0:T(8,128)(2,1)}, bf16[512,1024]{1,0:T(8,128)(2,1)}, f32[8,1024]{1,0:T(8,128)}) custom-call(bf16[512,4096]{1,0:T(8,128)(2,1)} %get-tuple-element.230.de.refs_0_, bf16[1024,1024]{1,0:T(8,128)(2,1)} %fusion.order, f32[512,1024]{1,0:T(8,128)} %get-tuple-element.214.mid.mid_ref, ...), custom_call_target="tpu_custom_call" | custom-call | flops 4294967296 | bytes 12582912 | tf_op jit(solution)/shard_map/up_back/pallas_call | solution.py:949
  219.2 6.4 %collective-permute-done.33 = bf16[4,128,1024]{2,1,0:T(8,128)(2,1)S(1)} collective-permute-done((bf16[4,128,1024]{2,1,0:T(8,128)(2,1)}, bf16[4,128,1024]{2,1,0:T(8,128)(2,1)S(1)}, u32[]{:S(2)}, u32[]{:S(2)}) %collective-permute-start.33) | collective-permute-done | bytes 1048608 | tf_op jit(solution)/shard_map/ppermute | solution.py:91
  228.7 13.6 %row_slopes.4 = (bf16[4,32,4096]{2,1,0:T(8,128)(2,1)}, bf16[4,32,4096]{2,1,0:T(8,128)(2,1)}, bf16[2,32,4096]{2,1,0:T(8,128)(2,1)}, bf16[2,32,4096]{2,1,0:T(8,128)(2,1)}, bf16[4,32,4096]{2,1,0:T(8,128)(2,1)}) custom-call(bf16[512,512]{1,0:T(8,128)(2,1)} %get-tuple-element.216.x_own, bf16[512,512]{1,0:T(8,128)(2,1)} %collective-permute-done.30.x_oth, ...), custom_call_target="tpu_custom_call" | custom-call | flops 4294967296 | bytes 20971520 | tf_op jit(solution)/shard_map/row_slopes/pallas_call | solution.py:860
  244.3 2.3 add_convert_fusion.3
  246.6 3.9 collective-permute-start.41
  252.0 16.8 %attend_back.2 = (bf16[512,512]{1,0:T(8,128)(2,1)}, bf16[512,512]{1,0:T(8,128)(2,1)}, bf16[512,512]{1,0:T(8,128)(2,1)}, f32[8,512]{1,0:T(8,128)}) custom-call(bf16[512,2048]{1,0:T(8,128)(2,1)} %project.2.q_ref.k_ref, bf16[512,2048]{1,0:T(8,128)(2,1)} %project.2.q_ref.k_ref, bf16[512,1024]{1,0:T(8,128)(2,1)} %project.3.v_ref, ...), custom_call_target="tpu_custom_call" | custom-call | flops 1342177280 | bytes 4718592 | tf_op jit(solution)/shard_map/attend_back/pallas_call | solution.py:620
  268.8 4.5 %collective-permute-done.41 = bf16[2,128,1024]{2,1,0:T(8,128)(2,1)S(1)} collective-permute-done((bf16[2,128,1024]{2,1,0:T(8,128)(2,1)}, bf16[2,128,1024]{2,1,0:T(8,128)(2,1)S(1)}, u32[]{:S(2)}, u32[]{:S(2)}) %collective-permute-start.41) | collective-permute-done | bytes 524320 | tf_op jit(solution)/shard_map/ppermute | solution.py:91
  281.4 1.9 collective-permute-done.46
  284.8 5.3 %row_slopes.5 = (bf16[4,32,1024]{2,1,0:T(8,128)(2,1)}, bf16[4,32,1024]{2,1,0:T(8,128)(2,1)}, bf16[2,32,1024]{2,1,0:T(8,128)(2,1)}, bf16[2,32,1024]{2,1,0:T(8,128)(2,1)}, bf16[4,32,1024]{2,1,0:T(8,128)(2,1)}) custom-call(bf16[512,512]{1,0:T(8,128)(2,1)} %get-tuple-element.261.x_own, bf16[512,512]{1,0:T(8,128)(2,1)} %collective-permute-done.42.x_oth, ...), custom_call_target="tpu_custom_call" | custom-call | flops 1073741824 | bytes 5242880 | tf_op jit(solution)/shard_map/row_slopes/pallas_call | solution.py:860
  290.1 17.1 %attend_back.3 = (bf16[512,512]{1,0:T(8,128)(2,1)}, bf16[512,512]{1,0:T(8,128)(2,1)}, bf16[512,512]{1,0:T(8,128)(2,1)}, f32[8,512]{1,0:T(8,128)}) custom-call(bf16[512,2048]{1,0:T(8,128)(2,1)} %project.2.q_ref.k_ref, bf16[512,2048]{1,0:T(8,128)(2,1)} %project.2.q_ref.k_ref, bf16[512,1024]{1,0:T(8,128)(2,1)} %project.3.v_ref, ...), custom_call_target="tpu_custom_call" | custom-call | flops 1342177280 | bytes 4718592 | tf_op jit(solution)/shard_map/attend_back/pallas_call | solution.py:620
  309.9 2.2 add_convert_fusion
  314.5 7.7 %row_slopes.6 = (bf16[4,32,1536]{2,1,0:T(8,128)(2,1)}, bf16[4,32,1536]{2,1,0:T(8,128)(2,1)}, bf16[2,32,1536]{2,1,0:T(8,128)(2,1)}, bf16[2,32,1536]{2,1,0:T(8,128)(2,1)}, bf16[4,32,1536]{2,1,0:T(8,128)(2,1)}) custom-call(bf16[512,512]{1,0:T(8,128)(2,1)} %get-tuple-element.203.x_own, bf16[512,512]{1,0:T(8,128)(2,1)} %copy-done.55, ...), custom_call_target="tpu_custom_call" | custom-call | flops 1610612736 | bytes 7864320 | tf_op jit(solution)/shard_map/row_slopes/pallas_call | solution.py:860
  323.0 3.3 collective-permute-start.54
  331.5 7.7 %row_slopes.7 = (bf16[4,32,1536]{2,1,0:T(8,128)(2,1)}, bf16[4,32,1536]{2,1,0:T(8,128)(2,1)}, bf16[2,32,1536]{2,1,0:T(8,128)(2,1)}, bf16[2,32,1536]{2,1,0:T(8,128)(2,1)}, bf16[4,32,1536]{2,1,0:T(8,128)(2,1)}) custom-call(bf16[512,512]{1,0:T(8,128)(2,1)} %get-tuple-element.203.x_own, bf16[512,512]{1,0:T(8,128)(2,1)} %copy-done.55, ...), custom_call_target="tpu_custom_call" | custom-call | flops 1610612736 | bytes 7864320 | tf_op jit(solution)/shard_map/row_slopes/pallas_call | solution.py:860
  339.2 10.6 %collective-permute-done.54 = bf16[2,32,4096]{2,1,0:T(8,128)(2,1)S(1)} collective-permute-done((bf16[2,32,4096]{2,1,0:T(8,128)(2,1)S(1)}, bf16[2,32,4096]{2,1,0:T(8,128)(2,1)S(1)}, u32[]{:S(2)}, u32[]{:S(2)}) %collective-permute-start.54) | collective-permute-done | bytes 524320 | tf_op jit(solution)/shard_map/ppermute | solution.py:91
  352.8 4.2 collective-permute-start.59
  357.6 12.9 %in_back.1 = (f32[512,1024]{1,0:T(8,128)}, f32[1,1024]{1,0:T(1,128)}) custom-call(bf16[512,512]{1,0:T(8,128)(2,1)} %get-tuple-element.320.refs_0_.dqa, bf16[512,512]{1,0:T(8,128)(2,1)} %get-tuple-element.321.refs_1_.dka, bf16[512,512]{1,0:T(8,128)(2,1)} %get-tuple-element.322.refs_2_.dva, bf16[512,512]{1,0:T(8,128)(2,1)} %get-tuple-element.323.refs_0_.dqb, ...), custom_call_target="tpu_custom_call" | custom-call | flops 3221225472 | bytes 6291456 | tf_op jit(solution)/shard_map/in_back/pallas_call | solution.py:995
  378.9 4.1 collective-permute-done.66
  386.7 2.4 collective-permute-done.73
  391.3 1.9 collective-permute-done.74
  394.6 3.4 collective-permute-done.75
  397.9 3.1 collective-permute-start.76
  401.1 6.3 %collective-permute-done.63 = bf16[2,32,1536]{2,1,0:T(8,128)(2,1)S(1)} collective-permute-done((bf16[2,32,1536]{2,1,0:T(8,128)(2,1)S(1)}, bf16[2,32,1536]{2,1,0:T(8,128)(2,1)S(1)}, u32[]{:S(2)}, u32[]{:S(2)}) %collective-permute-start.63) | collective-permute-done | bytes 196640 | tf_op jit(solution)/shard_map/ppermute | solution.py:91
  407.6 4.7 %collective-permute-done.76 = f32[105,128]{1,0:T(8,128)S(1)} collective-permute-done((f32[105,128]{1,0:T(8,128)S(1)}, f32[105,128]{1,0:T(8,128)S(1)}, u32[]{:S(2)}, u32[]{:S(2)}) %collective-permute-start.76) | collective-permute-done | bytes 53792 | tf_op jit(solution)/shard_map/ppermute | solution.py:91
  415.4 4.6 %collective-permute-done.70 = bf16[32,1536]{1,0:T(8,128)(2,1)S(1)} collective-permute-done((bf16[32,1536]{1,0:T(8,128)(2,1)S(1)}, bf16[32,1536]{1,0:T(8,128)(2,1)S(1)}, u32[]{:S(2)}, u32[]{:S(2)}) %collective-permute-start.70) | collective-permute-done | bytes 98336 | tf_op jit(solution)/shard_map/ppermute | solution.py:91
  (391 shorter events, 92.9 us)
Async XLA Ops:
  7.3 141.2 %all-gather.3.cloned.1.call-start = ((), (), s32[]{:S(2)}) async-start(), calls=%async_computation | async-start | bytes 17301504 | tf_op jit(solution)/shard_map/all_gather | solution.py:1128
  11.3 30.6 %collective-permute-start.2 = (bf16[32,2048]{1,0:T(8,128)(2,1)S(1)}, bf16[32,2048]{1,0:T(8,128)(2,1)S(1)}, u32[]{:S(2)}, u32[]{:S(2)}) collective-permute-start(bf16[32,2048]{1,0:T(8,128)(2,1)S(1)} %constant_dynamic-update-slice_fusion), channel_id=1, source_target_pairs={{0,24},{2,26},{4,28},{6,30},{8,16},{10,18},{12,20},{14,22},{16,8},... | collective-permute-start | bytes 393224 | tf_op jit(solution)/shard_map/ppermute | solution.py:91
  16.4 25.5 %collective-permute-start.1 = (bf16[32,2048]{1,0:T(8,128)(2,1)S(1)}, bf16[32,2048]{1,0:T(8,128)(2,1)S(1)}, u32[]{:S(2)}, u32[]{:S(2)}) collective-permute-start(bf16[32,2048]{1,0:T(8,128)(2,1)S(1)} %constant_dynamic-update-slice_fusion), channel_id=1, source_target_pairs={{0,16},{2,18},{4,20},{6,22},{8,24},{10,26},{12,28},{14,30},{16,0},... | collective-permute-start | bytes 393224 | tf_op jit(solution)/shard_map/ppermute | solution.py:91
  16.4 25.5 %collective-permute-start = (bf16[32,2048]{1,0:T(8,128)(2,1)S(1)}, bf16[32,2048]{1,0:T(8,128)(2,1)S(1)}, u32[]{:S(2)}, u32[]{:S(2)}) collective-permute-start(bf16[32,2048]{1,0:T(8,128)(2,1)S(1)} %constant_dynamic-update-slice_fusion), channel_id=1, source_target_pairs={{0,8},{2,10},{4,12},{6,14},{8,0},{10,2},{12,4},{14,6},{16,24},{18,... | collective-permute-start | bytes 393224 | tf_op jit(solution)/shard_map/ppermute | solution.py:91
  42.0 26.7 %collective-permute-start.9 = (bf16[4,32,2048]{2,1,0:T(8,128)(2,1)S(1)}, bf16[4,32,2048]{2,1,0:T(8,128)(2,1)}, u32[]{:S(2)}, u32[]{:S(2)}) collective-permute-start(bf16[4,32,2048]{2,1,0:T(8,128)(2,1)S(1)} %pad_maximum_fusion.refs_0_), channel_id=1, source_target_pairs={{0,4},{2,6},{4,0},{6,2},{8,12},{10,14},{12,8},{14,10},{16,20},{18,... | collective-permute-start | bytes 1572872 | tf_op jit(solution)/shard_map/ppermute | solution.py:91
  42.1 26.6 %collective-permute-start.8 = (bf16[4,32,2048]{2,1,0:T(8,128)(2,1)S(1)}, bf16[4,32,2048]{2,1,0:T(8,128)(2,1)}, u32[]{:S(2)}, u32[]{:S(2)}) collective-permute-start(bf16[4,32,2048]{2,1,0:T(8,128)(2,1)S(1)} %pad_maximum_fusion.refs_0_), channel_id=1, source_target_pairs={{0,2},{2,0},{4,6},{6,4},{8,10},{10,8},{12,14},{14,12},{16,18},{18,... | collective-permute-start | bytes 1572872 | tf_op jit(solution)/shard_map/ppermute | solution.py:91
  47.2 21.6 %collective-permute-start.11 = (bf16[32,2048]{1,0:T(8,128)(2,1)S(1)}, bf16[32,2048]{1,0:T(8,128)(2,1)S(1)}, u32[]{:S(2)}, u32[]{:S(2)}) collective-permute-start(bf16[32,2048]{1,0:T(8,128)(2,1)S(1)} %pad_maximum_fusion.3), channel_id=1, source_target_pairs={{0,16},{2,18},{4,20},{6,22},{8,24},{10,26},{12,28},{14,30},{16,0},... | collective-permute-start | bytes 393224 | tf_op jit(solution)/shard_map/ppermute | solution.py:91
  47.2 21.6 %collective-permute-start.10 = (bf16[32,2048]{1,0:T(8,128)(2,1)S(1)}, bf16[32,2048]{1,0:T(8,128)(2,1)S(1)}, u32[]{:S(2)}, u32[]{:S(2)}) collective-permute-start(bf16[32,2048]{1,0:T(8,128)(2,1)S(1)} %pad_maximum_fusion.3), channel_id=1, source_target_pairs={{0,8},{2,10},{4,12},{6,14},{8,0},{10,2},{12,4},{14,6},{16,24},{18,... | collective-permute-start | bytes 393224 | tf_op jit(solution)/shard_map/ppermute | solution.py:91
  53.6 35.7 %collective-permute-start.19 = (bf16[4,32,2048]{2,1,0:T(8,128)(2,1)S(1)}, bf16[4,32,2048]{2,1,0:T(8,128)(2,1)}, u32[]{:S(2)}, u32[]{:S(2)}) collective-permute-start(bf16[4,32,2048]{2,1,0:T(8,128)(2,1)S(1)} %pad_maximum_fusion.refs_0_), channel_id=1, source_target_pairs={{0,1},{1,0},{2,3},{3,2},{4,5},{5,4},{6,7},{7,6},{8,9},{9,8},{10,11... | collective-permute-start | bytes 1572872 | tf_op jit(solution)/shard_map/ppermute | solution.py:94
  68.9 17.3 %collective-permute-start.14 = (bf16[4,32,2048]{2,1,0:T(8,128)(2,1)S(1)}, bf16[4,32,2048]{2,1,0:T(8,128)(2,1)S(1)}, u32[]{:S(2)}, u32[]{:S(2)}) collective-permute-start(bf16[4,32,2048]{2,1,0:T(8,128)(2,1)S(1)} %pad_maximum_fusion.1.refs_0_.refs_10_), channel_id=1, source_target_pairs={{0,4},{2,6},{4,0},{6,2},{8,12},{10,14},{12,8},{14,10},{16,20},{18,... | collective-permute-start | bytes 1572872 | tf_op jit(solution)/shard_map/ppermute | solution.py:91
  69.0 17.2 %collective-permute-start.13 = (bf16[4,32,2048]{2,1,0:T(8,128)(2,1)S(1)}, bf16[4,32,2048]{2,1,0:T(8,128)(2,1)S(1)}, u32[]{:S(2)}, u32[]{:S(2)}) collective-permute-start(bf16[4,32,2048]{2,1,0:T(8,128)(2,1)S(1)} %pad_maximum_fusion.1.refs_0_.refs_10_), channel_id=1, source_target_pairs={{0,2},{2,0},{4,6},{6,4},{8,10},{10,8},{12,14},{14,12},{16,18},{18,... | collective-permute-start | bytes 1572872 | tf_op jit(solution)/shard_map/ppermute | solution.py:91
  89.3 23.7 %collective-permute-start.24 = (bf16[4,32,2048]{2,1,0:T(8,128)(2,1)S(1)}, bf16[4,32,2048]{2,1,0:T(8,128)(2,1)S(1)}, u32[]{:S(2)}, u32[]{:S(2)}) collective-permute-start(bf16[4,32,2048]{2,1,0:T(8,128)(2,1)S(1)} %pad_maximum_fusion.1.refs_0_.refs_10_), channel_id=1, source_target_pairs={{0,1},{1,0},{2,3},{3,2},{4,5},{5,4},{6,7},{7,6},{8,9},{9,8},{10,11... | collective-permute-start | bytes 1572872 | tf_op jit(solution)/shard_map/ppermute | solution.py:94
  89.5 23.5 %collective-permute-start.25 = (bf16[4,32,2048]{2,1,0:T(8,128)(2,1)S(1)}, bf16[4,32,2048]{2,1,0:T(8,128)(2,1)S(1)}, u32[]{:S(2)}, u32[]{:S(2)}) collective-permute-start(bf16[4,32,2048]{2,1,0:T(8,128)(2,1)S(1)} %collective-permute-done.13.refs_1_.refs_11_), channel_id=1, source_target_pairs={{0,1},{1,0},{2,3},{3,2},{4,5},{5,4},{6,7},{7,6},{8,9},{9,8},{10,11... | collective-permute-start | bytes 1572872 | tf_op jit(solution)/shard_map/ppermute | solution.py:94
  89.9 23.1 %collective-permute-start.26 = (bf16[4,32,2048]{2,1,0:T(8,128)(2,1)S(1)}, bf16[4,32,2048]{2,1,0:T(8,128)(2,1)S(1)}, u32[]{:S(2)}, u32[]{:S(2)}) collective-permute-start(bf16[4,32,2048]{2,1,0:T(8,128)(2,1)S(1)} %collective-permute-done.14.refs_2_.refs_12_), channel_id=1, source_target_pairs={{0,1},{1,0},{2,3},{3,2},{4,5},{5,4},{6,7},{7,6},{8,9},{9,8},{10,11... | collective-permute-start | bytes 1572872 | tf_op jit(solution)/shard_map/ppermute | solution.py:94
  162.3 27.5 %collective-permute-start.32 = (bf16[512,2048]{1,0:T(8,128)(2,1)}, bf16[512,2048]{1,0:T(8,128)(2,1)S(1)}, u32[]{:S(2)}, u32[]{:S(2)}) collective-permute-start(bf16[512,2048]{1,0:T(8,128)(2,1)} %get-tuple-element.213.a_sib), channel_id=1, source_target_pairs={{0,1},{1,0},{2,3},{3,2},{4,5},{5,4},{6,7},{7,6},{8,9},{9,8},{10,11... | collective-permute-start | bytes 6291464 | tf_op jit(solution)/shard_map/ppermute | solution.py:94
  189.8 36.1 %collective-permute-start.35 = (bf16[512,4096]{1,0:T(8,128)(2,1)}, bf16[512,4096]{1,0:T(8,128)(2,1)}, u32[]{:S(2)}, u32[]{:S(2)}) collective-permute-start(bf16[512,4096]{1,0:T(8,128)(2,1)} %get-tuple-element.230.de.refs_0_), channel_id=1, source_target_pairs={{0,1},{1,0},{2,3},{3,2},{4,5},{5,4},{6,7},{7,6},{8,9},{9,8},{10,11... | collective-permute-start | bytes 12582920 | tf_op jit(solution)/shard_map/ppermute | solution.py:94
  200.1 25.5 %collective-permute-start.33 = (bf16[4,128,1024]{2,1,0:T(8,128)(2,1)}, bf16[4,128,1024]{2,1,0:T(8,128)(2,1)S(1)}, u32[]{:S(2)}, u32[]{:S(2)}) collective-permute-start(bf16[4,128,1024]{2,1,0:T(8,128)(2,1)} %get-tuple-element.231), channel_id=1, source_target_pairs={{0,2},{2,0},{4,6},{6,4},{8,10},{10,8},{12,14},{14,12},{16,18},{18,... | collective-permute-start | bytes 3145736 | tf_op jit(solution)/shard_map/ppermute | solution.py:91
  200.7 25.2 %collective-permute-start.34 = (bf16[4,128,1024]{2,1,0:T(8,128)(2,1)}, bf16[4,128,1024]{2,1,0:T(8,128)(2,1)S(1)}, u32[]{:S(2)}, u32[]{:S(2)}) collective-permute-start(bf16[4,128,1024]{2,1,0:T(8,128)(2,1)} %get-tuple-element.232), channel_id=1, source_target_pairs={{0,4},{2,6},{4,0},{6,2},{8,12},{10,14},{12,8},{14,10},{16,20},{18,... | collective-permute-start | bytes 3145736 | tf_op jit(solution)/shard_map/ppermute | solution.py:91
  201.7 27.0 %collective-permute-start.30 = (bf16[512,512]{1,0:T(8,128)(2,1)}, bf16[512,512]{1,0:T(8,128)(2,1)}, u32[]{:S(2)}, u32[]{:S(2)}) collective-permute-start(bf16[512,512]{1,0:T(8,128)(2,1)} %get-tuple-element.217), channel_id=1, source_target_pairs={{0,1},{1,0},{2,3},{3,2},{4,5},{5,4},{6,7},{7,6},{8,9},{9,8},{10,11... | collective-permute-start | bytes 1572872 | tf_op jit(solution)/shard_map/ppermute | solution.py:94
  226.0 16.3 %collective-permute-start.38 = (bf16[512,1024]{1,0:T(8,128)(2,1)}, bf16[512,1024]{1,0:T(8,128)(2,1)}, u32[]{:S(2)}, u32[]{:S(2)}) collective-permute-start(bf16[512,1024]{1,0:T(8,128)(2,1)} %get-tuple-element.263.refs_0_), channel_id=1, source_target_pairs={{0,1},{1,0},{2,3},{3,2},{4,5},{5,4},{6,7},{7,6},{8,9},{9,8},{10,11... | collective-permute-start | bytes 3145736 | tf_op jit(solution)/shard_map/ppermute | solution.py:94
  226.2 16.1 %collective-permute-start.37 = (bf16[2,128,1024]{2,1,0:T(8,128)(2,1)S(1)}, bf16[2,128,1024]{2,1,0:T(8,128)(2,1)}, u32[]{:S(2)}, u32[]{:S(2)}) collective-permute-start(bf16[2,128,1024]{2,1,0:T(8,128)(2,1)S(1)} %add_convert_fusion.4), channel_id=1, source_target_pairs={{0,4},{2,6},{4,0},{6,2},{8,12},{10,14},{12,8},{14,10},{16,20},{18,... | collective-permute-start | bytes 1572872 | tf_op jit(solution)/shard_map/ppermute | solution.py:91
  227.4 14.9 %collective-permute-start.36 = (bf16[2,128,1024]{2,1,0:T(8,128)(2,1)S(1)}, bf16[2,128,1024]{2,1,0:T(8,128)(2,1)S(1)}, u32[]{:S(2)}, u32[]{:S(2)}) collective-permute-start(bf16[2,128,1024]{2,1,0:T(8,128)(2,1)S(1)} %add_convert_fusion.5), channel_id=1, source_target_pairs={{0,2},{2,0},{4,6},{6,4},{8,10},{10,8},{12,14},{14,12},{16,18},{18,... | collective-permute-start | bytes 1572872 | tf_op jit(solution)/shard_map/ppermute | solution.py:91
  242.3 31.0 %collective-permute-start.39 = (bf16[4,32,4096]{2,1,0:T(8,128)(2,1)}, bf16[4,32,4096]{2,1,0:T(8,128)(2,1)S(1)}, u32[]{:S(2)}, u32[]{:S(2)}) collective-permute-start(bf16[4,32,4096]{2,1,0:T(8,128)(2,1)} %get-tuple-element.254), channel_id=1, source_target_pairs={{0,2},{2,0},{4,6},{6,4},{8,10},{10,8},{12,14},{14,12},{16,18},{18,... | collective-permute-start | bytes 3145736 | tf_op jit(solution)/shard_map/ppermute | solution.py:91
  243.2 30.2 %collective-permute-start.40 = (bf16[4,32,4096]{2,1,0:T(8,128)(2,1)}, bf16[4,32,4096]{2,1,0:T(8,128)(2,1)S(1)}, u32[]{:S(2)}, u32[]{:S(2)}) collective-permute-start(bf16[4,32,4096]{2,1,0:T(8,128)(2,1)} %get-tuple-element.255), channel_id=1, source_target_pairs={{0,4},{2,6},{4,0},{6,2},{8,12},{10,14},{12,8},{14,10},{16,20},{18,... | collective-permute-start | bytes 3145736 | tf_op jit(solution)/shard_map/ppermute | solution.py:91
  246.6 26.8 %collective-permute-start.41 = (bf16[2,128,1024]{2,1,0:T(8,128)(2,1)}, bf16[2,128,1024]{2,1,0:T(8,128)(2,1)S(1)}, u32[]{:S(2)}, u32[]{:S(2)}) collective-permute-start(bf16[2,128,1024]{2,1,0:T(8,128)(2,1)} %add_convert_fusion.3), channel_id=1, source_target_pairs={{0,16},{2,18},{4,20},{6,22},{8,24},{10,26},{12,28},{14,30},{16,0},... | collective-permute-start | bytes 1572872 | tf_op jit(solution)/shard_map/ppermute | solution.py:91
  251.1 29.8 %collective-permute-start.42 = (bf16[512,512]{1,0:T(8,128)(2,1)}, bf16[512,512]{1,0:T(8,128)(2,1)}, u32[]{:S(2)}, u32[]{:S(2)}) collective-permute-start(bf16[512,512]{1,0:T(8,128)(2,1)} %get-tuple-element.262), channel_id=1, source_target_pairs={{0,1},{1,0},{2,3},{3,2},{4,5},{5,4},{6,7},{7,6},{8,9},{9,8},{10,11... | collective-permute-start | bytes 1572872 | tf_op jit(solution)/shard_map/ppermute | solution.py:94
  277.8 29.5 %collective-permute-start.48 = (bf16[2,32,4096]{2,1,0:T(8,128)(2,1)}, bf16[2,32,4096]{2,1,0:T(8,128)(2,1)}, u32[]{:S(2)}, u32[]{:S(2)}) collective-permute-start(bf16[2,32,4096]{2,1,0:T(8,128)(2,1)} %add_convert_fusion.1), channel_id=1, source_target_pairs={{0,4},{2,6},{4,0},{6,2},{8,12},{10,14},{12,8},{14,10},{16,20},{18,... | collective-permute-start | bytes 1572872 | tf_op jit(solution)/shard_map/ppermute | solution.py:91
  279.6 28.3 %collective-permute-start.47 = (bf16[2,32,4096]{2,1,0:T(8,128)(2,1)}, bf16[2,32,4096]{2,1,0:T(8,128)(2,1)}, u32[]{:S(2)}, u32[]{:S(2)}) collective-permute-start(bf16[2,32,4096]{2,1,0:T(8,128)(2,1)} %add_convert_fusion.2), channel_id=1, source_target_pairs={{0,2},{2,0},{4,6},{6,4},{8,10},{10,8},{12,14},{14,12},{16,18},{18,... | collective-permute-start | bytes 1572872 | tf_op jit(solution)/shard_map/ppermute | solution.py:91
  280.9 26.9 %collective-permute-start.43 = (bf16[512,512]{1,0:T(8,128)(2,1)}, bf16[512,512]{1,0:T(8,128)(2,1)}, u32[]{:S(2)}, u32[]{:S(2)}) collective-permute-start(bf16[512,512]{1,0:T(8,128)(2,1)} %get-tuple-element.320.refs_0_.dqa), channel_id=1, source_target_pairs={{0,1},{1,0},{2,3},{3,2},{4,5},{5,4},{6,7},{7,6},{8,9},{9,8},{10,11... | collective-permute-start | bytes 1572872 | tf_op jit(solution)/shard_map/ppermute | solution.py:94
  280.9 26.9 %collective-permute-start.44 = (bf16[512,512]{1,0:T(8,128)(2,1)}, bf16[512,512]{1,0:T(8,128)(2,1)}, u32[]{:S(2)}, u32[]{:S(2)}) collective-permute-start(bf16[512,512]{1,0:T(8,128)(2,1)} %get-tuple-element.321.refs_1_.dka), channel_id=1, source_target_pairs={{0,1},{1,0},{2,3},{3,2},{4,5},{5,4},{6,7},{7,6},{8,9},{9,8},{10,11... | collective-permute-start | bytes 1572872 | tf_op jit(solution)/shard_map/ppermute | solution.py:94
  283.3 24.5 %collective-permute-start.45 = (bf16[512,512]{1,0:T(8,128)(2,1)}, bf16[512,512]{1,0:T(8,128)(2,1)}, u32[]{:S(2)}, u32[]{:S(2)}) collective-permute-start(bf16[512,512]{1,0:T(8,128)(2,1)} %get-tuple-element.322.refs_2_.dva), channel_id=1, source_target_pairs={{0,1},{1,0},{2,3},{3,2},{4,5},{5,4},{6,7},{7,6},{8,9},{9,8},{10,11... | collective-permute-start | bytes 1572872 | tf_op jit(solution)/shard_map/ppermute | solution.py:94
  307.8 15.1 %collective-permute-start.52 = (bf16[4,32,1024]{2,1,0:T(8,128)(2,1)}, bf16[4,32,1024]{2,1,0:T(8,128)(2,1)}, u32[]{:S(2)}, u32[]{:S(2)}) collective-permute-start(bf16[4,32,1024]{2,1,0:T(8,128)(2,1)} %get-tuple-element.298), channel_id=1, source_target_pairs={{0,2},{2,0},{4,6},{6,4},{8,10},{10,8},{12,14},{14,12},{16,18},{18,... | collective-permute-start | bytes 786440 | tf_op jit(solution)/shard_map/ppermute | solution.py:91
  308.7 17.6 %collective-permute-start.49 = (bf16[512,512]{1,0:T(8,128)(2,1)}, bf16[512,512]{1,0:T(8,128)(2,1)}, u32[]{:S(2)}, u32[]{:S(2)}) collective-permute-start(bf16[512,512]{1,0:T(8,128)(2,1)} %get-tuple-element.323.refs_0_.dqb), channel_id=1, source_target_pairs={{0,1},{1,0},{2,3},{3,2},{4,5},{5,4},{6,7},{7,6},{8,9},{9,8},{10,11... | collective-permute-start | bytes 1572872 | tf_op jit(solution)/shard_map/ppermute | solution.py:94
  308.7 17.6 %collective-permute-start.50 = (bf16[512,512]{1,0:T(8,128)(2,1)}, bf16[512,512]{1,0:T(8,128)(2,1)}, u32[]{:S(2)}, u32[]{:S(2)}) collective-permute-start(bf16[512,512]{1,0:T(8,128)(2,1)} %get-tuple-element.324.refs_1_.dkb), channel_id=1, source_target_pairs={{0,1},{1,0},{2,3},{3,2},{4,5},{5,4},{6,7},{7,6},{8,9},{9,8},{10,11... | collective-permute-start | bytes 1572872 | tf_op jit(solution)/shard_map/ppermute | solution.py:94
  309.2 17.1 %collective-permute-start.51 = (bf16[512,512]{1,0:T(8,128)(2,1)}, bf16[512,512]{1,0:T(8,128)(2,1)}, u32[]{:S(2)}, u32[]{:S(2)}) collective-permute-start(bf16[512,512]{1,0:T(8,128)(2,1)} %get-tuple-element.325.refs_2_.dvb), channel_id=1, source_target_pairs={{0,1},{1,0},{2,3},{3,2},{4,5},{5,4},{6,7},{7,6},{8,9},{9,8},{10,11... | collective-permute-start | bytes 1572872 | tf_op jit(solution)/shard_map/ppermute | solution.py:94
  323.0 26.8 %collective-permute-start.54 = (bf16[2,32,4096]{2,1,0:T(8,128)(2,1)S(1)}, bf16[2,32,4096]{2,1,0:T(8,128)(2,1)S(1)}, u32[]{:S(2)}, u32[]{:S(2)}) collective-permute-start(bf16[2,32,4096]{2,1,0:T(8,128)(2,1)S(1)} %copy-done.19), channel_id=1, source_target_pairs={{0,16},{2,18},{4,20},{6,22},{8,24},{10,26},{12,28},{14,30},{16,0},... | collective-permute-start | bytes 1572872 | tf_op jit(solution)/shard_map/ppermute | solution.py:91
  327.3 22.5 %collective-permute-start.56 = (bf16[2,32,1024]{2,1,0:T(8,128)(2,1)S(1)}, bf16[2,32,1024]{2,1,0:T(8,128)(2,1)}, u32[]{:S(2)}, u32[]{:S(2)}) collective-permute-start(bf16[2,32,1024]{2,1,0:T(8,128)(2,1)S(1)} %add_convert_fusion.13), channel_id=1, source_target_pairs={{0,4},{2,6},{4,0},{6,2},{8,12},{10,14},{12,8},{14,10},{16,20},{18,... | collective-permute-start | bytes 393224 | tf_op jit(solution)/shard_map/ppermute | solution.py:91
  328.0 21.8 %collective-permute-start.55 = (bf16[2,32,1024]{2,1,0:T(8,128)(2,1)S(1)}, bf16[2,32,1024]{2,1,0:T(8,128)(2,1)}, u32[]{:S(2)}, u32[]{:S(2)}) collective-permute-start(bf16[2,32,1024]{2,1,0:T(8,128)(2,1)S(1)} %add_convert_fusion.14), channel_id=1, source_target_pairs={{0,2},{2,0},{4,6},{6,4},{8,10},{10,8},{12,14},{14,12},{16,18},{18,... | collective-permute-start | bytes 393224 | tf_op jit(solution)/shard_map/ppermute | solution.py:91
  329.3 42.6 %collective-permute-start.57 = (bf16[4,32,1536]{2,1,0:T(8,128)(2,1)}, bf16[4,32,1536]{2,1,0:T(8,128)(2,1)}, u32[]{:S(2)}, u32[]{:S(2)}) collective-permute-start(bf16[4,32,1536]{2,1,0:T(8,128)(2,1)} %get-tuple-element.331), channel_id=1, source_target_pairs={{0,2},{2,0},{4,6},{6,4},{8,10},{10,8},{12,14},{14,12},{16,18},{18,... | collective-permute-start | bytes 1179656 | tf_op jit(solution)/shard_map/ppermute | solution.py:91
  330.1 41.8 %collective-permute-start.58 = (bf16[4,32,1536]{2,1,0:T(8,128)(2,1)}, bf16[4,32,1536]{2,1,0:T(8,128)(2,1)S(1)}, u32[]{:S(2)}, u32[]{:S(2)}) collective-permute-start(bf16[4,32,1536]{2,1,0:T(8,128)(2,1)} %get-tuple-element.332), channel_id=1, source_target_pairs={{0,4},{2,6},{4,0},{6,2},{8,12},{10,14},{12,8},{14,10},{16,20},{18,... | collective-permute-start | bytes 1179656 | tf_op jit(solution)/shard_map/ppermute | solution.py:91
  351.5 19.1 %collective-permute-start.60 = (bf16[2,32,1024]{2,1,0:T(8,128)(2,1)}, bf16[2,32,1024]{2,1,0:T(8,128)(2,1)}, u32[]{:S(2)}, u32[]{:S(2)}) collective-permute-start(bf16[2,32,1024]{2,1,0:T(8,128)(2,1)} %add_convert_fusion.12), channel_id=1, source_target_pairs={{0,16},{2,18},{4,20},{6,22},{8,24},{10,26},{12,28},{14,30},{16,0},... | collective-permute-start | bytes 393224 | tf_op jit(solution)/shard_map/ppermute | solution.py:91
  352.8 19.1 %collective-permute-start.59 = (bf16[32,4096]{1,0:T(8,128)(2,1)S(1)}, bf16[32,4096]{1,0:T(8,128)(2,1)S(1)}, u32[]{:S(2)}, u32[]{:S(2)}) collective-permute-start(bf16[32,4096]{1,0:T(8,128)(2,1)S(1)} %fusion.14), channel_id=1, source_target_pairs={{0,8},{2,10},{4,12},{6,14},{8,0},{10,2},{12,4},{14,6},{16,24},{18,... | collective-permute-start | bytes 786440 | tf_op jit(solution)/shard_map/ppermute | solution.py:91
  357.0 21.9 %collective-permute-start.65 = (bf16[4,32,1536]{2,1,0:T(8,128)(2,1)}, bf16[4,32,1536]{2,1,0:T(8,128)(2,1)S(1)}, u32[]{:S(2)}, u32[]{:S(2)}) collective-permute-start(bf16[4,32,1536]{2,1,0:T(8,128)(2,1)} %get-tuple-element.342), channel_id=1, source_target_pairs={{0,2},{2,0},{4,6},{6,4},{8,10},{10,8},{12,14},{14,12},{16,18},{18,... | collective-permute-start | bytes 1179656 | tf_op jit(solution)/shard_map/ppermute | solution.py:91
  375.0 15.3 %collective-permute-start.62 = (bf16[2,32,1536]{2,1,0:T(8,128)(2,1)S(1)}, bf16[2,32,1536]{2,1,0:T(8,128)(2,1)S(1)}, u32[]{:S(2)}, u32[]{:S(2)}) collective-permute-start(bf16[2,32,1536]{2,1,0:T(8,128)(2,1)S(1)} %add_convert_fusion.10), channel_id=1, source_target_pairs={{0,4},{2,6},{4,0},{6,2},{8,12},{10,14},{12,8},{14,10},{16,20},{18,... | collective-permute-start | bytes 589832 | tf_op jit(solution)/shard_map/ppermute | solution.py:91
  376.0 25.1 %collective-permute-start.61 = (bf16[2,32,1536]{2,1,0:T(8,128)(2,1)S(1)}, bf16[2,32,1536]{2,1,0:T(8,128)(2,1)S(1)}, u32[]{:S(2)}, u32[]{:S(2)}) collective-permute-start(bf16[2,32,1536]{2,1,0:T(8,128)(2,1)S(1)} %add_convert_fusion.11), channel_id=1, source_target_pairs={{0,2},{2,0},{4,6},{6,4},{8,10},{10,8},{12,14},{14,12},{16,18},{18,... | collective-permute-start | bytes 589832 | tf_op jit(solution)/shard_map/ppermute | solution.py:91
  385.9 29.3 %collective-permute-start.67 = (bf16[2,32,1536]{2,1,0:T(8,128)(2,1)S(1)}, bf16[2,32,1536]{2,1,0:T(8,128)(2,1)S(1)}, u32[]{:S(2)}, u32[]{:S(2)}) collective-permute-start(bf16[2,32,1536]{2,1,0:T(8,128)(2,1)S(1)} %add_convert_fusion.8), channel_id=1, source_target_pairs={{0,2},{2,0},{4,6},{6,4},{8,10},{10,8},{12,14},{14,12},{16,18},{18,... | collective-permute-start | bytes 589832 | tf_op jit(solution)/shard_map/ppermute | solution.py:91
  391.3 16.2 %collective-permute-start.63 = (bf16[2,32,1536]{2,1,0:T(8,128)(2,1)S(1)}, bf16[2,32,1536]{2,1,0:T(8,128)(2,1)S(1)}, u32[]{:S(2)}, u32[]{:S(2)}) collective-permute-start(bf16[2,32,1536]{2,1,0:T(8,128)(2,1)S(1)} %add_convert_fusion.9), channel_id=1, source_target_pairs={{0,16},{2,18},{4,20},{6,22},{8,24},{10,26},{12,28},{14,30},{16,0},... | collective-permute-start | bytes 589832 | tf_op jit(solution)/shard_map/ppermute | solution.py:91
  393.5 21.7 %collective-permute-start.69 = (bf16[2,32,1536]{2,1,0:T(8,128)(2,1)S(1)}, bf16[2,32,1536]{2,1,0:T(8,128)(2,1)S(1)}, u32[]{:S(2)}, u32[]{:S(2)}) collective-permute-start(bf16[2,32,1536]{2,1,0:T(8,128)(2,1)S(1)} %add_convert_fusion.6), channel_id=1, source_target_pairs={{0,16},{2,18},{4,20},{6,22},{8,24},{10,26},{12,28},{14,30},{16,0},... | collective-permute-start | bytes 589832 | tf_op jit(solution)/shard_map/ppermute | solution.py:91
  (96 other events, 957.8 us)
Sparse Core Ops, SparseCore 0:
  11.4 137.1 all-gather.2
